TPU v7x, 128 devices: a whole 4x4x4 slice. The times are simulated.
128 devices in a mesh: req: 64 (over y, z, x), tp: 2 (over core).
Axes of the slice: x: 4, y: 4, z: 4, core: 2. Of those that a mesh axis runs over, the one named last changes fastest.
Arguments:
- tokens: bfloat16 [12288, 1536], P('req', 'tp'), may hold values from -6 to 6
- video_lengths: int32 [5], replicated, may hold values from 1 to 7680, 12288 in all
- timestep: int32 [1], replicated, may hold values from 1 to 1000
- time_weight: float32 [256, 4608], replicated, may hold values from -0.375 to 0.375
- block_mod: float32 [3, 1536], replicated, may hold values from -3 to 3
- w_query: bfloat16 [1536, 1536], P(None, 'tp')
- w_key: bfloat16 [1536, 1536], P(None, 'tp')
- w_value: bfloat16 [1536, 1536], P(None, 'tp'), may hold values from -0.15625 to 0.15625
- w_out: bfloat16 [1536, 1536], P('tp'), may hold values from -0.15625 to 0.15625
Outputs:
- velocity: bfloat16 [12288, 1536], P('req', 'tp')
- stepped: bfloat16 [12288, 1536], P('req', 'tp')
Inputs may be any that keep to these rules, and one draw needn't show every extreme that they name: `video_lengths`: the videos' lengths in packing order; they sum to 12288 and the longest has exactly 7680 tokens.
All inputs are finite; a program needn't handle non-finite values.
Results may differ from a plain program's by a relative error of at most 0.017.
Values may be sent and summed in bfloat16 or wider, within the bound.
A program may use at most 256 MiB of HBM per device.

v0:
```python
import math

import jax
import jax.numpy as jnp
from jax import lax
from jax.sharding import PartitionSpec as P

HEAD_DIM = 128
STEPS = 1000


def noise_level(step_value):
    frac = step_value / STEPS
    return 5.0 * frac / (1.0 + 4.0 * frac)


def on_device(
    tokens, video_lengths, timestep, time_weight, block_mod, w_query, w_key, w_value, w_out
):
    tok_rows = tokens.shape[0]
    width = time_weight.shape[1] // 3
    full_rows = lax.all_gather(tokens, "tp", axis=1, tiled=True)
    time_value = timestep[0].astype(jnp.float32)
    sigma = noise_level(time_value)
    delta_sigma = noise_level(time_value - 1.0) - sigma
    half_freq = time_weight.shape[0] // 2
    frequency = jnp.exp(-math.log(10000.0) * jnp.arange(half_freq, dtype=jnp.float32) / half_freq)
    angle = 1000.0 * sigma * frequency
    embedding = jnp.concatenate([jnp.cos(angle), jnp.sin(angle)])
    modulation = jnp.dot(
        jax.nn.silu(embedding)[None, :],
        time_weight,
        precision=lax.Precision.HIGHEST,
        preferred_element_type=jnp.float32,
    )[0]
    modulation = modulation.reshape(3, width) + block_mod
    shift, scale, gate = (modulation[0], modulation[1], modulation[2])
    as_float = full_rows.astype(jnp.float32)
    mean = jnp.mean(as_float, axis=1, keepdims=True)
    centred = as_float - mean
    variance = jnp.mean(centred * centred, axis=1, keepdims=True)
    normed = (centred * lax.rsqrt(variance + 1e-06) * (1.0 + scale) + shift).astype(jnp.bfloat16)
    query = jnp.dot(normed, w_query, preferred_element_type=jnp.float32).astype(jnp.bfloat16)
    keys = jnp.dot(normed, w_key, preferred_element_type=jnp.float32).astype(jnp.bfloat16)
    values = jnp.dot(normed, w_value, preferred_element_type=jnp.float32).astype(jnp.bfloat16)
    heads_here = query.shape[1] // HEAD_DIM
    query_heads = query.reshape(tok_rows, heads_here, HEAD_DIM)
    start_row = lax.axis_index("req") * tok_rows
    query_index = start_row + jnp.arange(tok_rows, dtype=jnp.int32)
    video_ends = jnp.cumsum(video_lengths)
    video_starts = video_ends - video_lengths
    inside = jnp.logical_and(
        query_index[:, None] >= video_starts[None, :], query_index[:, None] < video_ends[None, :]
    )
    query_low = jnp.sum(jnp.where(inside, video_starts[None, :], 0), axis=1)
    query_high = jnp.sum(jnp.where(inside, video_ends[None, :], 0), axis=1)
    span_low = jnp.min(query_low)
    span_high = jnp.max(query_high)

    def score_block(carry, pieces):
        row_max, row_sum, weighted = carry
        key_piece, value_piece = pieces
        count = key_piece.shape[0]
        key_heads = key_piece.reshape(count, heads_here, HEAD_DIM)
        value_heads = value_piece.reshape(count, heads_here, HEAD_DIM)
        scores = jnp.einsum(
            "qhd,khd->hqk", query_heads, key_heads, preferred_element_type=jnp.float32
        ) / math.sqrt(HEAD_DIM)
        key_index = jnp.arange(count, dtype=jnp.int32)
        valid = jnp.logical_and(
            key_index[None, :] >= query_low[:, None], key_index[None, :] < query_high[:, None]
        )[None, :, :]
        block_max = jnp.max(jnp.where(valid, scores, -1e30), axis=2)
        new_max = jnp.maximum(row_max, block_max)
        probs = jnp.where(valid, jnp.exp(scores - new_max[:, :, None]), 0.0)
        new_sum = jnp.sum(probs, axis=2)
        update = jnp.einsum(
            "hqk,khd->hqd",
            probs.astype(jnp.bfloat16),
            value_heads,
            preferred_element_type=jnp.float32,
        )
        return (new_max, new_sum, update)

    initial = (
        jnp.full((heads_here, tok_rows), -1e30, jnp.float32),
        jnp.zeros((heads_here, tok_rows), jnp.float32),
        jnp.zeros((heads_here, tok_rows, HEAD_DIM), jnp.float32),
    )
    pieces = (
        lax.all_gather(keys, "req", axis=0, tiled=True),
        lax.all_gather(values, "req", axis=0, tiled=True),
    )
    start = jnp.int32(0)
    count = pieces[0].shape[0]
    touches = jnp.logical_and(start < span_high, start + count > span_low)
    carry = lax.cond(
        touches, lambda state: score_block(state, pieces), lambda state: state, initial
    )
    row_max, row_sum, weighted = carry
    attended = (weighted / row_sum[:, :, None]).astype(jnp.bfloat16)
    attended = jnp.transpose(attended, (1, 0, 2)).reshape(tok_rows, heads_here * HEAD_DIM)
    partial_value = jnp.dot(attended, w_out, preferred_element_type=jnp.float32)
    own_sum = lax.psum_scatter(
        partial_value.astype(jnp.bfloat16), "tp", scatter_dimension=1, tiled=True
    ).astype(jnp.float32)
    share = own_sum.shape[1]
    gate_share = lax.dynamic_slice_in_dim(gate, lax.axis_index("tp") * share, share)
    branch = gate_share[None, :] * own_sum
    velocity = branch.astype(jnp.bfloat16)
    stepped = (tokens.astype(jnp.float32) + delta_sigma * branch).astype(jnp.bfloat16)
    return (velocity, stepped)


def solution(mesh):
    return jax.shard_map(
        on_device,
        mesh=mesh,
        in_specs=(
            P("req", "tp"),
            P(),
            P(),
            P(),
            P(),
            P(None, "tp"),
            P(None, "tp"),
            P(None, "tp"),
            P("tp", None),
        ),
        out_specs=(P("req", "tp"), P("req", "tp")),
        check_vma=False,
    )
```

profile of v0, /device:TPU:17, one launch (start us, length us, event | category | flops | bytes accessed | tf_op | source)
XLA Modules:
  0.0 401.2 jit_solution(11328318087569969528)
XLA Ops:
  7.2 0.0 copy-start
  7.2 0.0 all-gather.5.cloned.1.call-start
  8.1 6.0 %copy.24 = f32[256,4608]{0,1:T(8,128)} copy(f32[256,4608]{1,0:T(8,128)} %param.14) | data formatting | bytes 9437184 | tf_op args[3]
  14.2 0.0 copy-start.2
  14.2 6.4 %fusion.27 = f32[1,3,1536]{2,0,1:T(1,128)S(1)} fusion(f32[256,1,1]{0,1,2:T(1,128)S(1)} %bitcast.41, f32[3,1536,256]{2,1,0:T(8,128)} %bitcast.40), kind=kOutput, calls=%fused_computation.51 | convolution fusion | flops 14155776 | bytes 4738048 | tf_op jit(solution)/shard_map/dot_general | solution.py:30
  20.7 2.5 all_gather.9
  23.2 0.2 convert_reduce_fusion
  23.4 0.3 fusion.13
  23.7 1.5 convolution_convert_fusion.1
  25.2 0.0 all-gather.5.cloned.1.call-update
  25.2 0.0 all-gather.3.cloned.1.call-start
  25.3 3.1 convolution_convert_fusion.2
  28.4 0.0 all-gather.3.cloned.1.call-update
  28.4 0.0 reduce-scatter.2.cloned.1.call-start
  28.5 0.2 reduce-window.8
  28.7 0.1 select_reduce_fusion.1
  28.8 0.7 reduce_max.18
  30.0 0.7 reduce_min.9
  31.3 2.4 convolution_convert_fusion.3
  33.8 103.9 %all-gather.5.cloned.1.call-done = bf16[12288,768]{1,0:T(8,128)(2,1)} async-done(((bf16[192,768]{1,0:T(8,128)(2,1)}), bf16[12288,768]{1,0:T(8,128)(2,1)}) %all-gather.5.cloned.1.call-update) | async-done | bytes 18874384 | tf_op jit(solution)/shard_map/all_gather | solution.py:92
  137.7 113.3 %all-gather.3.cloned.1.call-done = bf16[12288,768]{1,0:T(8,128)(2,1)} async-done(((bf16[192,768]{1,0:T(8,128)(2,1)}), bf16[12288,768]{1,0:T(8,128)(2,1)}) %all-gather.3.cloned.1.call-update) | async-done | bytes 18874384 | tf_op jit(solution)/shard_map/all_gather | solution.py:91
  251.0 128.6 %conditional.1 = (f32[6,192]{1,0:T(8,128)}, f32[6,192,128]{2,1,0:T(8,128)S(1)}) conditional(s32[]{:T(128)} %convert_element_type.44, () %tuple.16, (s32[192]{0:T(256)S(1)}, s32[192]{0:T(256)S(1)}, bf16[192,768]{1,0:T(8,128)(2,1)S(1)}, bf16[12288,768]{1,0:T(8,128)(2,1)}, bf16[12288,768]{1,0:T(8,128)(2,1)}) %tuple.17), branch_computations={%region_7.8_spmd, %region_8.11_spmd} | conditional | flops 7410547712 | bytes 293466624 | solution.py:97
  251.0 3.4 fusion.5
  254.4 24.7 %copy.25 = bf16[12288,768]{0,1:T(8,128)(2,1)} copy(bf16[12288,768]{1,0:T(8,128)(2,1)} %get-tuple-element.30) | data formatting | bytes 37748736 | tf_op jit(solution)/shard_map
  279.0 27.5 %select_reduce_fusion = (f32[6,192]{1,0:T(8,128)S(1)}, f32[6,192,12288]{2,1,0:T(8,128)}) fusion(pred[192,12288]{1,0:T(8,128)(4,1)} %fusion.5, bf16[12288,6,128]{0,2,1:T(8,128)(2,1)} %bitcast.38, bf16[192,768]{1,0:T(8,128)(2,1)S(1)} %get-tuple-element.13), kind=kOutput, calls=%fused_computation.1 | convolution fusion | flops 3666344960 | bytes 78156288 | tf_op jit(solution)/shard_map/cond/branch_1_fun/qhd,khd->hqk/dot_general | solution.py:66
  306.5 24.7 %copy.26 = bf16[12288,768]{0,1:T(8,128)(2,1)} copy(bf16[12288,768]{1,0:T(8,128)(2,1)} %get-tuple-element.31) | data formatting | bytes 37748736 | tf_op jit(solution)/shard_map
  331.2 27.4 %fusion.2 = f32[6,192,128]{2,1,0:T(8,128)S(1)} fusion(bf16[12288,6,128]{0,2,1:T(8,128)(2,1)} %bitcast.39, f32[6,192,12288]{2,1,0:T(8,128)} %get-tuple-element.37, f32[6,192]{1,0:T(8,128)S(1)} %broadcast_maximum_fusion, pred[192,12288]{1,0:T(8,128)(4,1)} %fusion.5), kind=kOutput, calls=%fused_computation.4 | convolution fusion | flops 3680501760 | bytes 78451200 | tf_op jit(solution)/shard_map/cond/branch_1_fun/hqk,khd->hqd/dot_general | solution.py:77
  358.6 21.0 %fusion.1 = f32[6,192]{1,0:T(8,128)} fusion(f32[6,192,12288]{2,1,0:T(8,128)} %get-tuple-element.37, f32[6,192]{1,0:T(8,128)S(1)} %broadcast_maximum_fusion, pred[192,12288]{1,0:T(8,128)(4,1)} %fusion.5), kind=kLoop, calls=%fused_computation.3 | loop fusion | flops 56621952 | bytes 58991616 | tf_op jit(solution)/shard_map/cond/branch_1_fun/reduce_sum | solution.py:76
  379.5 2.2 convolution_convert_fusion
  381.7 0.0 reduce-scatter.2.cloned.1.call-update
  381.8 10.9 %reduce-scatter.2.cloned.1.call-done = bf16[192,768]{1,0:T(8,128)(2,1)} async-done(((bf16[192,1536]{1,0:T(8,128)(2,1)}), bf16[192,768]{1,0:T(8,128)(2,1)}) %reduce-scatter.2.cloned.1.call-update) | async-done | bytes 294928 | tf_op jit(solution)/shard_map/reduce_scatter | solution.py:104
  392.8 1.9 add_convert_fusion
  (26 shorter events, 0.2 us)
Async XLA Ops:
  7.2 372.4 %copy-start = (bf16[768,1536]{1,0:T(8,128)(2,1)S(1)}, bf16[768,1536]{1,0:T(8,128)(2,1)}, u32[]{:S(2)}) copy-start(bf16[768,1536]{1,0:T(8,128)(2,1)} %param.19) | copy-start | bytes 7077892
  7.2 130.5 %all-gather.5.cloned.1.call-start = ((), (), s32[]{:S(2)}) async-start(), calls=%async_computation.2 | async-start | bytes 19169280 | tf_op jit(solution)/shard_map/all_gather | solution.py:92
  14.2 6.4 %copy-start.2 = (f32[3,1536]{1,0:T(4,128)S(1)}, f32[3,1536]{1,0:T(4,128)}, u32[]{:S(2)}) copy-start(f32[3,1536]{1,0:T(4,128)} %param.15) | copy-start | bytes 55300
  14.2 6.5 %copy-start.1 = (bf16[192,768]{1,0:T(8,128)(2,1)S(1)}, bf16[192,768]{1,0:T(8,128)(2,1)}, u32[]{:S(2)}) copy-start(bf16[192,768]{1,0:T(8,128)(2,1)} %param.11) | copy-start | bytes 884740
  14.2 9.5 %copy-start.7 = (bf16[1536,768]{1,0:T(8,128)(2,1)S(1)}, bf16[1536,768]{1,0:T(8,128)(2,1)}, u32[]{:S(2)}) copy-start(bf16[1536,768]{1,0:T(8,128)(2,1)} %param.18) | copy-start | bytes 7077892
  20.6 4.6 %copy-start.3 = (f32[1536]{0:T(1024)}, f32[1536]{0:T(1024)S(1)}, u32[]{:S(2)}) copy-start(f32[1536]{0:T(1024)S(1)} %get-tuple-element.32) | copy-start | bytes 18436
  20.7 4.6 %copy-start.4 = (f32[1536]{0:T(1024)}, f32[1536]{0:T(1024)S(1)}, u32[]{:S(2)}) copy-start(f32[1536]{0:T(1024)S(1)} %get-tuple-element.33) | copy-start | bytes 18436
  23.4 1.9 copy-start.5
  23.7 4.7 %copy-start.6 = (f32[192]{0:T(256)}, f32[192]{0:T(256)S(1)}, u32[]{:S(2)}) copy-start(f32[192]{0:T(256)S(1)} %add_rsqrt_fusion) | copy-start | bytes 2308
  25.2 3.3 copy-start.8
  25.2 225.8 %all-gather.3.cloned.1.call-start = ((), (), s32[]{:S(2)}) async-start(), calls=%async_computation.1 | async-start | bytes 19169280 | tf_op jit(solution)/shard_map/all_gather | solution.py:91
  28.4 364.3 %reduce-scatter.2.cloned.1.call-start = ((), (), s32[]{:S(2)}) async-start(), calls=%async_computation.3 | async-start | bytes 884736 | tf_op jit(solution)/shard_map/reduce_scatter | solution.py:104
Sparse Core Ops, SparseCore 0:
  25.3 112.2 all-gather.4
  141.0 109.9 all-gather.2
  381.9 10.8 reduce-scatter.1
where the time goes:
time: 404 us; the launch traced here: 401 us
  waiting for transfers between devices  228 us (56%)
  matrix products  70.4 us (17%)
  local copies, waits for them, and re-layouts  55.4 us (14%)
  other arithmetic  28.5 us (7%)
  between operations  16 us (4%)
    all_gather x1, waiting for transfers between devices, on_device(): lax.all_gather(keys, 'req', axis=0, tiled=True)  113 us
    all_gather x1, waiting for transfers between devices, on_device(): lax.all_gather(values, 'req', axis=0, tiled=True)  104 us
    another operation x2, local copies, waits for them, and re-layouts  49.3 us
    dot_general x1, matrix products, score_block(): jnp.einsum('qhd,khd->hqk', query_heads, key_heads, preferred_element_type...  27.5 us
    dot_general x1, matrix products, score_block(): jnp.einsum('hqk,khd->hqd', probs.astype(jnp.bfloat16), value_heads, prefe...  27.4 us
    reduce_sum x1, other arithmetic, score_block(): new_sum = jnp.sum(probs, axis=2)  21 us
    reduce_scatter x1, waiting for transfers between devices, on_device(): lax.psum_scatter(partial_value.astype(jnp.bfloat16), 'tp', scatter_dimens...  10.9 us
  transfers between devices with their start and end apart: 3, of which 3 were waited for; matrix products, arithmetic and copies ran while one was open for 2% of the time, Pallas kernels for 0%

commit v1 on v0

--- a/solution.py
+++ b/solution.py
@@ -54,52 +54,28 @@
     )
     query_low = jnp.sum(jnp.where(inside, video_starts[None, :], 0), axis=1)
     query_high = jnp.sum(jnp.where(inside, video_ends[None, :], 0), axis=1)
-    span_low = jnp.min(query_low)
-    span_high = jnp.max(query_high)
-
-    def score_block(carry, pieces):
-        row_max, row_sum, weighted = carry
-        key_piece, value_piece = pieces
-        count = key_piece.shape[0]
-        key_heads = key_piece.reshape(count, heads_here, HEAD_DIM)
-        value_heads = value_piece.reshape(count, heads_here, HEAD_DIM)
-        scores = jnp.einsum(
-            "qhd,khd->hqk", query_heads, key_heads, preferred_element_type=jnp.float32
+    key_index = jnp.arange(tok_rows * lax.psum(1, "req"), dtype=jnp.int32)
+    valid = jnp.logical_and(
+        key_index[None, :] >= query_low[:, None], key_index[None, :] < query_high[:, None]
+    )
+    outputs = []
+    for head in range(heads_here):
+        cols = slice(head * HEAD_DIM, (head + 1) * HEAD_DIM)
+        packed = jnp.concatenate([keys[:, cols], values[:, cols]], axis=1)
+        gathered = lax.all_gather(packed, "req", axis=0, tiled=True)
+        key_head = gathered[:, :HEAD_DIM]
+        value_head = gathered[:, HEAD_DIM:]
+        scores = jnp.dot(
+            query[:, cols], key_head.T, preferred_element_type=jnp.float32
         ) / math.sqrt(HEAD_DIM)
-        key_index = jnp.arange(count, dtype=jnp.int32)
-        valid = jnp.logical_and(
-            key_index[None, :] >= query_low[:, None], key_index[None, :] < query_high[:, None]
-        )[None, :, :]
-        block_max = jnp.max(jnp.where(valid, scores, -1e30), axis=2)
-        new_max = jnp.maximum(row_max, block_max)
-        probs = jnp.where(valid, jnp.exp(scores - new_max[:, :, None]), 0.0)
-        new_sum = jnp.sum(probs, axis=2)
-        update = jnp.einsum(
-            "hqk,khd->hqd",
-            probs.astype(jnp.bfloat16),
-            value_heads,
-            preferred_element_type=jnp.float32,
+        row_max = jnp.max(jnp.where(valid, scores, -1e30), axis=1, keepdims=True)
+        probs = jnp.where(valid, jnp.exp(scores - row_max), 0.0)
+        row_sum = jnp.sum(probs, axis=1, keepdims=True)
+        weighted = jnp.dot(
+            probs.astype(jnp.bfloat16), value_head, preferred_element_type=jnp.float32
         )
-        return (new_max, new_sum, update)
-
-    initial = (
-        jnp.full((heads_here, tok_rows), -1e30, jnp.float32),
-        jnp.zeros((heads_here, tok_rows), jnp.float32),
-        jnp.zeros((heads_here, tok_rows, HEAD_DIM), jnp.float32),
-    )
-    pieces = (
-        lax.all_gather(keys, "req", axis=0, tiled=True),
-        lax.all_gather(values, "req", axis=0, tiled=True),
-    )
-    start = jnp.int32(0)
-    count = pieces[0].shape[0]
-    touches = jnp.logical_and(start < span_high, start + count > span_low)
-    carry = lax.cond(
-        touches, lambda state: score_block(state, pieces), lambda state: state, initial
-    )
-    row_max, row_sum, weighted = carry
-    attended = (weighted / row_sum[:, :, None]).astype(jnp.bfloat16)
-    attended = jnp.transpose(attended, (1, 0, 2)).reshape(tok_rows, heads_here * HEAD_DIM)
+        outputs.append((weighted / row_sum).astype(jnp.bfloat16))
+    attended = jnp.concatenate(outputs, axis=1)
     partial_value = jnp.dot(attended, w_out, preferred_element_type=jnp.float32)
     own_sum = lax.psum_scatter(
         partial_value.astype(jnp.bfloat16), "tp", scatter_dimension=1, tiled=True

time: 404 us -> 574 us (1.42)
  waiting for transfers between devices: 228 us -> 409 us
  local copies, waits for them, and re-layouts: 55.4 us -> 6.26 us
  matrix products: 70.4 us -> 114 us
  other arithmetic: 28.5 us -> 20.1 us
    all_gather x2 -> x6, waiting for transfers between devices: 217 us -> 398 us  [on_device(): gathered = lax.all_gather(packed, 'req', axis=0, tiled=True)]
    another operation x2 -> x0, local copies, waits for them, and re-layouts: 49.3 us -> none
    dot_general x2 -> x12, matrix products: 54.9 us -> 100 us  [the longest x6 64.1 us: on_device(): jnp.dot(query[:, cols], key_head.T, preferred_element_type=jnp.float32)]
    reduce_sum x1, other arithmetic: 21 us -> 13.4 us  [on_device(): row_sum = jnp.sum(probs, axis=1, keepdims=True)]
  transfers between devices with their start and end apart: 3 -> 7, of which waited for: 3 -> 7; matrix products, arithmetic and copies ran while one was open for 2% -> 8% of each run, Pallas kernels for 0% -> 0%
where the time goes in v1:
time: 574 us; the launch traced here: 568 us
  waiting for transfers between devices  409 us (71%)
  matrix products  114 us (20%)
  other arithmetic  20.1 us (4%)
  between operations  15.6 us (3%)
  local copies, waits for them, and re-layouts  6.26 us (1%)
    all_gather x6, waiting for transfers between devices, on_device(): gathered = lax.all_gather(packed, 'req', axis=0, tiled=True)  398 us
    dot_general x6, matrix products, on_device(): jnp.dot(query[:, cols], key_head.T, preferred_element_type=jnp.float32)  64.1 us
    dot_general x6, matrix products, on_device(): jnp.dot(probs.astype(jnp.bfloat16), value_head, preferred_element_type=jn...  36 us
    reduce_sum x1, other arithmetic, on_device(): row_sum = jnp.sum(probs, axis=1, keepdims=True)  13.4 us
  transfers between devices with their start and end apart: 7, of which 7 were waited for; matrix products, arithmetic and copies ran while one was open for 8% of the time, Pallas kernels for 0%

profile of v1, /device:TPU:17, one launch (start us, length us, event | category | flops | bytes accessed | tf_op | source)
XLA Modules:
  0.0 567.5 jit_solution(9086971898280065333)
XLA Ops:
  8.1 2.7 all_gather.21
  11.4 6.0 %copy.12 = f32[256,4608]{0,1:T(8,128)} copy(f32[256,4608]{1,0:T(8,128)} %param.12) | data formatting | bytes 9437184 | tf_op args[3]
  17.4 6.4 %fusion.172 = f32[1,3,1536]{2,0,1:T(1,128)S(1)} fusion(f32[256,1,1]{0,1,2:T(1,128)S(1)} %bitcast.27, f32[3,1536,256]{2,1,0:T(8,128)} %bitcast.24), kind=kOutput, calls=%fused_computation.133 | convolution fusion | flops 14155776 | bytes 4738048 | tf_op jit(solution)/shard_map/dot_general | solution.py:30
  23.9 2.4 convolution_convert_fusion.2
  26.3 0.7 convolution_convert_fusion.1
  27.1 0.7 pad_maximum_fusion
  27.9 0.7 pad_maximum_fusion.2
  29.4 0.6 pad_maximum_fusion.4
  30.1 0.7 pad_maximum_fusion.5
  32.0 2.4 convolution_convert_fusion.3
  34.4 67.3 %all-gather.7.cloned.1.call-done = bf16[12288,256]{1,0:T(8,128)(2,1)} async-done(((bf16[192,256]{1,0:T(8,128)(2,1)}), bf16[12288,256]{1,0:T(8,128)(2,1)}) %all-gather.7.cloned.1.call-update) | async-done | bytes 6291472 | tf_op jit(solution)/shard_map/all_gather | solution.py:65
  101.7 6.9 %convolution_multiply_fusion.5 = f32[192,12288]{1,0:T(8,128)} fusion(bf16[12288,256]{1,0:T(8,128)(2,1)} %all-gather.7.cloned.1.call-done, bf16[192,768]{1,0:T(8,128)(2,1)S(1)} %convolution_convert_fusion.3), kind=kOutput, calls=%fused_computation.5 | convolution fusion | flops 606339072 | bytes 12632064 | tf_op jit(solution)/shard_map/dot_general | solution.py:68
  108.6 67.4 %all-gather.11.cloned.1.call-done = bf16[12288,256]{1,0:T(8,128)(2,1)} async-done(((bf16[192,256]{1,0:T(8,128)(2,1)}), bf16[12288,256]{1,0:T(8,128)(2,1)}) %all-gather.11.cloned.1.call-update) | async-done | bytes 6291472 | tf_op jit(solution)/shard_map/all_gather | solution.py:65
  176.0 6.9 %convolution_multiply_fusion.3 = f32[192,12288]{1,0:T(8,128)} fusion(bf16[12288,256]{1,0:T(8,128)(2,1)} %all-gather.11.cloned.1.call-done, bf16[192,768]{1,0:T(8,128)(2,1)S(1)} %convolution_convert_fusion.3), kind=kOutput, calls=%fused_computation.3 | convolution fusion | flops 606339072 | bytes 12632064 | tf_op jit(solution)/shard_map/dot_general | solution.py:68
  182.9 67.4 %all-gather.13.cloned.1.call-done = bf16[12288,256]{1,0:T(8,128)(2,1)} async-done(((bf16[192,256]{1,0:T(8,128)(2,1)}), bf16[12288,256]{1,0:T(8,128)(2,1)}) %all-gather.13.cloned.1.call-update) | async-done | bytes 6291472 | tf_op jit(solution)/shard_map/all_gather | solution.py:65
  250.3 7.0 %convolution_multiply_fusion.2 = f32[192,12288]{1,0:T(8,128)} fusion(bf16[12288,256]{1,0:T(8,128)(2,1)} %all-gather.13.cloned.1.call-done, bf16[192,768]{1,0:T(8,128)(2,1)S(1)} %convolution_convert_fusion.3), kind=kOutput, calls=%fused_computation.2 | convolution fusion | flops 606339072 | bytes 12632064 | tf_op jit(solution)/shard_map/dot_general | solution.py:68
  257.3 67.1 %all-gather.15.cloned.1.call-done = bf16[12288,256]{1,0:T(8,128)(2,1)} async-done(((bf16[192,256]{1,0:T(8,128)(2,1)}), bf16[12288,256]{1,0:T(8,128)(2,1)}) %all-gather.15.cloned.1.call-update) | async-done | bytes 6291472 | tf_op jit(solution)/shard_map/all_gather | solution.py:65
  324.5 6.8 %convolution_multiply_fusion.1 = f32[192,12288]{1,0:T(8,128)} fusion(bf16[12288,256]{1,0:T(8,128)(2,1)} %all-gather.15.cloned.1.call-done, bf16[192,768]{1,0:T(8,128)(2,1)S(1)} %convolution_convert_fusion.3), kind=kOutput, calls=%fused_computation.1 | convolution fusion | flops 606339072 | bytes 12632064 | tf_op jit(solution)/shard_map/dot_general | solution.py:68
  331.3 67.9 %all-gather.17.cloned.1.call-done = bf16[12288,256]{1,0:T(8,128)(2,1)} async-done(((bf16[192,256]{1,0:T(8,128)(2,1)}), bf16[12288,256]{1,0:T(8,128)(2,1)}) %all-gather.17.cloned.1.call-update) | async-done | bytes 6291472 | tf_op jit(solution)/shard_map/all_gather | solution.py:65
  399.2 13.5 %select_reduce_fusion = (f32[192]{0:T(256)S(1)}, f32[192]{0:T(256)S(1)}, f32[192,12288]{1,0:T(8,128)}) fusion(s32[192]{0:T(256)S(1)} %get-tuple-element.17, s32[192]{0:T(256)S(1)} %get-tuple-element.16, f32[192,12288]{1,0:T(8,128)} %convolution_multiply_fusion.5, bf16[12288,256]{1,0:T(8,128)(2,1)} %all-gather.17.cloned.1.call-done, ...), kind=kOutput, calls=%fused_computation.7 | convolution fusion | flops 622853760 | bytes 22072832 | tf_op jit(solution)/shard_map/dot_general | solution.py:68
  412.6 60.7 %all-gather.9.cloned.1.call-done = bf16[12288,256]{1,0:T(8,128)(2,1)} async-done(((bf16[192,256]{1,0:T(8,128)(2,1)}), bf16[12288,256]{1,0:T(8,128)(2,1)}) %all-gather.9.cloned.1.call-update) | async-done | bytes 6291472 | tf_op jit(solution)/shard_map/all_gather | solution.py:65
  473.3 23.0 %fusion.11 = (f32[192]{0:T(256)S(1)}, f32[192]{0:T(256)S(1)}, f32[192]{0:T(256)S(1)}, f32[192]{0:T(256)S(1)}, f32[192]{0:T(256)S(1)}, /*index=5*/f32[192]{0:T(256)S(1)}, f32[192,12288]{1,0:T(8,128)}) fusion(f32[192,12288]{1,0:T(8,128)} %get-tuple-element.33, f32[192]{0:T(256)S(1)} %get-tuple-element.10, s32[192]{0:T(256)S(1)} %get-tuple-element.17, ...), kind=kOutput, calls=%fused_computation.31 | convolution fusion | flops 646445952 | bytes 59826688 | tf_op jit(solution)/shard_map/dot_general | solution.py:68
  496.4 13.4 %fusion.9 = (f32[192]{0:T(256)S(1)}, f32[192]{0:T(256)S(1)}, f32[192]{0:T(256)S(1)}, f32[192]{0:T(256)S(1)}) fusion(f32[192,12288]{1,0:T(8,128)S(1)} %bitcast.19, f32[192]{0:T(256)S(1)} %get-tuple-element.8, s32[192]{0:T(256)S(1)} %get-tuple-element.17, s32[192]{0:T(256)S(1)} %get-tuple-element.16, f32[192,12288]{1,0:T(8,128)} %get-tuple-element.34, ...), kind=kLoop, calls=%fused_computation.29 | loop fusion | flops 35388672 | bytes 37756416 | tf_op jit(solution)/shard_map/reduce_sum | solution.py:73
  509.8 7.7 %fusion.65 = bf16[192,768]{1,0:T(8,128)(2,1)S(1)} fusion(bf16[12288,256]{1,0:T(8,128)(2,1)} %all-gather.7.cloned.1.call-done, f32[192,12288]{1,0:T(8,128)} %convolution_multiply_fusion.5, f32[192]{0:T(256)S(1)} %get-tuple-element.11, f32[192]{0:T(256)S(1)} %get-tuple-element.9, s32[192]{0:T(256)S(1)} %get-tuple-element.17, s32[192]{0:T(256)S(1)} %get-tuple-element.16), kind=kOutput, calls=%fused_computation.77 | convolution fusion | flops 618184704 | bytes 12635136 | tf_op jit(solution)/shard_map/dot_general | solution.py:74
  517.6 7.8 %fusion.80 = bf16[192,768]{1,0:T(8,128)(2,1)S(1)} fusion(bf16[192,768]{1,0:T(8,128)(2,1)S(1)} %fusion.65, bf16[12288,256]{1,0:T(8,128)(2,1)} %all-gather.9.cloned.1.call-done, f32[192,12288]{1,0:T(8,128)} %get-tuple-element.34, f32[192]{0:T(256)S(1)} %get-tuple-element.5, f32[192]{0:T(256)S(1)} %get-tuple-element.13, s32[192]{0:T(256)S(1)} %get-tuple-element.17, ...), kind=kOutput, calls=%fused_computation.80 | convolution fusion | flops 618184704 | bytes 12636160 | tf_op jit(solution)/shard_map/dot_general | solution.py:74
  525.4 5.2 fusion.95
  530.7 5.4 fusion.110
  536.1 3.1 fusion.125
  539.3 6.8 %fusion.140 = bf16[192,768]{1,0:T(8,128)(2,1)S(1)} fusion(bf16[192,768]{1,0:T(8,128)(2,1)S(1)} %fusion.125, bf16[12288,256]{1,0:T(8,128)(2,1)S(1)} %bitcast.30, f32[192,12288]{1,0:T(8,128)} %get-tuple-element.33, f32[192]{0:T(256)S(1)} %get-tuple-element.10, f32[192]{0:T(256)S(1)} %get-tuple-element.4, s32[192]{0:T(256)S(1)} %get-tuple-element.17, ...), kind=kOutput, calls=%fused_computation.92 | convolution fusion | flops 618184704 | bytes 12636160 | tf_op jit(solution)/shard_map/dot_general | solution.py:74
  546.1 1.4 convolution_convert_fusion
  547.7 10.9 %reduce-scatter.2.cloned.1.call-done = bf16[192,768]{1,0:T(8,128)(2,1)} async-done(((bf16[192,1536]{1,0:T(8,128)(2,1)}), bf16[192,768]{1,0:T(8,128)(2,1)}) %reduce-scatter.2.cloned.1.call-update) | async-done | bytes 294928 | tf_op jit(solution)/shard_map/reduce_scatter | solution.py:80
  558.6 1.9 add_convert_fusion
  (72 shorter events, 3.0 us)
Async XLA Ops:
  7.2 539.0 %copy-start = (bf16[768,1536]{1,0:T(8,128)(2,1)S(1)}, bf16[768,1536]{1,0:T(8,128)(2,1)}, u32[]{:S(2)}) copy-start(bf16[768,1536]{1,0:T(8,128)(2,1)} %param.17) | copy-start | bytes 7077892
  7.2 94.5 %all-gather.7.cloned.1.call-start = ((), (), s32[]{:S(2)}) async-start(), calls=%async_computation.1 | async-start | bytes 6389760 | tf_op jit(solution)/shard_map/all_gather | solution.py:65
  11.3 12.4 %copy-start.2 = (f32[3,1536]{1,0:T(4,128)S(1)}, f32[3,1536]{1,0:T(4,128)}, u32[]{:S(2)}) copy-start(f32[3,1536]{1,0:T(4,128)} %param.13) | copy-start | bytes 55300
  17.4 8.9 %copy-start.3 = (bf16[1536,768]{1,0:T(8,128)(2,1)S(1)}, bf16[1536,768]{1,0:T(8,128)(2,1)}, u32[]{:S(2)}) copy-start(bf16[1536,768]{1,0:T(8,128)(2,1)} %param.16) | copy-start | bytes 7077892
  23.8 7.9 %copy-start.4 = (s32[5]{0:T(128)S(1)}, s32[5]{0:T(128)}, u32[]{:S(2)}) copy-start(s32[5]{0:T(128)} %param.10) | copy-start | bytes 64
  27.8 148.2 %all-gather.11.cloned.1.call-start = ((), (), s32[]{:S(2)}) async-start(), calls=%async_computation.3 | async-start | bytes 6389760 | tf_op jit(solution)/shard_map/all_gather | solution.py:65
  28.6 221.7 %all-gather.13.cloned.1.call-start = ((), (), s32[]{:S(2)}) async-start(), calls=%async_computation.4 | async-start | bytes 6389760 | tf_op jit(solution)/shard_map/all_gather | solution.py:65
  29.3 295.2 %all-gather.15.cloned.1.call-start = ((), (), s32[]{:S(2)}) async-start(), calls=%async_computation.5 | async-start | bytes 6389760 | tf_op jit(solution)/shard_map/all_gather | solution.py:65
  30.0 369.2 %all-gather.17.cloned.1.call-start = ((), (), s32[]{:S(2)}) async-start(), calls=%async_computation.6 | async-start | bytes 6389760 | tf_op jit(solution)/shard_map/all_gather | solution.py:65
  30.8 442.6 %all-gather.9.cloned.1.call-start = ((), (), s32[]{:S(2)}) async-start(), calls=%async_computation.2 | async-start | bytes 6389760 | tf_op jit(solution)/shard_map/all_gather | solution.py:65
  31.5 527.1 %reduce-scatter.2.cloned.1.call-start = ((), (), s32[]{:S(2)}) async-start(), calls=%async_computation.7 | async-start | bytes 884736 | tf_op jit(solution)/shard_map/reduce_scatter | solution.py:80
  473.3 23.0 %slice-start = ((s8[9437184]{0:T(1024)(128)(4,1)}), s8[4194304]{0:T(1024)(128)(4,1)S(1)}, s32[]{:S(2)}) async-start(s8[9437184]{0:T(1024)(128)(4,1)} %bitcast.18), calls=%async_computation.8 | async-start | bytes 8388608
  473.3 23.0 %slice-start.1 = ((s8[9437184]{0:T(1024)(128)(4,1)}), s8[4194304]{0:T(1024)(128)(4,1)S(1)}, s32[]{:S(2)}) async-start(s8[9437184]{0:T(1024)(128)(4,1)} %bitcast.18), calls=%async_computation.9 | async-start | bytes 8388608
  473.3 23.0 %slice-start.2 = ((s8[9437184]{0:T(1024)(128)(4,1)}), s8[1048576]{0:T(1024)(128)(4,1)S(1)}, s32[]{:S(2)}) async-start(s8[9437184]{0:T(1024)(128)(4,1)} %bitcast.18), calls=%async_computation.10 | async-start | bytes 2097152
  509.8 15.6 %slice-start.6 = ((s8[9437184]{0:T(1024)(128)(4,1)}), s8[4194304]{0:T(1024)(128)(4,1)S(1)}, s32[]{:S(2)}) async-start(s8[9437184]{0:T(1024)(128)(4,1)} %bitcast.22), calls=%async_computation.14 | async-start | bytes 8388608
  509.8 15.6 %slice-start.7 = ((s8[9437184]{0:T(1024)(128)(4,1)}), s8[4194304]{0:T(1024)(128)(4,1)S(1)}, s32[]{:S(2)}) async-start(s8[9437184]{0:T(1024)(128)(4,1)} %bitcast.22), calls=%async_computation.15 | async-start | bytes 8388608
  517.6 7.8 %slice-start.8 = ((s8[9437184]{0:T(1024)(128)(4,1)}), s8[1048576]{0:T(1024)(128)(4,1)S(1)}, s32[]{:S(2)}) async-start(s8[9437184]{0:T(1024)(128)(4,1)} %bitcast.22), calls=%async_computation.16 | async-start | bytes 2097152
  517.6 13.1 %slice-start.3 = ((s8[9437184]{0:T(1024)(128)(4,1)}), s8[4194304]{0:T(1024)(128)(4,1)S(1)}, s32[]{:S(2)}) async-start(s8[9437184]{0:T(1024)(128)(4,1)} %bitcast.20), calls=%async_computation.11 | async-start | bytes 8388608
  517.6 13.1 %slice-start.4 = ((s8[9437184]{0:T(1024)(128)(4,1)}), s8[4194304]{0:T(1024)(128)(4,1)S(1)}, s32[]{:S(2)}) async-start(s8[9437184]{0:T(1024)(128)(4,1)} %bitcast.20), calls=%async_computation.12 | async-start | bytes 8388608
  525.4 5.3 slice-start.5
  525.4 10.7 %slice-start.9 = ((s8[6291456]{0:T(1024)(128)(4,1)}), s8[2097152]{0:T(1024)(128)(4,1)S(1)}, s32[]{:S(2)}) async-start(s8[6291456]{0:T(1024)(128)(4,1)} %bitcast.25), calls=%async_computation.17 | async-start | bytes 4194304
  530.7 5.4 slice-start.10
  530.7 8.5 %slice-start.11 = ((s8[6291456]{0:T(1024)(128)(4,1)}), s8[2097152]{0:T(1024)(128)(4,1)S(1)}, s32[]{:S(2)}) async-start(s8[6291456]{0:T(1024)(128)(4,1)} %bitcast.29), calls=%async_computation.19 | async-start | bytes 4194304
  536.1 3.1 slice-start.12
  539.3 19.3 %copy-start.1 = (bf16[192,768]{1,0:T(8,128)(2,1)S(1)}, bf16[192,768]{1,0:T(8,128)(2,1)}, u32[]{:S(2)}) copy-start(bf16[192,768]{1,0:T(8,128)(2,1)} %param.9) | copy-start | bytes 884740
Sparse Core Ops, SparseCore 0:
  27.9 73.7 all-gather.6
  104.6 71.4 all-gather.10
  178.9 71.4 all-gather.12
  253.0 71.4 all-gather.14
  327.7 71.4 all-gather.16
  401.9 71.4 all-gather.8
  547.7 10.8 reduce-scatter.1

commit v2 on v0

--- a/solution.py
+++ b/solution.py
@@ -87,10 +87,8 @@
         jnp.zeros((heads_here, tok_rows), jnp.float32),
         jnp.zeros((heads_here, tok_rows, HEAD_DIM), jnp.float32),
     )
-    pieces = (
-        lax.all_gather(keys, "req", axis=0, tiled=True),
-        lax.all_gather(values, "req", axis=0, tiled=True),
-    )
+    gathered = lax.all_gather(jnp.concatenate([keys, values], axis=1), "req", axis=0, tiled=True)
+    pieces = (gathered[:, : keys.shape[1]], gathered[:, keys.shape[1] :])
     start = jnp.int32(0)
     count = pieces[0].shape[0]
     touches = jnp.logical_and(start < span_high, start + count > span_low)

time: 404 us -> 377 us (0.933)
  waiting for transfers between devices: 228 us -> 183 us
  local copies, waits for them, and re-layouts: 55.4 us -> 77.3 us
    all_gather x2 -> x1, waiting for transfers between devices: 217 us -> 172 us  [on_device(): lax.all_gather(jnp.concatenate([keys, values], axis=1), 'req', axis=0, ti...]
    slice x0 -> x1, local copies, waits for them, and re-layouts: none -> 25.1 us  [on_device(): pieces = (gathered[:, :keys.shape[1]], gathered[:, keys.shape[1]:])]
    another operation x2 -> x1, local copies, waits for them, and re-layouts: 49.3 us -> 44.6 us
  transfers between devices with their start and end apart: 3 -> 2, of which waited for: 3 -> 2; matrix products, arithmetic and copies ran while one was open for 2% -> 1% of each run, Pallas kernels for 0% -> 0%
where the time goes in v2:
time: 377 us; the launch traced here: 375 us
  waiting for transfers between devices  183 us (49%)
  local copies, waits for them, and re-layouts  77.3 us (21%)
  matrix products  67.3 us (18%)
  other arithmetic  28.5 us (8%)
  between operations  16.4 us (4%)
    all_gather x1, waiting for transfers between devices, on_device(): lax.all_gather(jnp.concatenate([keys, values], axis=1), 'req', axis=0, ti...  172 us
    another operation x1, local copies, waits for them, and re-layouts  44.6 us
    dot_general x1, matrix products, score_block(): jnp.einsum('qhd,khd->hqk', query_heads, key_heads, preferred_element_type...  27.5 us
    dot_general x1, matrix products, score_block(): jnp.einsum('hqk,khd->hqd', probs.astype(jnp.bfloat16), value_heads, prefe...  27.4 us
    slice x1, local copies, waits for them, and re-layouts, on_device(): pieces = (gathered[:, :keys.shape[1]], gathered[:, keys.shape[1]:])  25.1 us
    reduce_sum x1, other arithmetic, score_block(): new_sum = jnp.sum(probs, axis=2)  20.3 us
    reduce_scatter x1, waiting for transfers between devices, on_device(): lax.psum_scatter(partial_value.astype(jnp.bfloat16), 'tp', scatter_dimens...  10.9 us
  transfers between devices with their start and end apart: 2, of which 2 were waited for; matrix products, arithmetic and copies ran while one was open for 1% of the time, Pallas kernels for 0%

profile of v2, /device:TPU:17, one launch (start us, length us, event | category | flops | bytes accessed | tf_op | source)
XLA Modules:
  0.0 375.0 jit_solution(12618357246623783938)
XLA Ops:
  7.2 0.0 copy-start
  7.2 0.0 all-gather.2.cloned.1.call-start
  8.1 2.7 all_gather.6
  10.9 0.2 convert_reduce_fusion
  11.0 0.3 fusion.13
  11.3 6.0 %copy.21 = f32[256,4608]{0,1:T(8,128)} copy(f32[256,4608]{1,0:T(8,128)} %param.14) | data formatting | bytes 9437184 | tf_op args[3]
  17.4 0.0 copy-start.2
  17.4 6.4 %fusion.28 = f32[1,3,1536]{2,0,1:T(1,128)S(1)} fusion(f32[256,1,1]{0,1,2:T(1,128)S(1)} %bitcast.41, f32[3,1536,256]{2,1,0:T(8,128)} %bitcast.39), kind=kOutput, calls=%fused_computation.53 | convolution fusion | flops 14155776 | bytes 4738048 | tf_op jit(solution)/shard_map/dot_general | solution.py:30
  23.9 0.7 convolution_convert_fusion.2
  24.6 0.9 copy-done.5
  25.5 0.7 convolution_convert_fusion.1
  26.2 0.8 pad_maximum_fusion
  27.0 0.0 all-gather.2.cloned.1.call-update
  27.1 0.0 reduce-scatter.2.cloned.1.call-start
  27.1 0.2 reduce-window.8
  27.3 0.1 select_reduce_fusion.1
  27.4 0.6 reduce_max.18
  28.7 0.6 reduce_min.9
  30.0 2.4 convolution_convert_fusion.3
  32.4 171.8 %all-gather.2.cloned.1.call-done = bf16[12288,1536]{1,0:T(8,128)(2,1)} async-done(((bf16[192,1536]{1,0:T(8,128)(2,1)}), bf16[12288,1536]{1,0:T(8,128)(2,1)}) %all-gather.2.cloned.1.call-update) | async-done | bytes 37748752 | tf_op jit(solution)/shard_map/all_gather | solution.py:90
  204.2 148.2 %conditional.1 = (f32[6,192]{1,0:T(8,128)S(1)}, f32[6,192,128]{2,1,0:T(8,128)S(1)}) conditional(s32[]{:T(128)} %convert_element_type.44, () %tuple.16, (s32[192]{0:T(256)S(1)}, s32[192]{0:T(256)S(1)}, bf16[192,768]{1,0:T(8,128)(2,1)S(1)}, bf16[12288,1536]{1,0:T(8,128)(2,1)}) %tuple.17), branch_computations={%region_7.8_spmd, %region_8.11_spmd} | conditional | flops 7410547712 | bytes 368964096 | solution.py:95
  204.2 44.6 %copy.22 = bf16[12288,1536]{0,1:T(8,128)(2,1)} copy(bf16[12288,1536]{1,0:T(8,128)(2,1)} %get-tuple-element.29) | data formatting | bytes 75497472 | tf_op jit(solution)/shard_map
  248.8 25.1 %fusion.27 = (bf16[12288,768]{0,1:T(8,128)(2,1)}, bf16[12288,768]{0,1:T(8,128)(2,1)}) fusion(bf16[12288,1536]{0,1:T(8,128)(2,1)} %copy.22), kind=kLoop, calls=%fused_computation.52 | loop fusion | bytes 75497472 | tf_op jit(solution)/shard_map/slice | solution.py:91
  273.9 3.3 fusion.5
  277.2 27.5 %select_reduce_fusion = (f32[6,192]{1,0:T(8,128)S(1)}, f32[6,192,12288]{2,1,0:T(8,128)}) fusion(pred[192,12288]{1,0:T(8,128)(4,1)} %fusion.5, bf16[12288,6,128]{0,2,1:T(8,128)(2,1)} %bitcast.38, bf16[192,768]{1,0:T(8,128)(2,1)S(1)} %get-tuple-element.14), kind=kOutput, calls=%fused_computation.1 | convolution fusion | flops 3666344960 | bytes 78156288 | tf_op jit(solution)/shard_map/cond/branch_1_fun/qhd,khd->hqk/dot_general | solution.py:66
  304.7 27.4 %fusion.2 = f32[6,192,128]{2,1,0:T(8,128)S(1)} fusion(bf16[12288,6,128]{0,2,1:T(8,128)(2,1)} %bitcast.40, f32[6,192,12288]{2,1,0:T(8,128)} %get-tuple-element.37, f32[6,192]{1,0:T(8,128)S(1)} %broadcast_maximum_fusion, pred[192,12288]{1,0:T(8,128)(4,1)} %fusion.5), kind=kOutput, calls=%fused_computation.4 | convolution fusion | flops 3680501760 | bytes 78451200 | tf_op jit(solution)/shard_map/cond/branch_1_fun/hqk,khd->hqd/dot_general | solution.py:77
  332.1 20.3 %fusion.1 = f32[6,192]{1,0:T(8,128)S(1)} fusion(f32[6,192,12288]{2,1,0:T(8,128)} %get-tuple-element.37, f32[6,192]{1,0:T(8,128)S(1)} %broadcast_maximum_fusion, pred[192,12288]{1,0:T(8,128)(4,1)} %fusion.5), kind=kLoop, calls=%fused_computation.3 | loop fusion | flops 56621952 | bytes 58991616 | tf_op jit(solution)/shard_map/cond/branch_1_fun/reduce_sum | solution.py:76
  352.4 0.6 copy-done.3
  353.0 2.2 convolution_convert_fusion
  355.2 0.0 reduce-scatter.2.cloned.1.call-update
  355.3 10.9 %reduce-scatter.2.cloned.1.call-done = bf16[192,768]{1,0:T(8,128)(2,1)} async-done(((bf16[192,1536]{1,0:T(8,128)(2,1)}), bf16[192,768]{1,0:T(8,128)(2,1)}) %reduce-scatter.2.cloned.1.call-update) | async-done | bytes 294928 | tf_op jit(solution)/shard_map/reduce_scatter | solution.py:102
  366.3 1.9 add_convert_fusion
  (20 shorter events, 0.2 us)
Async XLA Ops:
  7.2 345.8 %copy-start = (bf16[768,1536]{1,0:T(8,128)(2,1)S(1)}, bf16[768,1536]{1,0:T(8,128)(2,1)}, u32[]{:S(2)}) copy-start(bf16[768,1536]{1,0:T(8,128)(2,1)} %param.19) | copy-start | bytes 7077892
  7.2 197.0 %all-gather.2.cloned.1.call-start = ((), (), s32[]{:S(2)}) async-start(), calls=%async_computation.1 | async-start | bytes 38338560 | tf_op jit(solution)/shard_map/all_gather | solution.py:90
  17.4 6.4 %copy-start.2 = (f32[3,1536]{1,0:T(4,128)S(1)}, f32[3,1536]{1,0:T(4,128)}, u32[]{:S(2)}) copy-start(f32[3,1536]{1,0:T(4,128)} %param.15) | copy-start | bytes 55300
  17.4 6.4 %copy-start.4 = (bf16[1536,768]{1,0:T(8,128)(2,1)S(1)}, bf16[1536,768]{1,0:T(8,128)(2,1)}, u32[]{:S(2)}) copy-start(bf16[1536,768]{1,0:T(8,128)(2,1)} %param.17) | copy-start | bytes 7077892
  23.8 1.7 copy-start.5
  25.5 1.7 copy-start.6
  27.1 339.2 %reduce-scatter.2.cloned.1.call-start = ((), (), s32[]{:S(2)}) async-start(), calls=%async_computation.2 | async-start | bytes 884736 | tf_op jit(solution)/shard_map/reduce_scatter | solution.py:102
  352.4 0.6 copy-start.3
  353.0 13.3 %copy-start.1 = (bf16[192,768]{1,0:T(8,128)(2,1)S(1)}, bf16[192,768]{1,0:T(8,128)(2,1)}, u32[]{:S(2)}) copy-start(bf16[192,768]{1,0:T(8,128)(2,1)} %param.11) | copy-start | bytes 884740
Sparse Core Ops, SparseCore 0:
  27.2 176.9 all-gather.1
  355.4 10.8 reduce-scatter.1

commit v3 on v1

--- a/solution.py
+++ b/solution.py
@@ -3,15 +3,101 @@
 import jax
 import jax.numpy as jnp
 from jax import lax
+from jax.experimental import pallas as pl
+from jax.experimental.pallas import tpu as pltpu
 from jax.sharding import PartitionSpec as P
 
 HEAD_DIM = 128
 STEPS = 1000
+KEY_BLOCK = 1024
 
 
 def noise_level(step_value):
     frac = step_value / STEPS
     return 5.0 * frac / (1.0 + 4.0 * frac)
+
+
+def attention_kernel(span_ref, query_ref, key_ref, value_ref, low_ref, high_ref, out_ref,
+                     max_ref, sum_ref, acc_ref):
+    block = pl.program_id(0)
+    heads = query_ref.shape[1] // HEAD_DIM
+    first = span_ref[0] // KEY_BLOCK
+    last = (span_ref[1] - 1) // KEY_BLOCK
+
+    @pl.when(block == 0)
+    def _():
+        max_ref[...] = jnp.full(max_ref.shape, -1e30, jnp.float32)
+        sum_ref[...] = jnp.zeros(sum_ref.shape, jnp.float32)
+        acc_ref[...] = jnp.zeros(acc_ref.shape, jnp.float32)
+
+    @pl.when(jnp.logical_and(block >= first, block <= last))
+    def _():
+        rows = query_ref.shape[0]
+        key_index = block * KEY_BLOCK + lax.broadcasted_iota(jnp.int32, (rows, KEY_BLOCK), 1)
+        valid = jnp.logical_and(key_index >= low_ref[...], key_index < high_ref[...])
+        for head in range(heads):
+            cols = slice(head * HEAD_DIM, (head + 1) * HEAD_DIM)
+            scores = lax.dot_general(
+                query_ref[:, cols], key_ref[:, cols], (((1,), (1,)), ((), ())),
+                preferred_element_type=jnp.float32,
+            ) * (1.0 / math.sqrt(HEAD_DIM))
+            old_max = max_ref[head]
+            new_max = jnp.maximum(
+                old_max, jnp.max(jnp.where(valid, scores, -1e30), axis=1, keepdims=True)
+            )
+            probs = jnp.where(valid, jnp.exp(scores - new_max), 0.0)
+            alpha = jnp.exp(old_max - new_max)
+            sum_ref[head] = alpha * sum_ref[head] + jnp.sum(probs, axis=1, keepdims=True)
+            acc_ref[:, cols] = alpha * acc_ref[:, cols] + jnp.dot(
+                probs.astype(jnp.bfloat16), value_ref[:, cols],
+                preferred_element_type=jnp.float32,
+            )
+            max_ref[head] = new_max
+
+    @pl.when(block == pl.num_programs(0) - 1)
+    def _():
+        for head in range(heads):
+            cols = slice(head * HEAD_DIM, (head + 1) * HEAD_DIM)
+            out_ref[:, cols] = (acc_ref[:, cols] / sum_ref[head]).astype(out_ref.dtype)
+
+
+def attention(span, query, packed, query_low, query_high):
+    rows, width = query.shape
+    blocks = packed.shape[0] // KEY_BLOCK
+
+    def key_map(block, span_ref):
+        first = span_ref[0] // KEY_BLOCK
+        last = (span_ref[1] - 1) // KEY_BLOCK
+        return (jnp.minimum(jnp.maximum(block, first), last), 0)
+
+    def value_map(block, span_ref):
+        first = span_ref[0] // KEY_BLOCK
+        last = (span_ref[1] - 1) // KEY_BLOCK
+        return (jnp.minimum(jnp.maximum(block, first), last), 1)
+
+    whole = lambda block, span_ref: (0, 0)
+    heads = width // HEAD_DIM
+    return pl.pallas_call(
+        attention_kernel,
+        grid_spec=pltpu.PrefetchScalarGridSpec(
+            num_scalar_prefetch=1,
+            grid=(blocks,),
+            in_specs=[
+                pl.BlockSpec((rows, width), whole),
+                pl.BlockSpec((KEY_BLOCK, width), key_map),
+                pl.BlockSpec((KEY_BLOCK, width), value_map),
+                pl.BlockSpec((rows, 1), whole),
+                pl.BlockSpec((rows, 1), whole),
+            ],
+            out_specs=pl.BlockSpec((rows, width), whole),
+            scratch_shapes=[
+                pltpu.VMEM((heads, rows, 1), jnp.float32),
+                pltpu.VMEM((heads, rows, 1), jnp.float32),
+                pltpu.VMEM((rows, width), jnp.float32),
+            ],
+        ),
+        out_shape=jax.ShapeDtypeStruct((rows, width), jnp.bfloat16),
+    )(span, query, packed, packed, query_low, query_high)
 
 
 def on_device(
@@ -43,8 +129,6 @@
     query = jnp.dot(normed, w_query, preferred_element_type=jnp.float32).astype(jnp.bfloat16)
     keys = jnp.dot(normed, w_key, preferred_element_type=jnp.float32).astype(jnp.bfloat16)
     values = jnp.dot(normed, w_value, preferred_element_type=jnp.float32).astype(jnp.bfloat16)
-    heads_here = query.shape[1] // HEAD_DIM
-    query_heads = query.reshape(tok_rows, heads_here, HEAD_DIM)
     start_row = lax.axis_index("req") * tok_rows
     query_index = start_row + jnp.arange(tok_rows, dtype=jnp.int32)
     video_ends = jnp.cumsum(video_lengths)
@@ -54,28 +138,9 @@
     )
     query_low = jnp.sum(jnp.where(inside, video_starts[None, :], 0), axis=1)
     query_high = jnp.sum(jnp.where(inside, video_ends[None, :], 0), axis=1)
-    key_index = jnp.arange(tok_rows * lax.psum(1, "req"), dtype=jnp.int32)
-    valid = jnp.logical_and(
-        key_index[None, :] >= query_low[:, None], key_index[None, :] < query_high[:, None]
-    )
-    outputs = []
-    for head in range(heads_here):
-        cols = slice(head * HEAD_DIM, (head + 1) * HEAD_DIM)
-        packed = jnp.concatenate([keys[:, cols], values[:, cols]], axis=1)
-        gathered = lax.all_gather(packed, "req", axis=0, tiled=True)
-        key_head = gathered[:, :HEAD_DIM]
-        value_head = gathered[:, HEAD_DIM:]
-        scores = jnp.dot(
-            query[:, cols], key_head.T, preferred_element_type=jnp.float32
-        ) / math.sqrt(HEAD_DIM)
-        row_max = jnp.max(jnp.where(valid, scores, -1e30), axis=1, keepdims=True)
-        probs = jnp.where(valid, jnp.exp(scores - row_max), 0.0)
-        row_sum = jnp.sum(probs, axis=1, keepdims=True)
-        weighted = jnp.dot(
-            probs.astype(jnp.bfloat16), value_head, preferred_element_type=jnp.float32
-        )
-        outputs.append((weighted / row_sum).astype(jnp.bfloat16))
-    attended = jnp.concatenate(outputs, axis=1)
+    span = jnp.stack([jnp.min(query_low), jnp.max(query_high)]).astype(jnp.int32)
+    packed = lax.all_gather(jnp.concatenate([keys, values], axis=1), "req", axis=0, tiled=True)
+    attended = attention(span, query, packed, query_low[:, None], query_high[:, None])
     partial_value = jnp.dot(attended, w_out, preferred_element_type=jnp.float32)
     own_sum = lax.psum_scatter(
         partial_value.astype(jnp.bfloat16), "tp", scatter_dimension=1, tiled=True

time: 574 us -> 269 us (0.47)
  waiting for transfers between devices: 409 us -> 184 us
  matrix products: 114 us -> 13.4 us
  Pallas kernels: 0 us -> 37.6 us
  other arithmetic: 20.1 us -> 6.8 us
    all_gather x6 -> x1, waiting for transfers between devices: 398 us -> 169 us  [on_device(): lax.all_gather(jnp.concatenate([keys, values], axis=1), 'req', axis=0, ti...]
    dot_general x12 -> x0, matrix products: 100 us -> none  [the longest x6 64.1 us: on_device(): jnp.dot(query[:, cols], key_head.T, preferred_element_type=jnp.float32)]
    pallas_call x0 -> x1, Pallas kernels: none -> 37.6 us  [attention(): pl.pallas_call(attention_kernel, grid_spec=pltpu.PrefetchScalarGridSpec(n...]
    reduce_sum x1 -> x0, other arithmetic: 13.4 us -> none  [on_device(): row_sum = jnp.sum(probs, axis=1, keepdims=True)]
  transfers between devices with their start and end apart: 7 -> 2, of which waited for: 7 -> 2; matrix products, arithmetic and copies ran while one was open for 8% -> 3% of each run, Pallas kernels for 0% -> 0%
where the time goes in v3:
time: 269 us; the launch traced here: 268 us
  waiting for transfers between devices  184 us (68%)
  Pallas kernels  37.6 us (14%)
  between operations  14.9 us (6%)
  matrix products  13.4 us (5%)
  local copies, waits for them, and re-layouts  8.53 us (3%)
  other arithmetic  6.8 us (3%)
  blocking collectives  2.87 us (1%)
    all_gather x1, waiting for transfers between devices, on_device(): lax.all_gather(jnp.concatenate([keys, values], axis=1), 'req', axis=0, ti...  169 us
    pallas_call x1, Pallas kernels, attention(): pl.pallas_call(attention_kernel, grid_spec=pltpu.PrefetchScalarGridSpec(n...  37.6 us
    reduce_scatter x1, waiting for transfers between devices, on_device(): lax.psum_scatter(partial_value.astype(jnp.bfloat16), 'tp', scatter_dimens...  14.7 us
    unnamed x13, local copies, waits for them, and re-layouts  6.99 us
    dot_general x1, matrix products, on_device(): jnp.dot(jax.nn.silu(embedding)[None, :], time_weight, precision=lax.Preci...  6.35 us
  transfers between devices with their start and end apart: 2, of which 2 were waited for; matrix products, arithmetic and copies ran while one was open for 3% of the time, Pallas kernels for 0%

profile of v3, /device:TPU:17, one launch (start us, length us, event | category | flops | bytes accessed | tf_op | source)
XLA Modules:
  0.0 267.8 jit_solution(7193358374950862067)
XLA Ops:
  7.2 0.0 copy-start
  7.2 0.0 all-gather.2.cloned.1.call-start
  7.2 2.9 %all_gather.6 = bf16[192,1536]{1,0:T(8,128)(2,1)S(1)} all-gather(bf16[192,768]{1,0:T(8,128)(2,1)} %param.9), channel_id=1, replica_groups=mesh['req'=64,'tp'=2] {'tp'}, dimensions={1}, use_global_device_ids=true | all-gather | bytes 884736 | tf_op jit(solution)/shard_map/all_gather | solution.py:108
  10.9 6.0 %copy.14 = f32[256,4608]{0,1:T(8,128)} copy(f32[256,4608]{1,0:T(8,128)} %param.12) | data formatting | bytes 9437184 | tf_op args[3]
  16.9 0.0 copy-start.2
  16.9 0.0 copy-start.3
  16.9 6.4 %fusion.13 = f32[1,3,1536]{2,0,1:T(1,128)S(1)} fusion(f32[256,1,1]{0,1,2:T(1,128)S(1)} %bitcast.25, f32[3,1536,256]{2,1,0:T(8,128)} %bitcast.22), kind=kOutput, calls=%fused_computation.34 | convolution fusion | flops 14155776 | bytes 4738048 | tf_op jit(solution)/shard_map/dot_general | solution.py:116
  23.4 0.2 convert_reduce_fusion
  23.5 0.3 fusion.2
  23.8 0.0 copy-start.4
  23.9 0.7 convolution_convert_fusion.1
  24.6 0.9 copy-done.4
  25.5 0.7 convolution_convert_fusion.2
  26.3 0.0 copy-start.5
  26.3 0.9 pad_maximum_fusion
  27.1 0.0 all-gather.2.cloned.1.call-update
  27.2 0.0 reduce-scatter.2.cloned.1.call-start
  27.2 0.2 reduce-window.8
  27.4 0.1 select_reduce_fusion.1
  27.5 0.6 reduce_min.9
  28.1 0.8 copy.15.low_ref
  28.9 0.6 reduce_max.9
  29.5 0.8 copy.16.high_ref
  30.3 1.9 pad_add_fusion.span_ref
  32.2 3.1 %convolution_convert_fusion.3.query_ref = bf16[192,768]{1,0:T(8,128)(2,1)} fusion(bf16[1536,768]{1,0:T(8,128)(2,1)} %param.14, bf16[192,1536]{1,0:T(8,128)(2,1)S(1)} %all_gather.6, f32[1536]{0:T(1024)S(1)} %get-tuple-element.3, f32[1536]{0:T(1024)S(1)} %get-tuple-element.2, f32[192]{0:T(256)S(1)} %add_rsqrt_fusion, f32[192]{0:T(256)S(1)} %broadcast_multiply_fusion), kind=kOutput, calls=%fused_computation.7 | convolution fusion | flops 454901760 | bytes 3257856 | tf_op jit(solution)/shard_map/dot_general | solution.py:129
  35.3 169.0 %all-gather.2.cloned.1.call-done.key_ref.value_ref = bf16[12288,1536]{1,0:T(8,128)(2,1)} async-done(((bf16[192,1536]{1,0:T(8,128)(2,1)}), bf16[12288,1536]{1,0:T(8,128)(2,1)}) %all-gather.2.cloned.1.call-update) | async-done | bytes 37748752 | tf_op jit(solution)/shard_map/all_gather | solution.py:142
  204.3 37.6 %shard_map.104 = bf16[192,768]{1,0:T(8,128)(2,1)} custom-call(s32[2]{0:T(128)} %pad_add_fusion.span_ref, bf16[192,768]{1,0:T(8,128)(2,1)} %convolution_convert_fusion.3.query_ref, bf16[12288,1536]{1,0:T(8,128)(2,1)} %all-gather.2.cloned.1.call-done.key_ref.value_ref, bf16[12288,1536]{1,0:T(8,128)(2,1)} %all-gather.2.cloned.1.call-done.key_ref.value_ref, ...), custom_call_target="tpu_custom_call" | custom-call | tf_op jit(solution)/shard_map/pallas_call | solution.py:80
  241.9 2.4 convolution_convert_fusion
  244.3 0.0 reduce-scatter.2.cloned.1.call-update
  244.4 14.7 %reduce-scatter.2.cloned.1.call-done = bf16[192,768]{1,0:T(8,128)(2,1)} async-done(((bf16[192,1536]{1,0:T(8,128)(2,1)}), bf16[192,768]{1,0:T(8,128)(2,1)}) %reduce-scatter.2.cloned.1.call-update) | async-done | bytes 294928 | tf_op jit(solution)/shard_map/reduce_scatter | solution.py:145
  259.1 0.0 copy-done.1
  259.1 1.9 add_convert_fusion
  (14 shorter events, 0.2 us)
Async XLA Ops:
  7.2 234.7 %copy-start = (bf16[768,1536]{1,0:T(8,128)(2,1)S(1)}, bf16[768,1536]{1,0:T(8,128)(2,1)}, u32[]{:S(2)}) copy-start(bf16[768,1536]{1,0:T(8,128)(2,1)} %param.17) | copy-start | bytes 7077892
  7.2 197.1 %all-gather.2.cloned.1.call-start = ((), (), s32[]{:S(2)}) async-start(), calls=%async_computation.1 | async-start | bytes 38338560 | tf_op jit(solution)/shard_map/all_gather | solution.py:142
  16.9 6.4 %copy-start.2 = (f32[3,1536]{1,0:T(4,128)S(1)}, f32[3,1536]{1,0:T(4,128)}, u32[]{:S(2)}) copy-start(f32[3,1536]{1,0:T(4,128)} %param.13) | copy-start | bytes 55300
  16.9 6.9 %copy-start.3 = (bf16[1536,768]{1,0:T(8,128)(2,1)S(1)}, bf16[1536,768]{1,0:T(8,128)(2,1)}, u32[]{:S(2)}) copy-start(bf16[1536,768]{1,0:T(8,128)(2,1)} %param.16) | copy-start | bytes 7077892
  23.8 1.7 copy-start.4
  26.3 1.0 copy-start.5
  27.2 231.9 %reduce-scatter.2.cloned.1.call-start = ((), (), s32[]{:S(2)}) async-start(), calls=%async_computation.2 | async-start | bytes 884736 | tf_op jit(solution)/shard_map/reduce_scatter | solution.py:145
  241.9 17.2 %copy-start.1 = (bf16[192,768]{1,0:T(8,128)(2,1)S(1)}, bf16[192,768]{1,0:T(8,128)(2,1)}, u32[]{:S(2)}) copy-start(bf16[192,768]{1,0:T(8,128)(2,1)} %param.9) | copy-start | bytes 884740
Sparse Core Ops, SparseCore 0:
  27.3 176.9 all-gather.1
  244.4 14.6 reduce-scatter.1

commit v4 on v3

--- a/solution.py
+++ b/solution.py
@@ -129,8 +129,19 @@
     query = jnp.dot(normed, w_query, preferred_element_type=jnp.float32).astype(jnp.bfloat16)
     keys = jnp.dot(normed, w_key, preferred_element_type=jnp.float32).astype(jnp.bfloat16)
     values = jnp.dot(normed, w_value, preferred_element_type=jnp.float32).astype(jnp.bfloat16)
-    start_row = lax.axis_index("req") * tok_rows
-    query_index = start_row + jnp.arange(tok_rows, dtype=jnp.int32)
+    group_width = query.shape[1] // 2
+    groups = []
+    for group in range(2):
+        cols = slice(group * group_width, (group + 1) * group_width)
+        groups.append(jnp.concatenate([keys[:, cols], values[:, cols], query[:, cols]], axis=1))
+    swapped = lax.all_to_all(
+        jnp.concatenate(groups, axis=0), "pair", split_axis=0, concat_axis=0, tiled=True
+    )
+    pair_rows = swapped.shape[0]
+    kv_local = swapped[:, : 2 * group_width]
+    query_local = swapped[:, 2 * group_width :]
+    start_row = lax.axis_index("r") * pair_rows
+    query_index = start_row + jnp.arange(pair_rows, dtype=jnp.int32)
     video_ends = jnp.cumsum(video_lengths)
     video_starts = video_ends - video_lengths
     inside = jnp.logical_and(
@@ -139,8 +150,9 @@
     query_low = jnp.sum(jnp.where(inside, video_starts[None, :], 0), axis=1)
     query_high = jnp.sum(jnp.where(inside, video_ends[None, :], 0), axis=1)
     span = jnp.stack([jnp.min(query_low), jnp.max(query_high)]).astype(jnp.int32)
-    packed = lax.all_gather(jnp.concatenate([keys, values], axis=1), "req", axis=0, tiled=True)
-    attended = attention(span, query, packed, query_low[:, None], query_high[:, None])
+    packed = lax.all_gather(kv_local, "r", axis=0, tiled=True)
+    attended_local = attention(span, query_local, packed, query_low[:, None], query_high[:, None])
+    attended = lax.all_to_all(attended_local, "pair", split_axis=0, concat_axis=1, tiled=True)
     partial_value = jnp.dot(attended, w_out, preferred_element_type=jnp.float32)
     own_sum = lax.psum_scatter(
         partial_value.astype(jnp.bfloat16), "tp", scatter_dimension=1, tiled=True
@@ -154,11 +166,16 @@
 
 
 def solution(mesh):
+    req_size, tp_size = mesh.devices.shape
+    split_mesh = jax.sharding.Mesh(
+        mesh.devices.reshape(req_size // 2, 2, tp_size), ("r", "pair", "tp")
+    )
+    rows = ("r", "pair")
     return jax.shard_map(
         on_device,
-        mesh=mesh,
+        mesh=split_mesh,
         in_specs=(
-            P("req", "tp"),
+            P(rows, "tp"),
             P(),
             P(),
             P(),
@@ -168,6 +185,6 @@
             P(None, "tp"),
             P("tp", None),
         ),
-        out_specs=(P("req", "tp"), P("req", "tp")),
+        out_specs=(P(rows, "tp"), P(rows, "tp")),
         check_vma=False,
     )

time: 269 us -> 281 us (1.045)
  blocking collectives: 2.87 us -> 24.4 us
  Pallas kernels: 37.6 us -> 30.7 us
  matrix products: 13.4 us -> 9.99 us
    all_to_all x0 -> x2, blocking collectives: none -> 21.5 us  [the longest x1 13.8 us: on_device(): lax.all_to_all(jnp.concatenate(groups, axis=0), 'pair', split_axis=0, con...]
    pallas_call x1, Pallas kernels: 37.6 us -> 30.7 us  [attention(): pl.pallas_call(attention_kernel, grid_spec=pltpu.PrefetchScalarGridSpec(n...]
    all_gather x1, waiting for transfers between devices: 169 us -> 165 us  [on_device(): packed = lax.all_gather(kv_local, 'r', axis=0, tiled=True)]
    unnamed x13 -> x15, local copies, waits for them, and re-layouts: 6.99 us -> 7.84 us
  transfers between devices with their start and end apart: 2 -> 2, of which waited for: 2 -> 2; matrix products, arithmetic and copies ran while one was open for 3% -> 2% of each run, Pallas kernels for 0% -> 0%
where the time goes in v4:
time: 281 us; the launch traced here: 280 us
  waiting for transfers between devices  183 us (65%)
  Pallas kernels  30.7 us (11%)
  blocking collectives  24.4 us (9%)
  between operations  15 us (5%)
  local copies, waits for them, and re-layouts  11.2 us (4%)
  matrix products  9.99 us (4%)
  other arithmetic  6.01 us (2%)
    all_gather x1, waiting for transfers between devices, on_device(): packed = lax.all_gather(kv_local, 'r', axis=0, tiled=True)  165 us
    pallas_call x1, Pallas kernels, attention(): pl.pallas_call(attention_kernel, grid_spec=pltpu.PrefetchScalarGridSpec(n...  30.7 us
    reduce_scatter x1, waiting for transfers between devices, on_device(): lax.psum_scatter(partial_value.astype(jnp.bfloat16), 'tp', scatter_dimens...  17.3 us
    all_to_all x1, blocking collectives, on_device(): lax.all_to_all(jnp.concatenate(groups, axis=0), 'pair', split_axis=0, con...  13.8 us
    unnamed x15, local copies, waits for them, and re-layouts  7.84 us
    all_to_all x1, blocking collectives, on_device(): lax.all_to_all(attended_local, 'pair', split_axis=0, concat_axis=1, tiled...  7.63 us
    dot_general x1, matrix products, on_device(): jnp.dot(jax.nn.silu(embedding)[None, :], time_weight, precision=lax.Preci...  6.35 us
  transfers between devices with their start and end apart: 2, of which 2 were waited for; matrix products, arithmetic and copies ran while one was open for 2% of the time, Pallas kernels for 0%

profile of v4, /device:TPU:17, one launch (start us, length us, event | category | flops | bytes accessed | tf_op | source)
XLA Modules:
  0.0 280.1 jit_solution(6400092910715694215)
XLA Ops:
  7.2 0.0 copy-start
  7.2 0.0 all-gather.2.cloned.1.call-start
  7.2 2.9 %all_gather.6 = bf16[192,1536]{1,0:T(8,128)(2,1)S(1)} all-gather(bf16[192,768]{1,0:T(8,128)(2,1)} %param.9), channel_id=1, replica_groups=mesh['r'=32,'pair'=2,'tp'=2] {'tp'}, dimensions={1}, use_global_device_ids=true | all-gather | bytes 884736 | tf_op jit(solution)/shard_map/all_gather | solution.py:108
  10.9 6.0 %copy.19 = f32[256,4608]{0,1:T(8,128)} copy(f32[256,4608]{1,0:T(8,128)} %param.12) | data formatting | bytes 9437184 | tf_op args[3]
  16.9 6.4 %fusion.16 = f32[1,3,1536]{2,0,1:T(1,128)S(1)} fusion(f32[256,1,1]{0,1,2:T(1,128)S(1)} %bitcast.33, f32[3,1536,256]{2,1,0:T(8,128)} %bitcast.26), kind=kOutput, calls=%fused_computation.37 | convolution fusion | flops 14155776 | bytes 4738048 | tf_op jit(solution)/shard_map/dot_general | solution.py:116
  23.4 0.2 convert_reduce_fusion
  23.5 0.3 fusion.2
  23.9 0.7 convolution_convert_fusion.1
  24.7 0.9 copy-done.4
  25.5 0.7 convolution_convert_fusion.2
  26.3 0.9 copy-done.5
  27.2 0.7 convolution_convert_fusion.3
  28.0 0.1 maximum_maximum_fusion
  28.1 13.8 %all_to_all.31 = bf16[2,192,1152]{2,1,0:T(8,128)(2,1)S(1)} all-to-all(bf16[2,192,1152]{2,1,0:T(8,128)(2,1)S(1)} %bitcast.29), channel_id=1, replica_groups=mesh['r'=32,'pair'=2,'tp'=2] {'pair'}, dimensions={0} | all-to-all | bytes 1769472 | tf_op jit(solution)/shard_map/all_to_all | solution.py:137
  41.9 0.9 slice.54
  42.8 0.0 all-gather.2.cloned.1.call-update
  42.8 0.0 reduce-scatter.2.cloned.1.call-start
  42.9 0.2 reduce-window.8
  43.1 0.1 select_reduce_fusion.1
  43.1 0.8 broadcast_in_dim.35.high_ref
  43.9 0.6 reduce_max.9
  44.6 0.8 broadcast_in_dim.34.low_ref
  45.4 0.6 reduce_min.9
  46.0 1.9 pad_add_fusion.span_ref
  47.9 0.7 slice.53.query_ref
  48.7 165.4 %all-gather.2.cloned.1.call-done.key_ref.value_ref = bf16[12288,768]{1,0:T(8,128)(2,1)} async-done(((bf16[384,768]{1,0:T(8,128)(2,1)}), bf16[12288,768]{1,0:T(8,128)(2,1)}) %all-gather.2.cloned.1.call-update) | async-done | bytes 18874384 | tf_op jit(solution)/shard_map/all_gather | solution.py:153
  214.1 30.7 %shard_map.104 = bf16[384,384]{1,0:T(8,128)(2,1)} custom-call(s32[2]{0:T(128)} %pad_add_fusion.span_ref, bf16[384,384]{1,0:T(8,128)(2,1)} %slice.53.query_ref, bf16[12288,768]{1,0:T(8,128)(2,1)} %all-gather.2.cloned.1.call-done.key_ref.value_ref, bf16[12288,768]{1,0:T(8,128)(2,1)} %all-gather.2.cloned.1.call-done.key_ref.value_ref, ...), custom_call_target="tpu_custom_call" | custom-call | tf_op jit(solution)/shard_map/pallas_call | solution.py:80
  244.8 7.6 %all_to_all.32 = bf16[2,192,384]{2,1,0:T(8,128)(2,1)S(1)} all-to-all(bf16[2,192,384]{2,1,0:T(8,128)(2,1)} %bitcast.30), channel_id=1, replica_groups=mesh['r'=32,'pair'=2,'tp'=2] {'pair'}, dimensions={0} | all-to-all | bytes 589824 | tf_op jit(solution)/shard_map/all_to_all | solution.py:155
  252.5 1.4 convolution_convert_fusion
  253.9 0.0 reduce-scatter.2.cloned.1.call-update
  254.1 17.3 %reduce-scatter.2.cloned.1.call-done = bf16[192,768]{1,0:T(8,128)(2,1)} async-done(((bf16[192,1536]{1,0:T(8,128)(2,1)}), bf16[192,768]{1,0:T(8,128)(2,1)}) %reduce-scatter.2.cloned.1.call-update) | async-done | bytes 294928 | tf_op jit(solution)/shard_map/reduce_scatter | solution.py:157
  271.3 1.9 add_convert_fusion
  (24 shorter events, 0.3 us)
Async XLA Ops:
  7.2 245.3 %copy-start = (bf16[768,1536]{1,0:T(8,128)(2,1)S(1)}, bf16[768,1536]{1,0:T(8,128)(2,1)}, u32[]{:S(2)}) copy-start(bf16[768,1536]{1,0:T(8,128)(2,1)} %param.17) | copy-start | bytes 7077892
  7.2 206.9 %all-gather.2.cloned.1.call-start = ((), (), s32[]{:S(2)}) async-start(), calls=%async_computation.3 | async-start | bytes 19464192 | tf_op jit(solution)/shard_map/all_gather | solution.py:153
  16.9 6.4 %copy-start.2 = (f32[3,1536]{1,0:T(4,128)S(1)}, f32[3,1536]{1,0:T(4,128)}, u32[]{:S(2)}) copy-start(f32[3,1536]{1,0:T(4,128)} %param.13) | copy-start | bytes 55300
  16.9 6.9 %copy-start.3 = (bf16[1536,768]{1,0:T(8,128)(2,1)S(1)}, bf16[1536,768]{1,0:T(8,128)(2,1)}, u32[]{:S(2)}) copy-start(bf16[1536,768]{1,0:T(8,128)(2,1)} %param.14) | copy-start | bytes 7077892
  23.8 1.7 copy-start.4
  25.5 1.7 copy-start.5
  28.1 14.8 %copy-start.6 = (s32[5]{0:T(128)S(1)}, s32[5]{0:T(128)}, u32[]{:S(2)}) copy-start(s32[5]{0:T(128)} %param.10) | copy-start | bytes 64
  42.8 228.5 %reduce-scatter.2.cloned.1.call-start = ((), (), s32[]{:S(2)}) async-start(), calls=%async_computation.4 | async-start | bytes 884736 | tf_op jit(solution)/shard_map/reduce_scatter | solution.py:157
  252.5 18.8 %copy-start.1 = (bf16[192,768]{1,0:T(8,128)(2,1)S(1)}, bf16[192,768]{1,0:T(8,128)(2,1)}, u32[]{:S(2)}) copy-start(bf16[192,768]{1,0:T(8,128)(2,1)} %param.9) | copy-start | bytes 884740
Sparse Core Ops, SparseCore 0:
  42.9 171.1 all-gather.1
  254.1 17.1 reduce-scatter.1

commit v5 on v3

--- a/solution.py
+++ b/solution.py
@@ -10,6 +10,7 @@
 HEAD_DIM = 128
 STEPS = 1000
 KEY_BLOCK = 1024
+EXP2_SCALE = math.log2(math.e) / math.sqrt(HEAD_DIM)
 
 
 def noise_level(step_value):
@@ -30,29 +31,46 @@
         sum_ref[...] = jnp.zeros(sum_ref.shape, jnp.float32)
         acc_ref[...] = jnp.zeros(acc_ref.shape, jnp.float32)
 
-    @pl.when(jnp.logical_and(block >= first, block <= last))
-    def _():
+    def step(masked):
         rows = query_ref.shape[0]
-        key_index = block * KEY_BLOCK + lax.broadcasted_iota(jnp.int32, (rows, KEY_BLOCK), 1)
-        valid = jnp.logical_and(key_index >= low_ref[...], key_index < high_ref[...])
+        if masked:
+            key_index = block * KEY_BLOCK + lax.broadcasted_iota(jnp.int32, (rows, KEY_BLOCK), 1)
+            valid = jnp.logical_and(key_index >= low_ref[...], key_index < high_ref[...])
         for head in range(heads):
             cols = slice(head * HEAD_DIM, (head + 1) * HEAD_DIM)
-            scores = lax.dot_general(
+            raw = lax.dot_general(
                 query_ref[:, cols], key_ref[:, cols], (((1,), (1,)), ((), ())),
                 preferred_element_type=jnp.float32,
-            ) * (1.0 / math.sqrt(HEAD_DIM))
+            )
             old_max = max_ref[head]
-            new_max = jnp.maximum(
-                old_max, jnp.max(jnp.where(valid, scores, -1e30), axis=1, keepdims=True)
-            )
-            probs = jnp.where(valid, jnp.exp(scores - new_max), 0.0)
-            alpha = jnp.exp(old_max - new_max)
+            if masked:
+                block_max = jnp.max(jnp.where(valid, raw, -1e30), axis=1, keepdims=True)
+            else:
+                block_max = jnp.max(raw, axis=1, keepdims=True)
+            new_max = jnp.maximum(old_max, block_max)
+            probs = jnp.exp2((raw - new_max) * EXP2_SCALE)
+            if masked:
+                probs = jnp.where(valid, probs, 0.0)
+            alpha = jnp.exp2((old_max - new_max) * EXP2_SCALE)
             sum_ref[head] = alpha * sum_ref[head] + jnp.sum(probs, axis=1, keepdims=True)
             acc_ref[:, cols] = alpha * acc_ref[:, cols] + jnp.dot(
                 probs.astype(jnp.bfloat16), value_ref[:, cols],
                 preferred_element_type=jnp.float32,
             )
             max_ref[head] = new_max
+
+    touched = jnp.logical_and(block >= first, block <= last)
+    whole_block = jnp.logical_and(
+        block * KEY_BLOCK >= span_ref[2], (block + 1) * KEY_BLOCK <= span_ref[3]
+    )
+
+    @pl.when(jnp.logical_and(touched, whole_block))
+    def _():
+        step(False)
+
+    @pl.when(jnp.logical_and(touched, jnp.logical_not(whole_block)))
+    def _():
+        step(True)
 
     @pl.when(block == pl.num_programs(0) - 1)
     def _():
@@ -113,12 +131,9 @@
     frequency = jnp.exp(-math.log(10000.0) * jnp.arange(half_freq, dtype=jnp.float32) / half_freq)
     angle = 1000.0 * sigma * frequency
     embedding = jnp.concatenate([jnp.cos(angle), jnp.sin(angle)])
-    modulation = jnp.dot(
-        jax.nn.silu(embedding)[None, :],
-        time_weight,
-        precision=lax.Precision.HIGHEST,
-        preferred_element_type=jnp.float32,
-    )[0]
+    modulation = jnp.sum(
+        jax.nn.silu(embedding)[:, None] * time_weight, axis=0
+    )
     modulation = modulation.reshape(3, width) + block_mod
     shift, scale, gate = (modulation[0], modulation[1], modulation[2])
     as_float = full_rows.astype(jnp.float32)
@@ -138,7 +153,9 @@
     )
     query_low = jnp.sum(jnp.where(inside, video_starts[None, :], 0), axis=1)
     query_high = jnp.sum(jnp.where(inside, video_ends[None, :], 0), axis=1)
-    span = jnp.stack([jnp.min(query_low), jnp.max(query_high)]).astype(jnp.int32)
+    span = jnp.stack(
+        [jnp.min(query_low), jnp.max(query_high), jnp.max(query_low), jnp.min(query_high)]
+    ).astype(jnp.int32)
     packed = lax.all_gather(jnp.concatenate([keys, values], axis=1), "req", axis=0, tiled=True)
     attended = attention(span, query, packed, query_low[:, None], query_high[:, None])
     partial_value = jnp.dot(attended, w_out, preferred_element_type=jnp.float32)

time: 269 us -> 254 us (0.944)
  local copies, waits for them, and re-layouts: 8.53 us -> 1.59 us
  Pallas kernels: 37.6 us -> 31.3 us
  matrix products: 13.4 us -> 8.84 us
  other arithmetic: 6.8 us -> 10.5 us
    unnamed x13 -> x10, local copies, waits for them, and re-layouts: 6.99 us -> 0.03 us
    dot_general x1 -> x0, matrix products: 6.35 us -> none  [on_device(): jnp.dot(jax.nn.silu(embedding)[None, :], time_weight, precision=lax.Preci...]
    pallas_call x1, Pallas kernels: 37.6 us -> 31.3 us  [attention(): pl.pallas_call(attention_kernel, grid_spec=pltpu.PrefetchScalarGridSpec(n...]
    reduce_sum x0 -> x1, other arithmetic: none -> 2.91 us  [on_device(): modulation = jnp.sum(jax.nn.silu(embedding)[:, None] * time_weight, axis=0)]
  transfers between devices with their start and end apart: 2 -> 2, of which waited for: 2 -> 2; matrix products, arithmetic and copies ran while one was open for 3% -> 4% of each run, Pallas kernels for 0% -> 0%
where the time goes in v5:
time: 254 us; the launch traced here: 253 us
  waiting for transfers between devices  183 us (72%)
  Pallas kernels  31.3 us (12%)
  between operations  14.9 us (6%)
  other arithmetic  10.5 us (4%)
  matrix products  8.84 us (3%)
  blocking collectives  2.87 us (1%)
    all_gather x1, waiting for transfers between devices, on_device(): lax.all_gather(jnp.concatenate([keys, values], axis=1), 'req', axis=0, ti...  168 us
    pallas_call x1, Pallas kernels, attention(): pl.pallas_call(attention_kernel, grid_spec=pltpu.PrefetchScalarGridSpec(n...  31.3 us
    reduce_scatter x1, waiting for transfers between devices, on_device(): lax.psum_scatter(partial_value.astype(jnp.bfloat16), 'tp', scatter_dimens...  14.6 us
  transfers between devices with their start and end apart: 2, of which 2 were waited for; matrix products, arithmetic and copies ran while one was open for 4% of the time, Pallas kernels for 0%

profile of v5, /device:TPU:17, one launch (start us, length us, event | category | flops | bytes accessed | tf_op | source)
XLA Modules:
  0.0 252.9 jit_solution(1546816133176542854)
XLA Ops:
  7.2 0.0 copy-start
  7.2 0.0 all-gather.2.cloned.1.call-start
  7.2 2.9 %all_gather.6 = bf16[192,1536]{1,0:T(8,128)(2,1)S(1)} all-gather(bf16[192,768]{1,0:T(8,128)(2,1)} %param.9), channel_id=1, replica_groups=mesh['req'=64,'tp'=2] {'tp'}, dimensions={1}, use_global_device_ids=true | all-gather | bytes 884736 | tf_op jit(solution)/shard_map/all_gather | solution.py:126
  10.9 0.0 copy-start.2
  10.9 2.9 %multiply_reduce_fusion = f32[4608]{0:T(1024)S(1)} fusion(f32[256,4608]{1,0:T(8,128)} %param.12, f32[256]{0:T(256)S(1)} %divide_multiply_fusion), kind=kLoop, calls=%fused_computation | loop fusion | flops 2354688 | bytes 4738048 | tf_op jit(solution)/shard_map/reduce_sum | solution.py:134
  13.8 0.0 copy-done.2
  13.9 0.2 convert_reduce_fusion
  14.1 0.3 fusion.2
  14.4 0.0 copy-start.3
  14.4 2.5 %convolution_convert_fusion.1 = bf16[192,768]{1,0:T(8,128)(2,1)S(1)} fusion(bf16[1536,768]{1,0:T(8,128)(2,1)} %param.16, bf16[192,1536]{1,0:T(8,128)(2,1)S(1)} %all_gather.6, f32[1536]{0:T(1024)S(1)} %get-tuple-element.3, f32[1536]{0:T(1024)S(1)} %get-tuple-element.2, f32[192]{0:T(256)S(1)} %add_rsqrt_fusion, f32[192]{0:T(256)S(1)} %broadcast_multiply_fusion), kind=kOutput, calls=%fused_computation.6 | convolution fusion | flops 454901760 | bytes 3257856 | tf_op jit(solution)/shard_map/dot_general | solution.py:146
  16.9 0.0 copy-done.3
  16.9 0.7 convolution_convert_fusion.2
  17.7 0.0 copy-start.4
  17.7 0.9 pad_maximum_fusion
  18.6 0.0 all-gather.2.cloned.1.call-update
  18.6 0.0 reduce-scatter.2.cloned.1.call-start
  18.7 0.0 copy-done.4
  18.7 0.2 reduce-window.8
  18.8 0.1 select_reduce_fusion.1
  18.9 0.8 copy.13.low_ref
  19.7 0.8 copy.14.high_ref
  20.5 0.7 fusion.13
  21.2 3.2 %pad_add_fusion.span_ref = s32[4]{0:T(128)} fusion(s32[1]{0:T(128)} %bitcast.6, s32[1]{0:T(128)} %bitcast.5, s32[1]{0:T(128)} %bitcast.4, s32[1]{0:T(128)} %bitcast.3), kind=kLoop, calls=%fused_computation.28 | loop fusion | flops 12 | bytes 32 | tf_op jit(solution)/shard_map/stack | solution.py:156
  24.4 3.1 %convolution_convert_fusion.3.query_ref = bf16[192,768]{1,0:T(8,128)(2,1)} fusion(bf16[1536,768]{1,0:T(8,128)(2,1)} %param.14, bf16[192,1536]{1,0:T(8,128)(2,1)S(1)} %all_gather.6, f32[1536]{0:T(1024)S(1)} %get-tuple-element.3, f32[1536]{0:T(1024)S(1)} %get-tuple-element.2, f32[192]{0:T(256)S(1)} %add_rsqrt_fusion, f32[192]{0:T(256)S(1)} %broadcast_multiply_fusion), kind=kOutput, calls=%fused_computation.8 | convolution fusion | flops 454901760 | bytes 3257856 | tf_op jit(solution)/shard_map/dot_general | solution.py:144
  27.5 168.2 %all-gather.2.cloned.1.call-done.key_ref.value_ref = bf16[12288,1536]{1,0:T(8,128)(2,1)} async-done(((bf16[192,1536]{1,0:T(8,128)(2,1)}), bf16[12288,1536]{1,0:T(8,128)(2,1)}) %all-gather.2.cloned.1.call-update) | async-done | bytes 37748752 | tf_op jit(solution)/shard_map/all_gather | solution.py:159
  195.7 31.3 %shard_map.104 = bf16[192,768]{1,0:T(8,128)(2,1)} custom-call(s32[4]{0:T(128)} %pad_add_fusion.span_ref, bf16[192,768]{1,0:T(8,128)(2,1)} %convolution_convert_fusion.3.query_ref, bf16[12288,1536]{1,0:T(8,128)(2,1)} %all-gather.2.cloned.1.call-done.key_ref.value_ref, bf16[12288,1536]{1,0:T(8,128)(2,1)} %all-gather.2.cloned.1.call-done.key_ref.value_ref, ...), custom_call_target="tpu_custom_call" | custom-call | tf_op jit(solution)/shard_map/pallas_call | solution.py:98
  227.0 0.0 copy-done
  227.0 2.4 convolution_convert_fusion
  229.5 0.0 reduce-scatter.2.cloned.1.call-update
  229.6 14.6 %reduce-scatter.2.cloned.1.call-done = bf16[192,768]{1,0:T(8,128)(2,1)} async-done(((bf16[192,1536]{1,0:T(8,128)(2,1)}), bf16[192,768]{1,0:T(8,128)(2,1)}) %reduce-scatter.2.cloned.1.call-update) | async-done | bytes 294928 | tf_op jit(solution)/shard_map/reduce_scatter | solution.py:162
  244.2 0.0 copy-done.1
  244.2 1.9 add_convert_fusion
  (11 shorter events, 0.2 us)
Async XLA Ops:
  7.2 219.9 %copy-start = (bf16[768,1536]{1,0:T(8,128)(2,1)S(1)}, bf16[768,1536]{1,0:T(8,128)(2,1)}, u32[]{:S(2)}) copy-start(bf16[768,1536]{1,0:T(8,128)(2,1)} %param.17) | copy-start | bytes 7077892
  7.2 188.5 %all-gather.2.cloned.1.call-start = ((), (), s32[]{:S(2)}) async-start(), calls=%async_computation.1 | async-start | bytes 38338560 | tf_op jit(solution)/shard_map/all_gather | solution.py:159
  10.9 2.9 %copy-start.2 = (f32[3,1536]{1,0:T(4,128)S(1)}, f32[3,1536]{1,0:T(4,128)}, u32[]{:S(2)}) copy-start(f32[3,1536]{1,0:T(4,128)} %param.13) | copy-start | bytes 55300
  14.4 2.6 %copy-start.3 = (bf16[1536,768]{1,0:T(8,128)(2,1)S(1)}, bf16[1536,768]{1,0:T(8,128)(2,1)}, u32[]{:S(2)}) copy-start(bf16[1536,768]{1,0:T(8,128)(2,1)} %param.15) | copy-start | bytes 7077892
  17.7 1.0 copy-start.4
  18.6 225.6 %reduce-scatter.2.cloned.1.call-start = ((), (), s32[]{:S(2)}) async-start(), calls=%async_computation.2 | async-start | bytes 884736 | tf_op jit(solution)/shard_map/reduce_scatter | solution.py:162
  227.0 17.1 %copy-start.1 = (bf16[192,768]{1,0:T(8,128)(2,1)S(1)}, bf16[192,768]{1,0:T(8,128)(2,1)}, u32[]{:S(2)}) copy-start(bf16[192,768]{1,0:T(8,128)(2,1)} %param.9) | copy-start | bytes 884740
Sparse Core Ops, SparseCore 0:
  18.7 176.9 all-gather.1
  229.6 14.4 reduce-scatter.1

commit v6 on v5

--- a/solution.py
+++ b/solution.py
@@ -81,17 +81,21 @@
 
 def attention(span, query, packed, query_low, query_high):
     rows, width = query.shape
-    blocks = packed.shape[0] // KEY_BLOCK
-
-    def key_map(block, span_ref):
+    half_blocks = packed.shape[0] // KEY_BLOCK
+    blocks = half_blocks * (packed.shape[1] // (2 * width))
+
+    def clamp(block, span_ref):
         first = span_ref[0] // KEY_BLOCK
         last = (span_ref[1] - 1) // KEY_BLOCK
-        return (jnp.minimum(jnp.maximum(block, first), last), 0)
+        return jnp.minimum(jnp.maximum(block, first), last)
+
+    def key_map(block, span_ref):
+        chosen = clamp(block, span_ref)
+        return (chosen % half_blocks, 2 * (chosen // half_blocks))
 
     def value_map(block, span_ref):
-        first = span_ref[0] // KEY_BLOCK
-        last = (span_ref[1] - 1) // KEY_BLOCK
-        return (jnp.minimum(jnp.maximum(block, first), last), 1)
+        chosen = clamp(block, span_ref)
+        return (chosen % half_blocks, 2 * (chosen // half_blocks) + 1)
 
     whole = lambda block, span_ref: (0, 0)
     heads = width // HEAD_DIM
@@ -144,20 +148,48 @@
     query = jnp.dot(normed, w_query, preferred_element_type=jnp.float32).astype(jnp.bfloat16)
     keys = jnp.dot(normed, w_key, preferred_element_type=jnp.float32).astype(jnp.bfloat16)
     values = jnp.dot(normed, w_value, preferred_element_type=jnp.float32).astype(jnp.bfloat16)
-    start_row = lax.axis_index("req") * tok_rows
-    query_index = start_row + jnp.arange(tok_rows, dtype=jnp.int32)
+    group_width = query.shape[1] // 2
+    pair = lax.axis_index("pair")
+    first_pair = pair == 0
+    groups = []
+    for group in range(2):
+        cols = slice(group * group_width, (group + 1) * group_width)
+        groups.append(jnp.concatenate([keys[:, cols], values[:, cols], query[:, cols]], axis=1))
+    own_group = jnp.where(first_pair, groups[0], groups[1])
+    sent_group = jnp.where(first_pair, groups[1], groups[0])
+    received = lax.ppermute(sent_group, "pair", perm=[(0, 1), (1, 0)])
+    halves = (jnp.where(first_pair, own_group, received), jnp.where(first_pair, received, own_group))
+    packed_here = jnp.concatenate([half[:, : 2 * group_width] for half in halves], axis=1)
+    packed = lax.all_gather(packed_here, "r", axis=0, tiled=True)
     video_ends = jnp.cumsum(video_lengths)
     video_starts = video_ends - video_lengths
-    inside = jnp.logical_and(
-        query_index[:, None] >= video_starts[None, :], query_index[:, None] < video_ends[None, :]
-    )
-    query_low = jnp.sum(jnp.where(inside, video_starts[None, :], 0), axis=1)
-    query_high = jnp.sum(jnp.where(inside, video_ends[None, :], 0), axis=1)
-    span = jnp.stack(
-        [jnp.min(query_low), jnp.max(query_high), jnp.max(query_low), jnp.min(query_high)]
-    ).astype(jnp.int32)
-    packed = lax.all_gather(jnp.concatenate([keys, values], axis=1), "req", axis=0, tiled=True)
-    attended = attention(span, query, packed, query_low[:, None], query_high[:, None])
+    half_tokens = packed.shape[0]
+    attended_halves = []
+    for half_index, half in enumerate(halves):
+        start_row = half_index * half_tokens + lax.axis_index("r") * tok_rows
+        query_index = start_row + jnp.arange(tok_rows, dtype=jnp.int32)
+        inside = jnp.logical_and(
+            query_index[:, None] >= video_starts[None, :],
+            query_index[:, None] < video_ends[None, :],
+        )
+        query_low = jnp.sum(jnp.where(inside, video_starts[None, :], 0), axis=1)
+        query_high = jnp.sum(jnp.where(inside, video_ends[None, :], 0), axis=1)
+        span = jnp.stack(
+            [jnp.min(query_low), jnp.max(query_high), jnp.max(query_low), jnp.min(query_high)]
+        ).astype(jnp.int32)
+        attended_halves.append(
+            attention(
+                span, half[:, 2 * group_width :], packed, query_low[:, None], query_high[:, None]
+            )
+        )
+    own_attended = jnp.where(first_pair, attended_halves[0], attended_halves[1])
+    sent_attended = jnp.where(first_pair, attended_halves[1], attended_halves[0])
+    other_attended = lax.ppermute(sent_attended, "pair", perm=[(0, 1), (1, 0)])
+    attended = jnp.where(
+        first_pair,
+        jnp.concatenate([own_attended, other_attended], axis=1),
+        jnp.concatenate([other_attended, own_attended], axis=1),
+    )
     partial_value = jnp.dot(attended, w_out, preferred_element_type=jnp.float32)
     own_sum = lax.psum_scatter(
         partial_value.astype(jnp.bfloat16), "tp", scatter_dimension=1, tiled=True
@@ -171,11 +203,16 @@
 
 
 def solution(mesh):
+    req_size, tp_size = mesh.devices.shape
+    split_mesh = jax.sharding.Mesh(
+        mesh.devices.reshape(2, req_size // 2, tp_size), ("pair", "r", "tp")
+    )
+    rows = ("pair", "r")
     return jax.shard_map(
         on_device,
-        mesh=mesh,
+        mesh=split_mesh,
         in_specs=(
-            P("req", "tp"),
+            P(rows, "tp"),
             P(),
             P(),
             P(),
@@ -185,6 +222,6 @@
             P(None, "tp"),
             P("tp", None),
         ),
-        out_specs=(P("req", "tp"), P("req", "tp")),
+        out_specs=(P(rows, "tp"), P(rows, "tp")),
         check_vma=False,
     )

time: 254 us -> 314 us (1.24)
  waiting for transfers between devices: 183 us -> 229 us
  other arithmetic: 10.5 us -> 16.9 us
  Pallas kernels: 31.3 us -> 37.1 us
  local copies, waits for them, and re-layouts: 1.59 us -> 5.96 us
  matrix products: 8.84 us -> 5.49 us
    all_gather x1, waiting for transfers between devices: 168 us -> 202 us  [on_device(): packed = lax.all_gather(packed_here, 'r', axis=0, tiled=True)]
    ppermute x0 -> x2, waiting for transfers between devices: none -> 18.1 us  [the longest x1 12.4 us: on_device(): received = lax.ppermute(sent_group, 'pair', perm=[(0, 1), (1, 0)])]
    reduce_scatter x1, waiting for transfers between devices: 14.6 us -> 8.45 us  [on_device(): lax.psum_scatter(partial_value.astype(jnp.bfloat16), 'tp', scatter_dimens...]
    pallas_call x1 -> x2, Pallas kernels: 31.3 us -> 37.1 us  [attention(): pl.pallas_call(attention_kernel, grid_spec=pltpu.PrefetchScalarGridSpec(n...]
    another operation x1 -> x2, other arithmetic: 3.2 us -> 6.44 us  [on_device(): jnp.stack([jnp.min(query_low), jnp.max(query_high), jnp.max(query_low), j...]
  transfers between devices with their start and end apart: 2 -> 4, of which waited for: 2 -> 4; matrix products, arithmetic and copies ran while one was open for 4% -> 4% of each run, Pallas kernels for 0% -> 0%
where the time goes in v6:
time: 314 us; the launch traced here: 313 us
  waiting for transfers between devices  229 us (73%)
  Pallas kernels  37.1 us (12%)
  other arithmetic  16.9 us (5%)
  between operations  15 us (5%)
  local copies, waits for them, and re-layouts  5.96 us (2%)
  matrix products  5.49 us (2%)
    all_gather x1, waiting for transfers between devices, on_device(): packed = lax.all_gather(packed_here, 'r', axis=0, tiled=True)  202 us
    pallas_call x2, Pallas kernels, attention(): pl.pallas_call(attention_kernel, grid_spec=pltpu.PrefetchScalarGridSpec(n...  37.1 us
    ppermute x1, waiting for transfers between devices, on_device(): received = lax.ppermute(sent_group, 'pair', perm=[(0, 1), (1, 0)])  12.4 us
    reduce_scatter x1, waiting for transfers between devices, on_device(): lax.psum_scatter(partial_value.astype(jnp.bfloat16), 'tp', scatter_dimens...  8.45 us
    another operation x2, other arithmetic, on_device(): jnp.stack([jnp.min(query_low), jnp.max(query_high), jnp.max(query_low), j...  6.44 us
  transfers between devices with their start and end apart: 4, of which 4 were waited for; matrix products, arithmetic and copies ran while one was open for 4% of the time, Pallas kernels for 0%

profile of v6, /device:TPU:17, one launch (start us, length us, event | category | flops | bytes accessed | tf_op | source)
XLA Modules:
  0.0 313.1 jit_solution(10911906528085941679)
XLA Ops:
  7.2 2.9 all_gather.6
  10.9 2.9 multiply_reduce_fusion
  13.9 0.2 convert_reduce_fusion
  14.1 0.3 fusion.2
  14.4 2.5 convolution_convert_fusion.1
  17.0 0.7 convolution_convert_fusion.2
  17.8 0.9 copy-done.9
  18.7 0.7 convolution_convert_fusion.3
  19.7 0.4 copy-done.3
  20.2 12.4 %collective-permute-done = bf16[192,1152]{1,0:T(8,128)(2,1)S(1)} collective-permute-done((bf16[192,1152]{1,0:T(8,128)(2,1)S(1)}, bf16[192,1152]{1,0:T(8,128)(2,1)S(1)}, u32[]{:S(2)}, u32[]{:S(2)}) %collective-permute-start) | collective-permute-done | bytes 442400 | tf_op jit(solution)/shard_map/ppermute | solution.py:160
  32.6 1.3 broadcast_select_fusion.1
  34.0 0.9 pad_maximum_fusion
  34.9 0.2 reduce-window.8
  35.2 0.8 copy.15.low_ref
  36.0 0.8 copy.16.high_ref
  36.8 0.8 copy.17.low_ref
  37.5 0.8 copy.18.high_ref
  38.3 0.7 fusion.20
  39.0 3.2 %pad_add_fusion.span_ref = s32[4]{0:T(128)} fusion(s32[1]{0:T(128)} %bitcast.6, s32[1]{0:T(128)} %bitcast.5, s32[1]{0:T(128)} %bitcast.4, s32[1]{0:T(128)} %bitcast.3), kind=kLoop, calls=%fused_computation.47 | loop fusion | flops 12 | bytes 32 | tf_op jit(solution)/shard_map/stack | solution.py:177
  42.3 0.7 fusion.22
  43.0 3.2 %pad_add_fusion.1.span_ref = s32[4]{0:T(128)} fusion(s32[1]{0:T(128)} %bitcast.12, s32[1]{0:T(128)} %bitcast.11, s32[1]{0:T(128)} %bitcast.10, s32[1]{0:T(128)} %bitcast.9), kind=kLoop, calls=%fused_computation.48 | loop fusion | flops 12 | bytes 32 | tf_op jit(solution)/shard_map/stack | solution.py:177
  46.2 0.7 slice.61.query_ref
  46.9 0.7 slice.64.query_ref
  47.6 202.4 %all-gather.2.cloned.1.call-done.key_ref.value_ref = bf16[6144,1536]{1,0:T(8,128)(2,1)} async-done(((bf16[192,1536]{1,0:T(8,128)(2,1)}), bf16[6144,1536]{1,0:T(8,128)(2,1)}) %all-gather.2.cloned.1.call-update) | async-done | bytes 18874384 | tf_op jit(solution)/shard_map/all_gather | solution.py:163
  250.0 18.5 %shard_map.104 = bf16[192,384]{1,0:T(8,128)(2,1)} custom-call(s32[4]{0:T(128)} %pad_add_fusion.span_ref, bf16[192,384]{1,0:T(8,128)(2,1)} %slice.61.query_ref, bf16[6144,1536]{1,0:T(8,128)(2,1)} %all-gather.2.cloned.1.call-done.key_ref.value_ref, bf16[6144,1536]{1,0:T(8,128)(2,1)} %all-gather.2.cloned.1.call-done.key_ref.value_ref, s32[192,1]{1,0:T(8,128)} %copy.15.low_ref, ...), custom_call_target="tpu_custom_call" | custom-call | tf_op jit(solution)/shard_map/pallas_call | solution.py:102
  268.5 18.6 %shard_map.105 = bf16[192,384]{1,0:T(8,128)(2,1)} custom-call(s32[4]{0:T(128)} %pad_add_fusion.1.span_ref, bf16[192,384]{1,0:T(8,128)(2,1)} %slice.64.query_ref, bf16[6144,1536]{1,0:T(8,128)(2,1)} %all-gather.2.cloned.1.call-done.key_ref.value_ref, bf16[6144,1536]{1,0:T(8,128)(2,1)} %all-gather.2.cloned.1.call-done.key_ref.value_ref, ...), custom_call_target="tpu_custom_call" | custom-call | tf_op jit(solution)/shard_map/pallas_call | solution.py:102
  287.1 0.9 broadcast_select_fusion.5
  288.1 0.6 collective-permute-start.1
  288.7 5.7 %collective-permute-done.1 = bf16[192,384]{1,0:T(8,128)(2,1)S(1)} collective-permute-done((bf16[192,384]{1,0:T(8,128)(2,1)S(1)}, bf16[192,384]{1,0:T(8,128)(2,1)S(1)}, u32[]{:S(2)}, u32[]{:S(2)}) %collective-permute-start.1) | collective-permute-done | bytes 147488 | tf_op jit(solution)/shard_map/ppermute | solution.py:187
  294.4 1.5 convolution_convert_fusion
  295.9 8.5 %reduce-scatter.2.cloned.1.call-done = bf16[192,768]{1,0:T(8,128)(2,1)} async-done(((bf16[192,1536]{1,0:T(8,128)(2,1)}), bf16[192,768]{1,0:T(8,128)(2,1)}) %reduce-scatter.2.cloned.1.call-update) | async-done | bytes 294928 | tf_op jit(solution)/shard_map/reduce_scatter | solution.py:194
  304.4 1.9 add_convert_fusion
  (43 shorter events, 0.8 us)
Async XLA Ops:
  7.2 287.2 %copy-start = (bf16[768,1536]{1,0:T(8,128)(2,1)S(1)}, bf16[768,1536]{1,0:T(8,128)(2,1)}, u32[]{:S(2)}) copy-start(bf16[768,1536]{1,0:T(8,128)(2,1)} %param.17) | copy-start | bytes 7077892
  7.2 242.8 %all-gather.2.cloned.1.call-start = ((), (), s32[]{:S(2)}) async-start(), calls=%async_computation.1 | async-start | bytes 19464192 | tf_op jit(solution)/shard_map/all_gather | solution.py:163
  10.9 2.9 copy-start.7
  14.4 2.6 copy-start.8
  17.0 1.7 copy-start.9
  18.6 0.8 copy-start.1
  18.7 0.8 copy-start.2
  19.4 0.7 copy-start.3
  19.5 0.7 copy-start.4
  19.6 13.0 %collective-permute-start = (bf16[192,1152]{1,0:T(8,128)(2,1)S(1)}, bf16[192,1152]{1,0:T(8,128)(2,1)S(1)}, u32[]{:S(2)}, u32[]{:S(2)}) collective-permute-start(bf16[192,1152]{1,0:T(8,128)(2,1)S(1)} %broadcast_select_fusion.2), channel_id=1, source_target_pairs={{0,64},{64,0},{1,65},{65,1},{2,66},{66,2},{3,67},{67,3},{4,68},{68... | collective-permute-start | bytes 1327112 | tf_op jit(solution)/shard_map/ppermute | solution.py:160
  34.0 1.0 copy-start.10
  34.9 269.5 %reduce-scatter.2.cloned.1.call-start = ((), (), s32[]{:S(2)}) async-start(), calls=%async_computation.2 | async-start | bytes 884736 | tf_op jit(solution)/shard_map/reduce_scatter | solution.py:194
  268.5 18.6 %copy-start.6 = (bf16[192,384]{1,0:T(8,128)(2,1)S(1)}, bf16[192,384]{1,0:T(8,128)(2,1)}, u32[]{:S(2)}) copy-start(bf16[192,384]{1,0:T(8,128)(2,1)} %shard_map.104) | copy-start | bytes 442372
  288.1 6.3 %collective-permute-start.1 = (bf16[192,384]{1,0:T(8,128)(2,1)S(1)}, bf16[192,384]{1,0:T(8,128)(2,1)S(1)}, u32[]{:S(2)}, u32[]{:S(2)}) collective-permute-start(bf16[192,384]{1,0:T(8,128)(2,1)S(1)} %get-tuple-element.23), channel_id=1, source_target_pairs={{0,64},{64,0},{1,65},{65,1},{2,66},{66,2},{3,67},{67,3},{4,68},{68... | collective-permute-start | bytes 442376 | tf_op jit(solution)/shard_map/ppermute | solution.py:187
  294.4 10.0 %copy-start.5 = (bf16[192,768]{1,0:T(8,128)(2,1)S(1)}, bf16[192,768]{1,0:T(8,128)(2,1)}, u32[]{:S(2)}) copy-start(bf16[192,768]{1,0:T(8,128)(2,1)} %param.9) | copy-start | bytes 884740
Sparse Core Ops, SparseCore 0:
  35.0 214.9 all-gather.1
  296.0 8.3 reduce-scatter.1

commit v7 on v5

--- a/solution.py
+++ b/solution.py
@@ -9,7 +9,7 @@
 
 HEAD_DIM = 128
 STEPS = 1000
-KEY_BLOCK = 1024
+KEY_BLOCK = 2048
 EXP2_SCALE = math.log2(math.e) / math.sqrt(HEAD_DIM)
 
 

time: 254 us -> 256 us (level)
  waiting for transfers between devices: 183 us -> 186 us
    reduce_scatter x1, waiting for transfers between devices: 14.6 us -> 17.5 us  [on_device(): lax.psum_scatter(partial_value.astype(jnp.bfloat16), 'tp', scatter_dimens...]
  transfers between devices with their start and end apart: 2 -> 2, of which waited for: 2 -> 2; matrix products, arithmetic and copies ran while one was open for 4% -> 3% of each run, Pallas kernels for 0% -> 0%
where the time goes in v7:
time: 256 us; the launch traced here: 254 us
  waiting for transfers between devices  186 us (73%)
  Pallas kernels  29.9 us (12%)
  between operations  14.9 us (6%)
  other arithmetic  10.5 us (4%)
  matrix products  8.84 us (3%)
  blocking collectives  2.87 us (1%)
    all_gather x1, waiting for transfers between devices, on_device(): lax.all_gather(jnp.concatenate([keys, values], axis=1), 'req', axis=0, ti...  168 us
    pallas_call x1, Pallas kernels, attention(): pl.pallas_call(attention_kernel, grid_spec=pltpu.PrefetchScalarGridSpec(n...  29.9 us
    reduce_scatter x1, waiting for transfers between devices, on_device(): lax.psum_scatter(partial_value.astype(jnp.bfloat16), 'tp', scatter_dimens...  17.5 us
  transfers between devices with their start and end apart: 2, of which 2 were waited for; matrix products, arithmetic and copies ran while one was open for 3% of the time, Pallas kernels for 0%

profile of v7, /device:TPU:17, one launch (start us, length us, event | category | flops | bytes accessed | tf_op | source)
XLA Modules:
  0.0 254.4 jit_solution(13263787905037010058)
XLA Ops:
  7.2 0.0 copy-start
  7.2 0.0 all-gather.2.cloned.1.call-start
  7.2 2.9 %all_gather.6 = bf16[192,1536]{1,0:T(8,128)(2,1)S(1)} all-gather(bf16[192,768]{1,0:T(8,128)(2,1)} %param.9), channel_id=1, replica_groups=mesh['req'=64,'tp'=2] {'tp'}, dimensions={1}, use_global_device_ids=true | all-gather | bytes 884736 | tf_op jit(solution)/shard_map/all_gather | solution.py:126
  10.9 0.0 copy-start.2
  10.9 2.9 %multiply_reduce_fusion = f32[4608]{0:T(1024)S(1)} fusion(f32[256,4608]{1,0:T(8,128)} %param.12, f32[256]{0:T(256)S(1)} %divide_multiply_fusion), kind=kLoop, calls=%fused_computation | loop fusion | flops 2354688 | bytes 4738048 | tf_op jit(solution)/shard_map/reduce_sum | solution.py:134
  13.8 0.0 copy-done.2
  13.9 0.2 convert_reduce_fusion
  14.1 0.3 fusion.2
  14.4 0.0 copy-start.3
  14.4 2.5 %convolution_convert_fusion.1 = bf16[192,768]{1,0:T(8,128)(2,1)S(1)} fusion(bf16[1536,768]{1,0:T(8,128)(2,1)} %param.16, bf16[192,1536]{1,0:T(8,128)(2,1)S(1)} %all_gather.6, f32[1536]{0:T(1024)S(1)} %get-tuple-element.3, f32[1536]{0:T(1024)S(1)} %get-tuple-element.2, f32[192]{0:T(256)S(1)} %add_rsqrt_fusion, f32[192]{0:T(256)S(1)} %broadcast_multiply_fusion), kind=kOutput, calls=%fused_computation.6 | convolution fusion | flops 454901760 | bytes 3257856 | tf_op jit(solution)/shard_map/dot_general | solution.py:146
  16.9 0.0 copy-done.3
  16.9 0.7 convolution_convert_fusion.2
  17.7 0.0 copy-start.4
  17.7 0.9 pad_maximum_fusion
  18.6 0.0 all-gather.2.cloned.1.call-update
  18.6 0.2 reduce-scatter.2.cloned.1.call-start
  18.8 0.0 copy-done.4
  18.8 0.2 reduce-window.8
  19.0 0.1 select_reduce_fusion.1
  19.1 0.8 copy.13.low_ref
  19.9 0.8 copy.14.high_ref
  20.6 0.7 fusion.13
  21.4 3.2 %pad_add_fusion.span_ref = s32[4]{0:T(128)} fusion(s32[1]{0:T(128)} %bitcast.6, s32[1]{0:T(128)} %bitcast.5, s32[1]{0:T(128)} %bitcast.4, s32[1]{0:T(128)} %bitcast.3), kind=kLoop, calls=%fused_computation.28 | loop fusion | flops 12 | bytes 32 | tf_op jit(solution)/shard_map/stack | solution.py:156
  24.6 3.1 %convolution_convert_fusion.3.query_ref = bf16[192,768]{1,0:T(8,128)(2,1)} fusion(bf16[1536,768]{1,0:T(8,128)(2,1)} %param.14, bf16[192,1536]{1,0:T(8,128)(2,1)S(1)} %all_gather.6, f32[1536]{0:T(1024)S(1)} %get-tuple-element.3, f32[1536]{0:T(1024)S(1)} %get-tuple-element.2, f32[192]{0:T(256)S(1)} %add_rsqrt_fusion, f32[192]{0:T(256)S(1)} %broadcast_multiply_fusion), kind=kOutput, calls=%fused_computation.8 | convolution fusion | flops 454901760 | bytes 3257856 | tf_op jit(solution)/shard_map/dot_general | solution.py:144
  27.7 168.0 %all-gather.2.cloned.1.call-done.key_ref.value_ref = bf16[12288,1536]{1,0:T(8,128)(2,1)} async-done(((bf16[192,1536]{1,0:T(8,128)(2,1)}), bf16[12288,1536]{1,0:T(8,128)(2,1)}) %all-gather.2.cloned.1.call-update) | async-done | bytes 37748752 | tf_op jit(solution)/shard_map/all_gather | solution.py:159
  195.7 29.9 %shard_map.104 = bf16[192,768]{1,0:T(8,128)(2,1)} custom-call(s32[4]{0:T(128)} %pad_add_fusion.span_ref, bf16[192,768]{1,0:T(8,128)(2,1)} %convolution_convert_fusion.3.query_ref, bf16[12288,1536]{1,0:T(8,128)(2,1)} %all-gather.2.cloned.1.call-done.key_ref.value_ref, bf16[12288,1536]{1,0:T(8,128)(2,1)} %all-gather.2.cloned.1.call-done.key_ref.value_ref, ...), custom_call_target="tpu_custom_call" | custom-call | tf_op jit(solution)/shard_map/pallas_call | solution.py:98
  225.6 0.0 copy-done
  225.6 2.4 convolution_convert_fusion
  228.1 0.0 reduce-scatter.2.cloned.1.call-update
  228.2 17.5 %reduce-scatter.2.cloned.1.call-done = bf16[192,768]{1,0:T(8,128)(2,1)} async-done(((bf16[192,1536]{1,0:T(8,128)(2,1)}), bf16[192,768]{1,0:T(8,128)(2,1)}) %reduce-scatter.2.cloned.1.call-update) | async-done | bytes 294928 | tf_op jit(solution)/shard_map/reduce_scatter | solution.py:162
  245.7 0.0 copy-done.1
  245.7 1.9 add_convert_fusion
  (11 shorter events, 0.2 us)
Async XLA Ops:
  7.2 218.5 %copy-start = (bf16[768,1536]{1,0:T(8,128)(2,1)S(1)}, bf16[768,1536]{1,0:T(8,128)(2,1)}, u32[]{:S(2)}) copy-start(bf16[768,1536]{1,0:T(8,128)(2,1)} %param.17) | copy-start | bytes 7077892
  7.2 188.5 %all-gather.2.cloned.1.call-start = ((), (), s32[]{:S(2)}) async-start(), calls=%async_computation.1 | async-start | bytes 38338560 | tf_op jit(solution)/shard_map/all_gather | solution.py:159
  10.9 2.9 %copy-start.2 = (f32[3,1536]{1,0:T(4,128)S(1)}, f32[3,1536]{1,0:T(4,128)}, u32[]{:S(2)}) copy-start(f32[3,1536]{1,0:T(4,128)} %param.13) | copy-start | bytes 55300
  14.4 2.6 %copy-start.3 = (bf16[1536,768]{1,0:T(8,128)(2,1)S(1)}, bf16[1536,768]{1,0:T(8,128)(2,1)}, u32[]{:S(2)}) copy-start(bf16[1536,768]{1,0:T(8,128)(2,1)} %param.15) | copy-start | bytes 7077892
  17.7 1.1 copy-start.4
  18.6 227.1 %reduce-scatter.2.cloned.1.call-start = ((), (), s32[]{:S(2)}) async-start(), calls=%async_computation.2 | async-start | bytes 884736 | tf_op jit(solution)/shard_map/reduce_scatter | solution.py:162
  225.6 20.0 %copy-start.1 = (bf16[192,768]{1,0:T(8,128)(2,1)S(1)}, bf16[192,768]{1,0:T(8,128)(2,1)}, u32[]{:S(2)}) copy-start(bf16[192,768]{1,0:T(8,128)(2,1)} %param.9) | copy-start | bytes 884740
Sparse Core Ops, SparseCore 0:
  18.7 176.9 all-gather.1
  228.2 17.4 reduce-scatter.1

commit v8 on v7

--- a/solution.py
+++ b/solution.py
@@ -158,13 +158,18 @@
     ).astype(jnp.int32)
     packed = lax.all_gather(jnp.concatenate([keys, values], axis=1), "req", axis=0, tiled=True)
     attended = attention(span, query, packed, query_low[:, None], query_high[:, None])
-    partial_value = jnp.dot(attended, w_out, preferred_element_type=jnp.float32)
-    own_sum = lax.psum_scatter(
-        partial_value.astype(jnp.bfloat16), "tp", scatter_dimension=1, tiled=True
-    ).astype(jnp.float32)
-    share = own_sum.shape[1]
-    gate_share = lax.dynamic_slice_in_dim(gate, lax.axis_index("tp") * share, share)
-    branch = gate_share[None, :] * own_sum
+    share = w_out.shape[1] // 2
+    core = lax.axis_index("tp")
+    swap = [(0, 1), (1, 0)]
+    own_columns = lax.dynamic_slice_in_dim(w_out, core * share, share, axis=1)
+    other_columns = lax.dynamic_slice_in_dim(w_out, (1 - core) * share, share, axis=1)
+    partner_rows = lax.ppermute(other_columns, "tp", perm=swap)
+    partner_attended = lax.ppermute(attended, "tp", perm=swap)
+    projected = jnp.dot(attended, own_columns, preferred_element_type=jnp.float32) + jnp.dot(
+        partner_attended, partner_rows, preferred_element_type=jnp.float32
+    )
+    gate_share = lax.dynamic_slice_in_dim(gate, core * share, share)
+    branch = gate_share[None, :] * projected
     velocity = branch.astype(jnp.bfloat16)
     stepped = (tokens.astype(jnp.float32) + delta_sigma * branch).astype(jnp.bfloat16)
     return (velocity, stepped)

time: 256 us -> 244 us (0.953)
  the two profiles are of different devices: /device:TPU:17 before, /device:TPU:101 now
where the time goes in v8:
time: 244 us; the launch traced here: 243 us
  waiting for transfers between devices  166 us (68%)
  Pallas kernels  37.1 us (15%)
  between operations  15.1 us (6%)
  matrix products  10.3 us (4%)
  other arithmetic  8.66 us (4%)
  blocking collectives  2.74 us (1%)
  local copies, waits for them, and re-layouts  2.71 us (1%)
    all_gather x1, waiting for transfers between devices, on_device(): lax.all_gather(jnp.concatenate([keys, values], axis=1), 'req', axis=0, ti...  166 us
    pallas_call x1, Pallas kernels, attention(): pl.pallas_call(attention_kernel, grid_spec=pltpu.PrefetchScalarGridSpec(n...  37.1 us
  transfers between devices with their start and end apart: 3, of which 1 were waited for; matrix products, arithmetic and copies ran while one was open for 5% of the time, Pallas kernels for 15%

profile of v8, /device:TPU:101, one launch (start us, length us, event | category | flops | bytes accessed | tf_op | source)
XLA Modules:
  0.0 243.2 jit_solution(12953549157358744803)
XLA Ops:
  7.2 0.0 copy-start
  7.2 0.0 all-gather.2.cloned.1.call-start
  8.0 2.7 %all_gather.6 = bf16[192,1536]{1,0:T(8,128)(2,1)S(1)} all-gather(bf16[192,768]{1,0:T(8,128)(2,1)} %param.9), channel_id=1, replica_groups=mesh['req'=64,'tp'=2] {'tp'}, dimensions={1}, use_global_device_ids=true | all-gather | bytes 884736 | tf_op jit(solution)/shard_map/all_gather | solution.py:126
  10.9 0.0 copy-start.2
  10.9 2.9 %multiply_reduce_fusion = f32[4608]{0:T(1024)S(1)} fusion(f32[256,4608]{1,0:T(8,128)} %param.12, f32[256]{0:T(256)S(1)} %divide_multiply_fusion), kind=kLoop, calls=%fused_computation | loop fusion | flops 2354688 | bytes 4738048 | tf_op jit(solution)/shard_map/reduce_sum | solution.py:134
  13.8 0.0 copy-done.2
  13.9 0.2 convert_reduce_fusion
  14.1 0.3 fusion.3
  14.4 0.0 copy-start.3
  14.4 2.5 %convolution_convert_fusion = bf16[192,768]{1,0:T(8,128)(2,1)S(1)} fusion(bf16[1536,768]{1,0:T(8,128)(2,1)} %param.16, bf16[192,1536]{1,0:T(8,128)(2,1)S(1)} %all_gather.6, f32[1536]{0:T(1024)S(1)} %get-tuple-element.3, f32[1536]{0:T(1024)S(1)} %get-tuple-element.2, f32[192]{0:T(256)S(1)} %add_rsqrt_fusion, f32[192]{0:T(256)S(1)} %broadcast_multiply_fusion), kind=kOutput, calls=%fused_computation.7 | convolution fusion | flops 454901760 | bytes 3257856 | tf_op jit(solution)/shard_map/dot_general | solution.py:146
  17.0 0.0 copy-done.3
  17.0 0.7 convolution_convert_fusion.1
  17.7 0.9 pad_maximum_fusion
  18.6 0.0 all-gather.2.cloned.1.call-update
  18.7 0.0 copy-done
  18.7 0.0 copy-start.4
  18.7 1.1 constant_dynamic-slice_fusion
  19.8 0.4 collective-permute-start.1
  20.2 0.2 reduce-window.8
  20.3 0.1 select_reduce_fusion.1
  20.4 0.8 copy.13.low_ref
  21.2 0.8 copy.14.high_ref
  22.0 0.8 fusion.16
  22.7 3.2 %pad_add_fusion.span_ref = s32[4]{0:T(128)} fusion(s32[1]{0:T(128)} %bitcast.6, s32[1]{0:T(128)} %bitcast.5, s32[1]{0:T(128)} %bitcast.4, s32[1]{0:T(128)} %bitcast.3), kind=kLoop, calls=%fused_computation.31 | loop fusion | flops 12 | bytes 32 | tf_op jit(solution)/shard_map/stack | solution.py:156
  26.0 3.1 %convolution_convert_fusion.2.query_ref = bf16[192,768]{1,0:T(8,128)(2,1)} fusion(bf16[1536,768]{1,0:T(8,128)(2,1)} %param.14, bf16[192,1536]{1,0:T(8,128)(2,1)S(1)} %all_gather.6, f32[1536]{0:T(1024)S(1)} %get-tuple-element.3, f32[1536]{0:T(1024)S(1)} %get-tuple-element.2, f32[192]{0:T(256)S(1)} %add_rsqrt_fusion, f32[192]{0:T(256)S(1)} %broadcast_multiply_fusion), kind=kOutput, calls=%fused_computation.9 | convolution fusion | flops 454901760 | bytes 3257856 | tf_op jit(solution)/shard_map/dot_general | solution.py:144
  29.1 165.6 %all-gather.2.cloned.1.call-done.key_ref.value_ref = bf16[12288,1536]{1,0:T(8,128)(2,1)} async-done(((bf16[192,1536]{1,0:T(8,128)(2,1)}), bf16[12288,1536]{1,0:T(8,128)(2,1)}) %all-gather.2.cloned.1.call-update) | async-done | bytes 37748752 | tf_op jit(solution)/shard_map/all_gather | solution.py:159
  194.6 37.1 %shard_map.104 = bf16[192,768]{1,0:T(8,128)(2,1)} custom-call(s32[4]{0:T(128)} %pad_add_fusion.span_ref, bf16[192,768]{1,0:T(8,128)(2,1)} %convolution_convert_fusion.2.query_ref, bf16[12288,1536]{1,0:T(8,128)(2,1)} %all-gather.2.cloned.1.call-done.key_ref.value_ref, bf16[12288,1536]{1,0:T(8,128)(2,1)} %all-gather.2.cloned.1.call-done.key_ref.value_ref, ...), custom_call_target="tpu_custom_call" | custom-call | tf_op jit(solution)/shard_map/pallas_call | solution.py:98
  231.7 0.7 collective-permute-start
  232.4 1.4 fusion.7
  233.8 0.0 collective-permute-done.1
  233.8 0.0 collective-permute-done
  233.8 2.5 %add_convert_fusion = (bf16[192,768]{1,0:T(8,128)(2,1)}, bf16[192,768]{1,0:T(8,128)(2,1)}) fusion(bf16[192,768]{1,0:T(8,128)(2,1)S(1)} %copy-done.1, f32[]{:T(128)} %bitcast.9, f32[192,768]{1,0:T(8,128)S(1)} %fusion.7, bf16[192,768]{1,0:T(8,128)(2,1)S(1)} %collective-permute-done, bf16[768,768]{1,0:T(8,128)(2,1)} %collective-permute-done.1, ...), kind=kOutput, calls=%fused_computation.17 | convolution fusion | flops 227524608 | bytes 2952196 | tf_op jit(solution)/shard_map/dot_general | solution.py:168
  (13 shorter events, 0.2 us)
Async XLA Ops:
  7.2 11.5 %copy-start = (bf16[768,1536]{1,0:T(8,128)(2,1)S(1)}, bf16[768,1536]{1,0:T(8,128)(2,1)}, u32[]{:S(2)}) copy-start(bf16[768,1536]{1,0:T(8,128)(2,1)} %param.17) | copy-start | bytes 7077892
  7.2 187.4 %all-gather.2.cloned.1.call-start = ((), (), s32[]{:S(2)}) async-start(), calls=%async_computation | async-start | bytes 38338560 | tf_op jit(solution)/shard_map/all_gather | solution.py:159
  10.9 2.9 %copy-start.2 = (f32[3,1536]{1,0:T(4,128)S(1)}, f32[3,1536]{1,0:T(4,128)}, u32[]{:S(2)}) copy-start(f32[3,1536]{1,0:T(4,128)} %param.13) | copy-start | bytes 55300
  14.4 2.6 %copy-start.3 = (bf16[1536,768]{1,0:T(8,128)(2,1)S(1)}, bf16[1536,768]{1,0:T(8,128)(2,1)}, u32[]{:S(2)}) copy-start(bf16[1536,768]{1,0:T(8,128)(2,1)} %param.15) | copy-start | bytes 7077892
  18.7 1.5 copy-start.4
  19.8 214.0 %collective-permute-start.1 = (bf16[768,768]{1,0:T(8,128)(2,1)}, bf16[768,768]{1,0:T(8,128)(2,1)}, u32[]{:S(2)}, u32[]{:S(2)}) collective-permute-start(bf16[768,768]{1,0:T(8,128)(2,1)} %constant_dynamic-slice_fusion), channel_id=1, source_target_pairs={{0,1},{1,0},{2,3},{3,2},{4,5},{5,4},{6,7},{7,6},{8,9},{9,8},{10,11... | collective-permute-start | bytes 3538952 | tf_op jit(solution)/shard_map/ppermute | solution.py:166
  231.7 2.2 copy-start.1
  231.7 2.1 collective-permute-start
Sparse Core Ops, SparseCore 0:
  18.8 175.8 all-gather.1

commit v9 on v8

--- a/solution.py
+++ b/solution.py
@@ -123,7 +123,13 @@
 ):
     tok_rows = tokens.shape[0]
     width = time_weight.shape[1] // 3
-    full_rows = lax.all_gather(tokens, "tp", axis=1, tiled=True)
+    first_core = lax.axis_index("tp") == 0
+    other_half = lax.ppermute(tokens, "tp", perm=[(0, 1), (1, 0)])
+    full_rows = jnp.where(
+        first_core,
+        jnp.concatenate([tokens, other_half], axis=1),
+        jnp.concatenate([other_half, tokens], axis=1),
+    )
     time_value = timestep[0].astype(jnp.float32)
     sigma = noise_level(time_value)
     delta_sigma = noise_level(time_value - 1.0) - sigma
@@ -131,11 +137,11 @@
     frequency = jnp.exp(-math.log(10000.0) * jnp.arange(half_freq, dtype=jnp.float32) / half_freq)
     angle = 1000.0 * sigma * frequency
     embedding = jnp.concatenate([jnp.cos(angle), jnp.sin(angle)])
-    modulation = jnp.sum(
-        jax.nn.silu(embedding)[:, None] * time_weight, axis=0
-    )
-    modulation = modulation.reshape(3, width) + block_mod
-    shift, scale, gate = (modulation[0], modulation[1], modulation[2])
+    activated = jax.nn.silu(embedding)[:, None]
+    shift_scale = jnp.sum(activated * time_weight[:, : 2 * width], axis=0).reshape(2, width)
+    shift = shift_scale[0] + block_mod[0]
+    scale = shift_scale[1] + block_mod[1]
+    gate = jnp.sum(activated * time_weight[:, 2 * width :], axis=0) + block_mod[2]
     as_float = full_rows.astype(jnp.float32)
     mean = jnp.mean(as_float, axis=1, keepdims=True)
     centred = as_float - mean

time: 244 us -> 236 us (0.967)
  the two profiles are of different devices: /device:TPU:101 before, /device:TPU:17 now
where the time goes in v9:
time: 236 us; the launch traced here: 234 us
  waiting for transfers between devices  165 us (70%)
  Pallas kernels  30 us (13%)
  between operations  15 us (6%)
  matrix products  10.4 us (4%)
  other arithmetic  9.78 us (4%)
  local copies, waits for them, and re-layouts  2.69 us (1%)
    all_gather x1, waiting for transfers between devices, on_device(): lax.all_gather(jnp.concatenate([keys, values], axis=1), 'req', axis=0, ti...  165 us
    pallas_call x1, Pallas kernels, attention(): pl.pallas_call(attention_kernel, grid_spec=pltpu.PrefetchScalarGridSpec(n...  30 us
  transfers between devices with their start and end apart: 4, of which 1 were waited for; matrix products, arithmetic and copies ran while one was open for 7% of the time, Pallas kernels for 13%

profile of v9, /device:TPU:17, one launch (start us, length us, event | category | flops | bytes accessed | tf_op | source)
XLA Modules:
  0.0 234.5 jit_solution(9772579217440224885)
XLA Ops:
  7.2 0.0 copy-start
  7.2 0.0 all-gather.2.cloned.1.call-start
  7.2 0.8 collective-permute-start
  8.8 0.0 copy-start.2
  8.8 0.0 copy-start.1
  8.8 2.3 multiply_reduce_fusion
  11.1 0.1 slice_reduce_fusion
  11.2 0.0 collective-permute-done
  11.2 0.2 convert_reduce_fusion
  11.4 0.3 fusion.3
  11.7 0.0 copy-start.3
  11.8 2.6 %convolution_convert_fusion = bf16[192,768]{1,0:T(8,128)(2,1)S(1)} fusion(bf16[1536,768]{1,0:T(8,128)(2,1)} %param.16, f32[1536]{0:T(1024)S(1)} %get-tuple-element.3, f32[1536]{0:T(1024)S(1)} %get-tuple-element.4, f32[192]{0:T(256)S(1)} %add_rsqrt_fusion, f32[192]{0:T(256)S(1)} %broadcast_multiply_fusion, bf16[192,768]{1,0:T(8,128)(2,1)S(1)} %copy-done.1, ...), kind=kOutput, calls=%fused_computation.8 | convolution fusion | flops 457555968 | bytes 3257857 | tf_op jit(solution)/shard_map/dot_general | solution.py:152
  14.3 0.8 convolution_convert_fusion.1
  15.1 0.9 pad_maximum_fusion
  16.0 0.0 all-gather.2.cloned.1.call-update
  16.1 0.0 copy-start.4
  16.1 1.1 constant_dynamic-slice_fusion
  17.2 0.1 collective-permute-start.2
  17.3 0.2 reduce-window.8
  17.5 0.1 select_reduce_fusion.1
  17.6 0.8 copy.13.low_ref
  18.4 0.8 copy.14.high_ref
  19.2 0.8 fusion.15
  19.9 3.2 %pad_add_fusion.span_ref = s32[4]{0:T(128)} fusion(s32[1]{0:T(128)} %bitcast.6, s32[1]{0:T(128)} %bitcast.5, s32[1]{0:T(128)} %bitcast.4, s32[1]{0:T(128)} %bitcast.3), kind=kLoop, calls=%fused_computation.31 | loop fusion | flops 12 | bytes 32 | tf_op jit(solution)/shard_map/stack | solution.py:162
  23.1 1.6 multiply_reduce_fusion.1
  24.7 3.1 %convolution_convert_fusion.2.query_ref = bf16[192,768]{1,0:T(8,128)(2,1)} fusion(bf16[1536,768]{1,0:T(8,128)(2,1)} %param.14, f32[1536]{0:T(1024)S(1)} %get-tuple-element.3, f32[1536]{0:T(1024)S(1)} %get-tuple-element.4, f32[192]{0:T(256)S(1)} %add_rsqrt_fusion, f32[192]{0:T(256)S(1)} %broadcast_multiply_fusion, bf16[192,768]{1,0:T(8,128)(2,1)S(1)} %copy-done.1, ...), kind=kOutput, calls=%fused_computation.10 | convolution fusion | flops 457555968 | bytes 3257857 | tf_op jit(solution)/shard_map/dot_general | solution.py:150
  27.9 165.1 %all-gather.2.cloned.1.call-done.key_ref.value_ref = bf16[12288,1536]{1,0:T(8,128)(2,1)} async-done(((bf16[192,1536]{1,0:T(8,128)(2,1)}), bf16[12288,1536]{1,0:T(8,128)(2,1)}) %all-gather.2.cloned.1.call-update) | async-done | bytes 37748752 | tf_op jit(solution)/shard_map/all_gather | solution.py:165
  193.0 30.0 %shard_map.104 = bf16[192,768]{1,0:T(8,128)(2,1)} custom-call(s32[4]{0:T(128)} %pad_add_fusion.span_ref, bf16[192,768]{1,0:T(8,128)(2,1)} %convolution_convert_fusion.2.query_ref, bf16[12288,1536]{1,0:T(8,128)(2,1)} %all-gather.2.cloned.1.call-done.key_ref.value_ref, bf16[12288,1536]{1,0:T(8,128)(2,1)} %all-gather.2.cloned.1.call-done.key_ref.value_ref, ...), custom_call_target="tpu_custom_call" | custom-call | tf_op jit(solution)/shard_map/pallas_call | solution.py:98
  222.9 0.7 collective-permute-start.1
  223.6 0.1 dynamic-slice_add_fusion
  223.7 1.4 fusion.7
  225.1 2.5 %add_convert_fusion = (bf16[192,768]{1,0:T(8,128)(2,1)}, bf16[192,768]{1,0:T(8,128)(2,1)}) fusion(bf16[192,768]{1,0:T(8,128)(2,1)S(1)} %copy-done.1, f32[]{:T(128)} %bitcast.9, f32[192,768]{1,0:T(8,128)S(1)} %fusion.7, bf16[192,768]{1,0:T(8,128)(2,1)S(1)} %collective-permute-done.1, bf16[768,768]{1,0:T(8,128)(2,1)} %collective-permute-done.2, ...), kind=kOutput, calls=%fused_computation.19 | convolution fusion | flops 227524608 | bytes 2952196 | tf_op jit(solution)/shard_map/dot_general | solution.py:174
  (14 shorter events, 0.1 us)
Async XLA Ops:
  7.2 8.9 %copy-start = (bf16[768,1536]{1,0:T(8,128)(2,1)S(1)}, bf16[768,1536]{1,0:T(8,128)(2,1)}, u32[]{:S(2)}) copy-start(bf16[768,1536]{1,0:T(8,128)(2,1)} %param.17) | copy-start | bytes 7077892
  7.2 185.8 %all-gather.2.cloned.1.call-start = ((), (), s32[]{:S(2)}) async-start(), calls=%async_computation | async-start | bytes 38338560 | tf_op jit(solution)/shard_map/all_gather | solution.py:165
  7.2 4.0 %collective-permute-start = (bf16[192,768]{1,0:T(8,128)(2,1)}, bf16[192,768]{1,0:T(8,128)(2,1)S(1)}, u32[]{:S(2)}, u32[]{:S(2)}) collective-permute-start(bf16[192,768]{1,0:T(8,128)(2,1)} %param.9), channel_id=1, source_target_pairs={{0,1},{1,0},{2,3},{3,2},{4,5},{5,4},{6,7},{7,6},{8,9},{9,8},{10,11... | collective-permute-start | bytes 884744 | tf_op jit(solution)/shard_map/ppermute | solution.py:127
  8.8 2.4 %copy-start.2 = (f32[3,1536]{1,0:T(4,128)S(1)}, f32[3,1536]{1,0:T(4,128)}, u32[]{:S(2)}) copy-start(f32[3,1536]{1,0:T(4,128)} %param.13) | copy-start | bytes 55300
  8.8 2.4 %copy-start.1 = (bf16[192,768]{1,0:T(8,128)(2,1)S(1)}, bf16[192,768]{1,0:T(8,128)(2,1)}, u32[]{:S(2)}) copy-start(bf16[192,768]{1,0:T(8,128)(2,1)} %param.9) | copy-start | bytes 884740
  11.7 2.6 %copy-start.3 = (bf16[1536,768]{1,0:T(8,128)(2,1)S(1)}, bf16[1536,768]{1,0:T(8,128)(2,1)}, u32[]{:S(2)}) copy-start(bf16[1536,768]{1,0:T(8,128)(2,1)} %param.15) | copy-start | bytes 7077892
  16.1 1.3 copy-start.4
  17.2 207.9 %collective-permute-start.2 = (bf16[768,768]{1,0:T(8,128)(2,1)}, bf16[768,768]{1,0:T(8,128)(2,1)}, u32[]{:S(2)}, u32[]{:S(2)}) collective-permute-start(bf16[768,768]{1,0:T(8,128)(2,1)} %constant_dynamic-slice_fusion), channel_id=1, source_target_pairs={{0,1},{1,0},{2,3},{3,2},{4,5},{5,4},{6,7},{7,6},{8,9},{9,8},{10,11... | collective-permute-start | bytes 3538952 | tf_op jit(solution)/shard_map/ppermute | solution.py:172
  222.9 2.2 collective-permute-start.1
Sparse Core Ops, SparseCore 0:
  16.2 176.7 all-gather.1

commit v10 on v9

--- a/solution.py
+++ b/solution.py
@@ -31,15 +31,18 @@
         sum_ref[...] = jnp.zeros(sum_ref.shape, jnp.float32)
         acc_ref[...] = jnp.zeros(acc_ref.shape, jnp.float32)
 
-    def step(masked):
+    def step(masked, offset, size):
         rows = query_ref.shape[0]
+        keys = pl.ds(offset, size)
         if masked:
-            key_index = block * KEY_BLOCK + lax.broadcasted_iota(jnp.int32, (rows, KEY_BLOCK), 1)
+            key_index = (
+                block * KEY_BLOCK + offset + lax.broadcasted_iota(jnp.int32, (rows, size), 1)
+            )
             valid = jnp.logical_and(key_index >= low_ref[...], key_index < high_ref[...])
         for head in range(heads):
             cols = slice(head * HEAD_DIM, (head + 1) * HEAD_DIM)
             raw = lax.dot_general(
-                query_ref[:, cols], key_ref[:, cols], (((1,), (1,)), ((), ())),
+                query_ref[:, cols], key_ref[keys, cols], (((1,), (1,)), ((), ())),
                 preferred_element_type=jnp.float32,
             )
             old_max = max_ref[head]
@@ -54,23 +57,34 @@
             alpha = jnp.exp2((old_max - new_max) * EXP2_SCALE)
             sum_ref[head] = alpha * sum_ref[head] + jnp.sum(probs, axis=1, keepdims=True)
             acc_ref[:, cols] = alpha * acc_ref[:, cols] + jnp.dot(
-                probs.astype(jnp.bfloat16), value_ref[:, cols],
+                probs.astype(jnp.bfloat16), value_ref[keys, cols],
                 preferred_element_type=jnp.float32,
             )
             max_ref[head] = new_max
 
+    half = KEY_BLOCK // 2
+    base = block * KEY_BLOCK
     touched = jnp.logical_and(block >= first, block <= last)
-    whole_block = jnp.logical_and(
-        block * KEY_BLOCK >= span_ref[2], (block + 1) * KEY_BLOCK <= span_ref[3]
-    )
+    whole_block = jnp.logical_and(base >= span_ref[2], base + KEY_BLOCK <= span_ref[3])
+    edge = jnp.logical_and(touched, jnp.logical_not(whole_block))
+    need_low = jnp.logical_and(base < span_ref[1], base + half > span_ref[0])
+    need_high = jnp.logical_and(base + half < span_ref[1], base + KEY_BLOCK > span_ref[0])
 
     @pl.when(jnp.logical_and(touched, whole_block))
     def _():
-        step(False)
-
-    @pl.when(jnp.logical_and(touched, jnp.logical_not(whole_block)))
-    def _():
-        step(True)
+        step(False, 0, KEY_BLOCK)
+
+    @pl.when(jnp.logical_and(edge, jnp.logical_and(need_low, need_high)))
+    def _():
+        step(True, 0, KEY_BLOCK)
+
+    @pl.when(jnp.logical_and(edge, jnp.logical_and(need_low, jnp.logical_not(need_high))))
+    def _():
+        step(True, 0, half)
+
+    @pl.when(jnp.logical_and(edge, jnp.logical_and(need_high, jnp.logical_not(need_low))))
+    def _():
+        step(True, half, half)
 
     @pl.when(block == pl.num_programs(0) - 1)
     def _():

time: 236 us -> 235 us (level); the launches traced: 234 us -> 231 us
  Pallas kernels: 30 us -> 26.6 us
    pallas_call x1, Pallas kernels: 30 us -> 26.6 us  [attention(): pl.pallas_call(attention_kernel, grid_spec=pltpu.PrefetchScalarGridSpec(n...]
  transfers between devices with their start and end apart: 4 -> 4, of which waited for: 1 -> 1; matrix products, arithmetic and copies ran while one was open for 7% -> 7% of each run, Pallas kernels for 13% -> 12%
where the time goes in v10:
time: 235 us; the launch traced here: 231 us
  waiting for transfers between devices  165 us (70%)
  Pallas kernels  26.6 us (11%)
  between operations  15 us (6%)
  matrix products  10.4 us (4%)
  other arithmetic  9.78 us (4%)
  local copies, waits for them, and re-layouts  2.69 us (1%)
    all_gather x1, waiting for transfers between devices, on_device(): lax.all_gather(jnp.concatenate([keys, values], axis=1), 'req', axis=0, ti...  165 us
    pallas_call x1, Pallas kernels, attention(): pl.pallas_call(attention_kernel, grid_spec=pltpu.PrefetchScalarGridSpec(n...  26.6 us
  transfers between devices with their start and end apart: 4, of which 1 were waited for; matrix products, arithmetic and copies ran while one was open for 7% of the time, Pallas kernels for 12%

profile of v10, /device:TPU:17, one launch (start us, length us, event | category | flops | bytes accessed | tf_op | source)
XLA Modules:
  0.0 231.1 jit_solution(12955947358681136816)
XLA Ops:
  7.2 0.0 copy-start
  7.2 0.0 all-gather.2.cloned.1.call-start
  7.2 0.8 collective-permute-start
  8.8 0.0 copy-start.2
  8.8 0.0 copy-start.1
  8.8 2.3 %multiply_reduce_fusion = f32[3072]{0:T(1024)S(1)} fusion(f32[256,4608]{1,0:T(8,128)} %param.12, f32[256]{0:T(256)S(1)} %divide_multiply_fusion), kind=kLoop, calls=%fused_computation | loop fusion | flops 1569792 | bytes 3159040 | tf_op jit(solution)/shard_map/reduce_sum | solution.py:155
  11.1 0.1 slice_reduce_fusion
  11.2 0.0 collective-permute-done
  11.2 0.2 convert_reduce_fusion
  11.4 0.3 fusion.3
  11.7 0.0 copy-start.3
  11.8 2.6 %convolution_convert_fusion = bf16[192,768]{1,0:T(8,128)(2,1)S(1)} fusion(bf16[1536,768]{1,0:T(8,128)(2,1)} %param.16, f32[1536]{0:T(1024)S(1)} %get-tuple-element.3, f32[1536]{0:T(1024)S(1)} %get-tuple-element.4, f32[192]{0:T(256)S(1)} %add_rsqrt_fusion, f32[192]{0:T(256)S(1)} %broadcast_multiply_fusion, bf16[192,768]{1,0:T(8,128)(2,1)S(1)} %copy-done.1, ...), kind=kOutput, calls=%fused_computation.8 | convolution fusion | flops 457555968 | bytes 3257857 | tf_op jit(solution)/shard_map/dot_general | solution.py:166
  14.3 0.8 convolution_convert_fusion.1
  15.1 0.9 pad_maximum_fusion
  16.0 0.0 all-gather.2.cloned.1.call-update
  16.1 0.0 copy-start.4
  16.1 1.1 constant_dynamic-slice_fusion
  17.2 0.1 collective-permute-start.2
  17.3 0.2 reduce-window.8
  17.5 0.1 select_reduce_fusion.1
  17.6 0.8 copy.13.low_ref
  18.4 0.8 copy.14.high_ref
  19.2 0.8 fusion.15
  19.9 3.2 %pad_add_fusion.span_ref = s32[4]{0:T(128)} fusion(s32[1]{0:T(128)} %bitcast.6, s32[1]{0:T(128)} %bitcast.5, s32[1]{0:T(128)} %bitcast.4, s32[1]{0:T(128)} %bitcast.3), kind=kLoop, calls=%fused_computation.31 | loop fusion | flops 12 | bytes 32 | tf_op jit(solution)/shard_map/stack | solution.py:176
  23.1 1.6 multiply_reduce_fusion.1
  24.7 3.1 %convolution_convert_fusion.2.query_ref = bf16[192,768]{1,0:T(8,128)(2,1)} fusion(bf16[1536,768]{1,0:T(8,128)(2,1)} %param.14, f32[1536]{0:T(1024)S(1)} %get-tuple-element.3, f32[1536]{0:T(1024)S(1)} %get-tuple-element.4, f32[192]{0:T(256)S(1)} %add_rsqrt_fusion, f32[192]{0:T(256)S(1)} %broadcast_multiply_fusion, bf16[192,768]{1,0:T(8,128)(2,1)S(1)} %copy-done.1, ...), kind=kOutput, calls=%fused_computation.10 | convolution fusion | flops 457555968 | bytes 3257857 | tf_op jit(solution)/shard_map/dot_general | solution.py:164
  27.9 165.1 %all-gather.2.cloned.1.call-done.key_ref.value_ref = bf16[12288,1536]{1,0:T(8,128)(2,1)} async-done(((bf16[192,1536]{1,0:T(8,128)(2,1)}), bf16[12288,1536]{1,0:T(8,128)(2,1)}) %all-gather.2.cloned.1.call-update) | async-done | bytes 37748752 | tf_op jit(solution)/shard_map/all_gather | solution.py:179
  193.0 26.6 %shard_map.104 = bf16[192,768]{1,0:T(8,128)(2,1)} custom-call(s32[4]{0:T(128)} %pad_add_fusion.span_ref, bf16[192,768]{1,0:T(8,128)(2,1)} %convolution_convert_fusion.2.query_ref, bf16[12288,1536]{1,0:T(8,128)(2,1)} %all-gather.2.cloned.1.call-done.key_ref.value_ref, bf16[12288,1536]{1,0:T(8,128)(2,1)} %all-gather.2.cloned.1.call-done.key_ref.value_ref, ...), custom_call_target="tpu_custom_call" | custom-call | tf_op jit(solution)/shard_map/pallas_call | solution.py:112
  219.6 0.7 collective-permute-start.1
  220.2 0.1 dynamic-slice_add_fusion
  220.4 1.4 fusion.7
  221.8 2.5 %add_convert_fusion = (bf16[192,768]{1,0:T(8,128)(2,1)}, bf16[192,768]{1,0:T(8,128)(2,1)}) fusion(bf16[192,768]{1,0:T(8,128)(2,1)S(1)} %copy-done.1, f32[]{:T(128)} %bitcast.9, f32[192,768]{1,0:T(8,128)S(1)} %fusion.7, bf16[192,768]{1,0:T(8,128)(2,1)S(1)} %collective-permute-done.1, bf16[768,768]{1,0:T(8,128)(2,1)} %collective-permute-done.2, ...), kind=kOutput, calls=%fused_computation.19 | convolution fusion | flops 227524608 | bytes 2952196 | tf_op jit(solution)/shard_map/dot_general | solution.py:188
  (14 shorter events, 0.1 us)
Async XLA Ops:
  7.2 8.9 %copy-start = (bf16[768,1536]{1,0:T(8,128)(2,1)S(1)}, bf16[768,1536]{1,0:T(8,128)(2,1)}, u32[]{:S(2)}) copy-start(bf16[768,1536]{1,0:T(8,128)(2,1)} %param.17) | copy-start | bytes 7077892
  7.2 185.8 %all-gather.2.cloned.1.call-start = ((), (), s32[]{:S(2)}) async-start(), calls=%async_computation | async-start | bytes 38338560 | tf_op jit(solution)/shard_map/all_gather | solution.py:179
  7.2 4.0 %collective-permute-start = (bf16[192,768]{1,0:T(8,128)(2,1)}, bf16[192,768]{1,0:T(8,128)(2,1)S(1)}, u32[]{:S(2)}, u32[]{:S(2)}) collective-permute-start(bf16[192,768]{1,0:T(8,128)(2,1)} %param.9), channel_id=1, source_target_pairs={{0,1},{1,0},{2,3},{3,2},{4,5},{5,4},{6,7},{7,6},{8,9},{9,8},{10,11... | collective-permute-start | bytes 884744 | tf_op jit(solution)/shard_map/ppermute | solution.py:141
  8.8 2.4 %copy-start.2 = (f32[3,1536]{1,0:T(4,128)S(1)}, f32[3,1536]{1,0:T(4,128)}, u32[]{:S(2)}) copy-start(f32[3,1536]{1,0:T(4,128)} %param.13) | copy-start | bytes 55300
  8.8 2.4 %copy-start.1 = (bf16[192,768]{1,0:T(8,128)(2,1)S(1)}, bf16[192,768]{1,0:T(8,128)(2,1)}, u32[]{:S(2)}) copy-start(bf16[192,768]{1,0:T(8,128)(2,1)} %param.9) | copy-start | bytes 884740
  11.7 2.6 %copy-start.3 = (bf16[1536,768]{1,0:T(8,128)(2,1)S(1)}, bf16[1536,768]{1,0:T(8,128)(2,1)}, u32[]{:S(2)}) copy-start(bf16[1536,768]{1,0:T(8,128)(2,1)} %param.15) | copy-start | bytes 7077892
  16.1 1.3 copy-start.4
  17.2 204.5 %collective-permute-start.2 = (bf16[768,768]{1,0:T(8,128)(2,1)}, bf16[768,768]{1,0:T(8,128)(2,1)}, u32[]{:S(2)}, u32[]{:S(2)}) collective-permute-start(bf16[768,768]{1,0:T(8,128)(2,1)} %constant_dynamic-slice_fusion), channel_id=1, source_target_pairs={{0,1},{1,0},{2,3},{3,2},{4,5},{5,4},{6,7},{7,6},{8,9},{9,8},{10,11... | collective-permute-start | bytes 3538952 | tf_op jit(solution)/shard_map/ppermute | solution.py:186
  219.6 2.2 collective-permute-start.1
Sparse Core Ops, SparseCore 0:
  16.2 176.7 all-gather.1

commit v11 on v9

--- a/solution.py
+++ b/solution.py
@@ -118,6 +118,35 @@
     )(span, query, packed, packed, query_low, query_high)
 
 
+def project_kernel(rows_ref, shift_ref, scale_ref, key_w_ref, value_w_ref, packed_ref, normed_ref):
+    as_float = rows_ref[...].astype(jnp.float32)
+    mean = jnp.mean(as_float, axis=1, keepdims=True)
+    centred = as_float - mean
+    variance = jnp.mean(centred * centred, axis=1, keepdims=True)
+    normed = (
+        centred * lax.rsqrt(variance + 1e-06) * (1.0 + scale_ref[...]) + shift_ref[...]
+    ).astype(jnp.bfloat16)
+    normed_ref[...] = normed
+    width = key_w_ref.shape[1]
+    packed_ref[:, :width] = jnp.dot(
+        normed, key_w_ref[...], preferred_element_type=jnp.float32
+    ).astype(jnp.bfloat16)
+    packed_ref[:, width:] = jnp.dot(
+        normed, value_w_ref[...], preferred_element_type=jnp.float32
+    ).astype(jnp.bfloat16)
+
+
+def project(full_rows, shift, scale, w_key, w_value):
+    rows, features = full_rows.shape
+    return pl.pallas_call(
+        project_kernel,
+        out_shape=(
+            jax.ShapeDtypeStruct((rows, 2 * w_key.shape[1]), jnp.bfloat16),
+            jax.ShapeDtypeStruct((rows, features), jnp.bfloat16),
+        ),
+    )(full_rows, shift[None, :], scale[None, :], w_key, w_value)
+
+
 def on_device(
     tokens, video_lengths, timestep, time_weight, block_mod, w_query, w_key, w_value, w_out
 ):
@@ -142,14 +171,8 @@
     shift = shift_scale[0] + block_mod[0]
     scale = shift_scale[1] + block_mod[1]
     gate = jnp.sum(activated * time_weight[:, 2 * width :], axis=0) + block_mod[2]
-    as_float = full_rows.astype(jnp.float32)
-    mean = jnp.mean(as_float, axis=1, keepdims=True)
-    centred = as_float - mean
-    variance = jnp.mean(centred * centred, axis=1, keepdims=True)
-    normed = (centred * lax.rsqrt(variance + 1e-06) * (1.0 + scale) + shift).astype(jnp.bfloat16)
+    kv_rows, normed = project(full_rows, shift, scale, w_key, w_value)
     query = jnp.dot(normed, w_query, preferred_element_type=jnp.float32).astype(jnp.bfloat16)
-    keys = jnp.dot(normed, w_key, preferred_element_type=jnp.float32).astype(jnp.bfloat16)
-    values = jnp.dot(normed, w_value, preferred_element_type=jnp.float32).astype(jnp.bfloat16)
     start_row = lax.axis_index("req") * tok_rows
     query_index = start_row + jnp.arange(tok_rows, dtype=jnp.int32)
     video_ends = jnp.cumsum(video_lengths)
@@ -162,7 +185,7 @@
     span = jnp.stack(
         [jnp.min(query_low), jnp.max(query_high), jnp.max(query_low), jnp.min(query_high)]
     ).astype(jnp.int32)
-    packed = lax.all_gather(jnp.concatenate([keys, values], axis=1), "req", axis=0, tiled=True)
+    packed = lax.all_gather(kv_rows, "req", axis=0, tiled=True)
     attended = attention(span, query, packed, query_low[:, None], query_high[:, None])
     share = w_out.shape[1] // 2
     core = lax.axis_index("tp")

time: 236 us -> 238 us (level)
  Pallas kernels: 30 us -> 34.8 us
  matrix products: 10.4 us -> 6.9 us
    pallas_call x0 -> x1, Pallas kernels: none -> 4.83 us  [project(): pl.pallas_call(project_kernel, out_shape=(jax.ShapeDtypeStruct((rows, 2 *...]
    dot_general x2 -> x0, matrix products: 3.34 us -> none  [the longest x1 2.57 us: on_device(): jnp.dot(normed, w_value, preferred_element_type=jnp.float32)]
where the time goes in v11:
time: 238 us; the launch traced here: 236 us
  waiting for transfers between devices  165 us (69%)
  Pallas kernels  34.8 us (15%)
  between operations  14.9 us (6%)
  other arithmetic  9.87 us (4%)
  matrix products  6.9 us (3%)
  local copies, waits for them, and re-layouts  2.65 us (1%)
    all_gather x1, waiting for transfers between devices, on_device(): packed = lax.all_gather(kv_rows, 'req', axis=0, tiled=True)  165 us
    pallas_call x1, Pallas kernels, attention(): pl.pallas_call(attention_kernel, grid_spec=pltpu.PrefetchScalarGridSpec(n...  30 us
    pallas_call x1, Pallas kernels, project(): pl.pallas_call(project_kernel, out_shape=(jax.ShapeDtypeStruct((rows, 2 *...  4.83 us
  transfers between devices with their start and end apart: 4, of which 1 were waited for; matrix products, arithmetic and copies ran while one was open for 7% of the time, Pallas kernels for 13%

profile of v11, /device:TPU:17, one launch (start us, length us, event | category | flops | bytes accessed | tf_op | source)
XLA Modules:
  0.0 236.0 jit_solution(6066542048970289241)
XLA Ops:
  7.2 0.0 copy-start
  7.2 0.0 copy-start.1
  7.2 0.0 copy-start.2
  7.2 0.0 all-gather.2.cloned.1.call-start
  7.2 0.8 collective-permute-start
  8.8 2.3 multiply_reduce_fusion
  11.1 0.6 slice_reduce_fusion
  11.7 0.0 collective-permute-done
  11.7 0.0 copy-done.1
  11.7 1.0 maximum_select_fusion.rows_ref
  12.7 4.8 %shard_map.104 = (bf16[192,1536]{1,0:T(8,128)(2,1)}, bf16[192,1536]{1,0:T(8,128)(2,1)}) custom-call(bf16[192,1536]{1,0:T(8,128)(2,1)} %maximum_select_fusion.rows_ref, f32[1,1536]{1,0:T(1,128)} %get-tuple-element.16.shift_ref, f32[1,1536]{1,0:T(1,128)} %get-tuple-element.15.scale_ref, bf16[1536,768]{1,0:T(8,128)(2,1)} %key_w_ref.1, bf16[1536,768]{1,0:T(8,128)(2,1)} %value_w_ref.1), custom_call_target="tpu_custom_call" | custom-call | tf_op jit(solution)/shard_map/pallas_call | solution.py:141
  17.5 0.0 all-gather.2.cloned.1.call-update
  17.6 1.1 constant_dynamic-slice_fusion
  18.7 0.2 collective-permute-start.2
  18.8 0.0 copy-done.4
  18.8 0.2 reduce-window.8
  19.0 0.1 select_reduce_fusion.1
  19.1 0.8 copy.13.low_ref
  19.9 0.8 copy.14.high_ref
  20.6 0.8 fusion.6
  21.4 3.3 %pad_add_fusion.span_ref = s32[4]{0:T(128)} fusion(s32[1]{0:T(128)} %bitcast.6, s32[1]{0:T(128)} %bitcast.5, s32[1]{0:T(128)} %bitcast.4, s32[1]{0:T(128)} %bitcast.3), kind=kLoop, calls=%fused_computation.19 | loop fusion | flops 12 | bytes 32 | tf_op jit(solution)/shard_map/stack | solution.py:185
  24.6 1.6 multiply_reduce_fusion.1
  26.2 0.0 copy-done.3
  26.2 3.0 %convolution_convert_fusion.query_ref = bf16[192,768]{1,0:T(8,128)(2,1)} fusion(bf16[192,1536]{1,0:T(8,128)(2,1)S(1)} %copy-done.3, bf16[1536,768]{1,0:T(8,128)(2,1)} %param.14), kind=kOutput, calls=%fused_computation.4 | convolution fusion | flops 453132288 | bytes 3244032 | tf_op jit(solution)/shard_map/dot_general | solution.py:175
  29.2 165.2 %all-gather.2.cloned.1.call-done.key_ref.value_ref = bf16[12288,1536]{1,0:T(8,128)(2,1)} async-done(((bf16[192,1536]{1,0:T(8,128)(2,1)}), bf16[12288,1536]{1,0:T(8,128)(2,1)}) %all-gather.2.cloned.1.call-update) | async-done | bytes 37748752 | tf_op jit(solution)/shard_map/all_gather | solution.py:188
  194.5 30.0 %shard_map.105 = bf16[192,768]{1,0:T(8,128)(2,1)} custom-call(s32[4]{0:T(128)} %pad_add_fusion.span_ref, bf16[192,768]{1,0:T(8,128)(2,1)} %convolution_convert_fusion.query_ref, bf16[12288,1536]{1,0:T(8,128)(2,1)} %all-gather.2.cloned.1.call-done.key_ref.value_ref, bf16[12288,1536]{1,0:T(8,128)(2,1)} %all-gather.2.cloned.1.call-done.key_ref.value_ref, ...), custom_call_target="tpu_custom_call" | custom-call | tf_op jit(solution)/shard_map/pallas_call | solution.py:98
  224.4 0.7 collective-permute-start.1
  225.1 0.1 dynamic-slice_add_fusion
  225.2 1.4 fusion.1
  226.6 0.0 collective-permute-done.2
  226.6 0.0 collective-permute-done.1
  226.6 2.5 %add_convert_fusion = (bf16[192,768]{1,0:T(8,128)(2,1)}, bf16[192,768]{1,0:T(8,128)(2,1)}) fusion(bf16[192,768]{1,0:T(8,128)(2,1)S(1)} %copy-done.1, f32[]{:T(128)} %bitcast.9, f32[192,768]{1,0:T(8,128)S(1)} %fusion.1, bf16[192,768]{1,0:T(8,128)(2,1)S(1)} %collective-permute-done.1, bf16[768,768]{1,0:T(8,128)(2,1)} %collective-permute-done.2, ...), kind=kOutput, calls=%fused_computation.8 | convolution fusion | flops 227524608 | bytes 2952196 | tf_op jit(solution)/shard_map/dot_general | solution.py:197
  (9 shorter events, 0.1 us)
Async XLA Ops:
  7.2 10.4 %copy-start = (bf16[768,1536]{1,0:T(8,128)(2,1)S(1)}, bf16[768,1536]{1,0:T(8,128)(2,1)}, u32[]{:S(2)}) copy-start(bf16[768,1536]{1,0:T(8,128)(2,1)} %param.17) | copy-start | bytes 7077892
  7.2 4.5 %copy-start.1 = (bf16[192,768]{1,0:T(8,128)(2,1)S(1)}, bf16[192,768]{1,0:T(8,128)(2,1)}, u32[]{:S(2)}) copy-start(bf16[192,768]{1,0:T(8,128)(2,1)} %param.9) | copy-start | bytes 884740
  7.2 3.9 %copy-start.2 = (f32[3,1536]{1,0:T(4,128)S(1)}, f32[3,1536]{1,0:T(4,128)}, u32[]{:S(2)}) copy-start(f32[3,1536]{1,0:T(4,128)} %param.13) | copy-start | bytes 55300
  7.2 187.3 %all-gather.2.cloned.1.call-start = ((), (), s32[]{:S(2)}) async-start(), calls=%async_computation | async-start | bytes 38338560 | tf_op jit(solution)/shard_map/all_gather | solution.py:188
  7.2 4.5 %collective-permute-start = (bf16[192,768]{1,0:T(8,128)(2,1)}, bf16[192,768]{1,0:T(8,128)(2,1)S(1)}, u32[]{:S(2)}, u32[]{:S(2)}) collective-permute-start(bf16[192,768]{1,0:T(8,128)(2,1)} %param.9), channel_id=1, source_target_pairs={{0,1},{1,0},{2,3},{3,2},{4,5},{5,4},{6,7},{7,6},{8,9},{9,8},{10,11... | collective-permute-start | bytes 884744 | tf_op jit(solution)/shard_map/ppermute | solution.py:156
  17.5 1.3 copy-start.4
  17.5 8.7 %copy-start.3 = (bf16[192,1536]{1,0:T(8,128)(2,1)S(1)}, bf16[192,1536]{1,0:T(8,128)(2,1)}, u32[]{:S(2)}) copy-start(bf16[192,1536]{1,0:T(8,128)(2,1)} %get-tuple-element.4) | copy-start | bytes 1769476
  18.7 207.9 %collective-permute-start.2 = (bf16[768,768]{1,0:T(8,128)(2,1)}, bf16[768,768]{1,0:T(8,128)(2,1)}, u32[]{:S(2)}, u32[]{:S(2)}) collective-permute-start(bf16[768,768]{1,0:T(8,128)(2,1)} %constant_dynamic-slice_fusion), channel_id=1, source_target_pairs={{0,1},{1,0},{2,3},{3,2},{4,5},{5,4},{6,7},{7,6},{8,9},{9,8},{10,11... | collective-permute-start | bytes 3538952 | tf_op jit(solution)/shard_map/ppermute | solution.py:195
  224.4 2.2 collective-permute-start.1
Sparse Core Ops, SparseCore 0:
  17.7 176.7 all-gather.1

commit v12 on v9

--- a/solution.py
+++ b/solution.py
@@ -18,8 +18,8 @@
     return 5.0 * frac / (1.0 + 4.0 * frac)
 
 
-def attention_kernel(span_ref, query_ref, key_ref, value_ref, low_ref, high_ref, out_ref,
-                     max_ref, sum_ref, acc_ref):
+def attention_kernel(span_ref, query_ref, key_ref, value_ref, low_ref, high_ref, own_w_ref,
+                     other_w_ref, own_ref, other_ref, max_ref, sum_ref, acc_ref, attended_ref):
     block = pl.program_id(0)
     heads = query_ref.shape[1] // HEAD_DIM
     first = span_ref[0] // KEY_BLOCK
@@ -76,10 +76,16 @@
     def _():
         for head in range(heads):
             cols = slice(head * HEAD_DIM, (head + 1) * HEAD_DIM)
-            out_ref[:, cols] = (acc_ref[:, cols] / sum_ref[head]).astype(out_ref.dtype)
-
-
-def attention(span, query, packed, query_low, query_high):
+            attended_ref[:, cols] = (acc_ref[:, cols] / sum_ref[head]).astype(jnp.bfloat16)
+        own_ref[...] = jnp.dot(
+            attended_ref[...], own_w_ref[...], preferred_element_type=jnp.float32
+        )
+        other_ref[...] = jnp.dot(
+            attended_ref[...], other_w_ref[...], preferred_element_type=jnp.float32
+        )
+
+
+def attention(span, query, packed, query_low, query_high, own_w, other_w):
     rows, width = query.shape
     blocks = packed.shape[0] // KEY_BLOCK
 
@@ -106,16 +112,25 @@
                 pl.BlockSpec((KEY_BLOCK, width), value_map),
                 pl.BlockSpec((rows, 1), whole),
                 pl.BlockSpec((rows, 1), whole),
+                pl.BlockSpec(own_w.shape, whole),
+                pl.BlockSpec(other_w.shape, whole),
             ],
-            out_specs=pl.BlockSpec((rows, width), whole),
+            out_specs=[
+                pl.BlockSpec((rows, own_w.shape[1]), whole),
+                pl.BlockSpec((rows, other_w.shape[1]), whole),
+            ],
             scratch_shapes=[
                 pltpu.VMEM((heads, rows, 1), jnp.float32),
                 pltpu.VMEM((heads, rows, 1), jnp.float32),
                 pltpu.VMEM((rows, width), jnp.float32),
+                pltpu.VMEM((rows, width), jnp.bfloat16),
             ],
         ),
-        out_shape=jax.ShapeDtypeStruct((rows, width), jnp.bfloat16),
-    )(span, query, packed, packed, query_low, query_high)
+        out_shape=(
+            jax.ShapeDtypeStruct((rows, own_w.shape[1]), jnp.float32),
+            jax.ShapeDtypeStruct((rows, other_w.shape[1]), jnp.float32),
+        ),
+    )(span, query, packed, packed, query_low, query_high, own_w, other_w)
 
 
 def on_device(
@@ -163,17 +178,15 @@
         [jnp.min(query_low), jnp.max(query_high), jnp.max(query_low), jnp.min(query_high)]
     ).astype(jnp.int32)
     packed = lax.all_gather(jnp.concatenate([keys, values], axis=1), "req", axis=0, tiled=True)
-    attended = attention(span, query, packed, query_low[:, None], query_high[:, None])
     share = w_out.shape[1] // 2
     core = lax.axis_index("tp")
-    swap = [(0, 1), (1, 0)]
     own_columns = lax.dynamic_slice_in_dim(w_out, core * share, share, axis=1)
     other_columns = lax.dynamic_slice_in_dim(w_out, (1 - core) * share, share, axis=1)
-    partner_rows = lax.ppermute(other_columns, "tp", perm=swap)
-    partner_attended = lax.ppermute(attended, "tp", perm=swap)
-    projected = jnp.dot(attended, own_columns, preferred_element_type=jnp.float32) + jnp.dot(
-        partner_attended, partner_rows, preferred_element_type=jnp.float32
-    )
+    own_part, other_part = attention(
+        span, query, packed, query_low[:, None], query_high[:, None], own_columns, other_columns
+    )
+    partner_part = lax.ppermute(other_part, "tp", perm=[(0, 1), (1, 0)])
+    projected = own_part + partner_part
     gate_share = lax.dynamic_slice_in_dim(gate, core * share, share)
     branch = gate_share[None, :] * projected
     velocity = branch.astype(jnp.bfloat16)

time: 236 us -> 235 us (level)
  matrix products: 10.4 us -> 3.01 us
  local copies, waits for them, and re-layouts: 2.69 us -> 5.8 us
    dot_general x2 -> x0, matrix products: 3.88 us -> none  [the longest x1 2.51 us: on_device(): jnp.dot(partner_attended, partner_rows, preferred_element_type=jnp.float32)]
  transfers between devices with their start and end apart: 4 -> 3, of which waited for: 1 -> 2; matrix products, arithmetic and copies ran while one was open for 7% -> 6% of each run, Pallas kernels for 13% -> 0%
where the time goes in v12:
time: 235 us; the launch traced here: 234 us
  waiting for transfers between devices  167 us (71%)
  Pallas kernels  31.7 us (13%)
  between operations  14.9 us (6%)
  other arithmetic  10.6 us (5%)
  local copies, waits for them, and re-layouts  5.8 us (2%)
  matrix products  3.01 us (1%)
    all_gather x1, waiting for transfers between devices, on_device(): lax.all_gather(jnp.concatenate([keys, values], axis=1), 'req', axis=0, ti...  166 us
    pallas_call x1, Pallas kernels, attention(): pl.pallas_call(attention_kernel, grid_spec=pltpu.PrefetchScalarGridSpec(n...  31.7 us
  transfers between devices with their start and end apart: 3, of which 2 were waited for; matrix products, arithmetic and copies ran while one was open for 6% of the time, Pallas kernels for 0%

profile of v12, /device:TPU:17, one launch (start us, length us, event | category | flops | bytes accessed | tf_op | source)
XLA Modules:
  0.0 234.1 jit_solution(8456531748776808804)
XLA Ops:
  7.2 0.0 copy-start
  7.2 0.0 all-gather.2.cloned.1.call-start
  7.2 0.8 collective-permute-start
  8.8 0.0 copy-start.3
  8.8 0.0 copy-start.1
  8.8 2.3 multiply_reduce_fusion
  11.1 0.1 slice_reduce_fusion
  11.2 0.0 collective-permute-done
  11.2 0.2 convert_reduce_fusion
  11.4 0.3 fusion.2
  11.7 0.0 copy-start.4
  11.8 0.8 convolution_convert_fusion.1
  12.5 0.9 copy-done.4
  13.4 0.8 convolution_convert_fusion
  14.2 0.0 copy-start.6
  14.2 0.9 pad_maximum_fusion
  15.1 0.0 all-gather.2.cloned.1.call-update
  15.2 0.2 reduce-window.8
  15.4 0.1 select_reduce_fusion.1
  15.4 0.8 copy.14.high_ref
  16.2 0.8 copy.13.low_ref
  17.0 0.7 fusion.12
  17.7 3.1 %pad_add_fusion.span_ref = s32[4]{0:T(128)} fusion(s32[1]{0:T(128)} %bitcast.6, s32[1]{0:T(128)} %bitcast.5, s32[1]{0:T(128)} %bitcast.4, s32[1]{0:T(128)} %bitcast.3), kind=kLoop, calls=%fused_computation.29 | loop fusion | flops 12 | bytes 32 | tf_op jit(solution)/shard_map/stack | solution.py:177
  20.8 3.3 %constant_dynamic-slice_fusion = (bf16[768,768]{1,0:T(8,128)(2,1)}, bf16[768,768]{1,0:T(8,128)(2,1)}) fusion(bf16[768,1536]{1,0:T(8,128)(2,1)} %param.17, s32[]{:T(128)S(6)} %select_n.27, s32[]{:T(128)S(6)} %select_n.22), kind=kLoop, calls=%fused_computation.31 | loop fusion | bytes 4718600 | tf_op jit(solution)/shard_map/dynamic_slice | solution.py:184
  24.1 1.5 convolution_convert_fusion.2.query_ref
  25.6 166.5 %all-gather.2.cloned.1.call-done.key_ref.value_ref = bf16[12288,1536]{1,0:T(8,128)(2,1)} async-done(((bf16[192,1536]{1,0:T(8,128)(2,1)}), bf16[12288,1536]{1,0:T(8,128)(2,1)}) %all-gather.2.cloned.1.call-update) | async-done | bytes 37748752 | tf_op jit(solution)/shard_map/all_gather | solution.py:180
  192.1 31.7 %shard_map.104 = (f32[192,768]{1,0:T(8,128)}, f32[192,768]{1,0:T(8,128)}) custom-call(s32[4]{0:T(128)} %pad_add_fusion.span_ref, bf16[192,768]{1,0:T(8,128)(2,1)} %convolution_convert_fusion.2.query_ref, bf16[12288,1536]{1,0:T(8,128)(2,1)} %all-gather.2.cloned.1.call-done.key_ref.value_ref, ...), custom_call_target="tpu_custom_call" | custom-call | tf_op jit(solution)/shard_map/pallas_call | solution.py:104
  223.8 0.7 collective-permute-start.1
  224.5 1.6 multiply_reduce_fusion.1
  226.1 0.1 dynamic-slice_add_fusion
  226.2 0.1 collective-permute-done.1
  226.3 0.9 add_convert_fusion
  (15 shorter events, 0.1 us)
Async XLA Ops:
  7.2 4.6 %copy-start = (bf16[1536,768]{1,0:T(8,128)(2,1)S(1)}, bf16[1536,768]{1,0:T(8,128)(2,1)}, u32[]{:S(2)}) copy-start(bf16[1536,768]{1,0:T(8,128)(2,1)} %param.15) | copy-start | bytes 7077892
  7.2 184.9 %all-gather.2.cloned.1.call-start = ((), (), s32[]{:S(2)}) async-start(), calls=%async_computation | async-start | bytes 38338560 | tf_op jit(solution)/shard_map/all_gather | solution.py:180
  7.2 4.0 %collective-permute-start = (bf16[192,768]{1,0:T(8,128)(2,1)}, bf16[192,768]{1,0:T(8,128)(2,1)S(1)}, u32[]{:S(2)}, u32[]{:S(2)}) collective-permute-start(bf16[192,768]{1,0:T(8,128)(2,1)} %param.9), channel_id=1, source_target_pairs={{0,1},{1,0},{2,3},{3,2},{4,5},{5,4},{6,7},{7,6},{8,9},{9,8},{10,11... | collective-permute-start | bytes 884744 | tf_op jit(solution)/shard_map/ppermute | solution.py:142
  8.8 2.4 %copy-start.3 = (f32[3,1536]{1,0:T(4,128)S(1)}, f32[3,1536]{1,0:T(4,128)}, u32[]{:S(2)}) copy-start(f32[3,1536]{1,0:T(4,128)} %param.13) | copy-start | bytes 55300
  8.8 2.4 %copy-start.1 = (bf16[192,768]{1,0:T(8,128)(2,1)S(1)}, bf16[192,768]{1,0:T(8,128)(2,1)}, u32[]{:S(2)}) copy-start(bf16[192,768]{1,0:T(8,128)(2,1)} %param.9) | copy-start | bytes 884740
  11.7 1.7 copy-start.4
  14.2 1.0 copy-start.6
  20.8 3.3 %copy-start.5 = (bf16[1536,768]{1,0:T(8,128)(2,1)S(1)}, bf16[1536,768]{1,0:T(8,128)(2,1)}, u32[]{:S(2)}) copy-start(bf16[1536,768]{1,0:T(8,128)(2,1)} %param.14) | copy-start | bytes 7077892
  223.8 2.5 %copy-start.2 = (f32[192,768]{1,0:T(8,128)S(1)}, f32[192,768]{1,0:T(8,128)}, u32[]{:S(2)}) copy-start(f32[192,768]{1,0:T(8,128)} %get-tuple-element.4) | copy-start | bytes 1769476
  223.8 2.5 %collective-permute-start.1 = (f32[192,768]{1,0:T(8,128)}, f32[192,768]{1,0:T(8,128)S(1)}, u32[]{:S(2)}, u32[]{:S(2)}) collective-permute-start(f32[192,768]{1,0:T(8,128)} %get-tuple-element.5), channel_id=1, source_target_pairs={{0,1},{1,0},{2,3},{3,2},{4,5},{5,4},{6,7},{7,6},{8,9},{9,8},{10,11... | collective-permute-start | bytes 1769480 | tf_op jit(solution)/shard_map/ppermute | solution.py:188
Sparse Core Ops, SparseCore 0:
  15.3 176.7 all-gather.1

commit v13 on v12

--- a/solution.py
+++ b/solution.py
@@ -182,6 +182,7 @@
     core = lax.axis_index("tp")
     own_columns = lax.dynamic_slice_in_dim(w_out, core * share, share, axis=1)
     other_columns = lax.dynamic_slice_in_dim(w_out, (1 - core) * share, share, axis=1)
+    query, gate = lax.optimization_barrier((query, gate))
     own_part, other_part = attention(
         span, query, packed, query_low[:, None], query_high[:, None], own_columns, other_columns
     )

time: 235 us -> 240 us (1.021)
  the two profiles are of different devices: /device:TPU:17 before, /device:TPU:87 now
where the time goes in v13:
time: 240 us
  waiting for transfers between devices  164 us (68%)
  Pallas kernels  38.8 us (16%)
  between operations  14.9 us (6%)
  other arithmetic  11.6 us (5%)
  local copies, waits for them, and re-layouts  5.88 us (2%)
  matrix products  3.01 us (1%)
    all_gather x1, waiting for transfers between devices, on_device(): lax.all_gather(jnp.concatenate([keys, values], axis=1), 'req', axis=0, ti...  162 us
    pallas_call x1, Pallas kernels, attention(): pl.pallas_call(attention_kernel, grid_spec=pltpu.PrefetchScalarGridSpec(n...  38.8 us
  transfers between devices with their start and end apart: 3, of which 2 were waited for; matrix products, arithmetic and copies ran while one was open for 6% of the time, Pallas kernels for 0%

profile of v13, /device:TPU:87, one launch (start us, length us, event | category | flops | bytes accessed | tf_op | source)
XLA Modules:
  0.0 239.8 jit_solution(9422351679847310627)
XLA Ops:
  7.2 0.0 copy-start
  7.2 0.0 all-gather.2.cloned.1.call-start
  7.2 0.8 collective-permute-start
  8.8 0.0 copy-start.2
  8.8 0.0 copy-start.1
  8.8 2.3 multiply_reduce_fusion
  11.1 0.1 slice_reduce_fusion
  11.2 0.0 collective-permute-done
  11.2 0.2 convert_reduce_fusion
  11.4 0.3 fusion.2
  11.7 0.0 copy-start.3
  11.8 0.8 convolution_convert_fusion.1
  12.5 0.9 copy-done.3
  13.4 0.8 convolution_convert_fusion
  14.2 0.0 copy-start.5
  14.2 0.9 pad_maximum_fusion
  15.1 0.0 all-gather.2.cloned.1.call-update
  15.2 0.2 reduce-window.8
  15.3 0.1 select_reduce_fusion.1
  15.4 0.8 copy.14.high_ref
  16.2 0.8 copy.13.low_ref
  17.0 1.6 multiply_reduce_fusion.1
  18.6 0.7 fusion.12
  19.3 3.1 %pad_add_fusion.span_ref = s32[4]{0:T(128)} fusion(s32[1]{0:T(128)} %bitcast.6, s32[1]{0:T(128)} %bitcast.5, s32[1]{0:T(128)} %bitcast.4, s32[1]{0:T(128)} %bitcast.3), kind=kLoop, calls=%fused_computation.28 | loop fusion | flops 12 | bytes 32 | tf_op jit(solution)/shard_map/stack | solution.py:177
  22.4 3.3 %constant_dynamic-slice_fusion = (bf16[768,768]{1,0:T(8,128)(2,1)}, bf16[768,768]{1,0:T(8,128)(2,1)}) fusion(bf16[768,1536]{1,0:T(8,128)(2,1)} %param.17, s32[]{:T(128)S(6)} %select_n.27, s32[]{:T(128)S(6)} %select_n.24), kind=kLoop, calls=%fused_computation.31 | loop fusion | bytes 4718600 | tf_op jit(solution)/shard_map/dynamic_slice | solution.py:184
  25.7 1.5 convolution_convert_fusion.2.query_ref
  27.2 162.4 %all-gather.2.cloned.1.call-done.key_ref.value_ref = bf16[12288,1536]{1,0:T(8,128)(2,1)} async-done(((bf16[192,1536]{1,0:T(8,128)(2,1)}), bf16[12288,1536]{1,0:T(8,128)(2,1)}) %all-gather.2.cloned.1.call-update) | async-done | bytes 37748752 | tf_op jit(solution)/shard_map/all_gather | solution.py:180
  189.6 38.8 %shard_map.104 = (f32[192,768]{1,0:T(8,128)}, f32[192,768]{1,0:T(8,128)}) custom-call(s32[4]{0:T(128)} %pad_add_fusion.span_ref, bf16[192,768]{1,0:T(8,128)(2,1)} %convolution_convert_fusion.2.query_ref, bf16[12288,1536]{1,0:T(8,128)(2,1)} %all-gather.2.cloned.1.call-done.key_ref.value_ref, ...), custom_call_target="tpu_custom_call" | custom-call | tf_op jit(solution)/shard_map/pallas_call | solution.py:104
  228.4 0.7 collective-permute-start.1
  229.2 0.1 dynamic_slice.9
  229.3 1.7 collective-permute-done.1
  231.0 2.0 add_convert_fusion
  (14 shorter events, 0.1 us)
Async XLA Ops:
  7.2 4.6 %copy-start = (bf16[1536,768]{1,0:T(8,128)(2,1)S(1)}, bf16[1536,768]{1,0:T(8,128)(2,1)}, u32[]{:S(2)}) copy-start(bf16[1536,768]{1,0:T(8,128)(2,1)} %param.15) | copy-start | bytes 7077892
  7.2 182.4 %all-gather.2.cloned.1.call-start = ((), (), s32[]{:S(2)}) async-start(), calls=%async_computation | async-start | bytes 38338560 | tf_op jit(solution)/shard_map/all_gather | solution.py:180
  7.2 4.0 %collective-permute-start = (bf16[192,768]{1,0:T(8,128)(2,1)}, bf16[192,768]{1,0:T(8,128)(2,1)S(1)}, u32[]{:S(2)}, u32[]{:S(2)}) collective-permute-start(bf16[192,768]{1,0:T(8,128)(2,1)} %param.9), channel_id=1, source_target_pairs={{0,1},{1,0},{2,3},{3,2},{4,5},{5,4},{6,7},{7,6},{8,9},{9,8},{10,11... | collective-permute-start | bytes 884744 | tf_op jit(solution)/shard_map/ppermute | solution.py:142
  8.8 2.4 copy-start.2
  8.8 2.4 %copy-start.1 = (bf16[192,768]{1,0:T(8,128)(2,1)S(1)}, bf16[192,768]{1,0:T(8,128)(2,1)}, u32[]{:S(2)}) copy-start(bf16[192,768]{1,0:T(8,128)(2,1)} %param.9) | copy-start | bytes 884740
  11.7 1.7 copy-start.3
  14.2 1.0 copy-start.5
  22.4 3.3 %copy-start.4 = (bf16[1536,768]{1,0:T(8,128)(2,1)S(1)}, bf16[1536,768]{1,0:T(8,128)(2,1)}, u32[]{:S(2)}) copy-start(bf16[1536,768]{1,0:T(8,128)(2,1)} %param.14) | copy-start | bytes 7077892
  228.4 2.5 %collective-permute-start.1 = (f32[192,768]{1,0:T(8,128)}, f32[192,768]{1,0:T(8,128)S(1)}, u32[]{:S(2)}, u32[]{:S(2)}) collective-permute-start(f32[192,768]{1,0:T(8,128)} %get-tuple-element.9), channel_id=1, source_target_pairs={{0,1},{1,0},{2,3},{3,2},{4,5},{5,4},{6,7},{7,6},{8,9},{9,8},{10,11... | collective-permute-start | bytes 1769480 | tf_op jit(solution)/shard_map/ppermute | solution.py:189
Sparse Core Ops, SparseCore 0:
  15.3 174.2 all-gather.1

commit v14 on v12

--- a/solution.py
+++ b/solution.py
@@ -31,15 +31,18 @@
         sum_ref[...] = jnp.zeros(sum_ref.shape, jnp.float32)
         acc_ref[...] = jnp.zeros(acc_ref.shape, jnp.float32)
 
-    def step(masked):
+    def step(masked, offset, size):
         rows = query_ref.shape[0]
+        keys = pl.ds(offset, size)
         if masked:
-            key_index = block * KEY_BLOCK + lax.broadcasted_iota(jnp.int32, (rows, KEY_BLOCK), 1)
+            key_index = (
+                block * KEY_BLOCK + offset + lax.broadcasted_iota(jnp.int32, (rows, size), 1)
+            )
             valid = jnp.logical_and(key_index >= low_ref[...], key_index < high_ref[...])
         for head in range(heads):
             cols = slice(head * HEAD_DIM, (head + 1) * HEAD_DIM)
             raw = lax.dot_general(
-                query_ref[:, cols], key_ref[:, cols], (((1,), (1,)), ((), ())),
+                query_ref[:, cols], key_ref[keys, cols], (((1,), (1,)), ((), ())),
                 preferred_element_type=jnp.float32,
             )
             old_max = max_ref[head]
@@ -54,23 +57,34 @@
             alpha = jnp.exp2((old_max - new_max) * EXP2_SCALE)
             sum_ref[head] = alpha * sum_ref[head] + jnp.sum(probs, axis=1, keepdims=True)
             acc_ref[:, cols] = alpha * acc_ref[:, cols] + jnp.dot(
-                probs.astype(jnp.bfloat16), value_ref[:, cols],
+                probs.astype(jnp.bfloat16), value_ref[keys, cols],
                 preferred_element_type=jnp.float32,
             )
             max_ref[head] = new_max
 
+    half = KEY_BLOCK // 2
+    base = block * KEY_BLOCK
     touched = jnp.logical_and(block >= first, block <= last)
-    whole_block = jnp.logical_and(
-        block * KEY_BLOCK >= span_ref[2], (block + 1) * KEY_BLOCK <= span_ref[3]
-    )
+    whole_block = jnp.logical_and(base >= span_ref[2], base + KEY_BLOCK <= span_ref[3])
+    edge = jnp.logical_and(touched, jnp.logical_not(whole_block))
+    need_low = jnp.logical_and(base < span_ref[1], base + half > span_ref[0])
+    need_high = jnp.logical_and(base + half < span_ref[1], base + KEY_BLOCK > span_ref[0])
 
     @pl.when(jnp.logical_and(touched, whole_block))
     def _():
-        step(False)
-
-    @pl.when(jnp.logical_and(touched, jnp.logical_not(whole_block)))
-    def _():
-        step(True)
+        step(False, 0, KEY_BLOCK)
+
+    @pl.when(jnp.logical_and(edge, jnp.logical_and(need_low, need_high)))
+    def _():
+        step(True, 0, KEY_BLOCK)
+
+    @pl.when(jnp.logical_and(edge, jnp.logical_and(need_low, jnp.logical_not(need_high))))
+    def _():
+        step(True, 0, half)
+
+    @pl.when(jnp.logical_and(edge, jnp.logical_and(need_high, jnp.logical_not(need_low))))
+    def _():
+        step(True, half, half)
 
     @pl.when(block == pl.num_programs(0) - 1)
     def _():

time: 235 us -> 229 us (0.974)
  Pallas kernels: 31.7 us -> 26.4 us
    pallas_call x1, Pallas kernels: 31.7 us -> 26.4 us  [attention(): pl.pallas_call(attention_kernel, grid_spec=pltpu.PrefetchScalarGridSpec(n...]
where the time goes in v14:
time: 229 us
  waiting for transfers between devices  167 us (73%)
  Pallas kernels  26.4 us (12%)
  between operations  14.9 us (7%)
  other arithmetic  10.6 us (5%)
  local copies, waits for them, and re-layouts  5.8 us (3%)
  matrix products  3.01 us (1%)
    all_gather x1, waiting for transfers between devices, on_device(): lax.all_gather(jnp.concatenate([keys, values], axis=1), 'req', axis=0, ti...  166 us
    pallas_call x1, Pallas kernels, attention(): pl.pallas_call(attention_kernel, grid_spec=pltpu.PrefetchScalarGridSpec(n...  26.4 us
  transfers between devices with their start and end apart: 3, of which 2 were waited for; matrix products, arithmetic and copies ran while one was open for 6% of the time, Pallas kernels for 0%

profile of v14, /device:TPU:17, one launch (start us, length us, event | category | flops | bytes accessed | tf_op | source)
XLA Modules:
  0.0 228.8 jit_solution(17673579822778738806)
XLA Ops:
  7.2 0.0 copy-start
  7.2 0.0 all-gather.2.cloned.1.call-start
  7.2 0.8 collective-permute-start
  8.8 0.0 copy-start.3
  8.8 0.0 copy-start.1
  8.8 2.3 %multiply_reduce_fusion = f32[3072]{0:T(1024)S(1)} fusion(f32[256,4608]{1,0:T(8,128)} %param.12, f32[256]{0:T(256)S(1)} %divide_multiply_fusion), kind=kLoop, calls=%fused_computation | loop fusion | flops 1569792 | bytes 3159040 | tf_op jit(solution)/shard_map/reduce_sum | solution.py:170
  11.1 0.1 slice_reduce_fusion
  11.2 0.0 collective-permute-done
  11.2 0.2 convert_reduce_fusion
  11.4 0.3 fusion.2
  11.7 0.0 copy-start.4
  11.8 0.8 convolution_convert_fusion.1
  12.5 0.9 copy-done.4
  13.4 0.8 convolution_convert_fusion
  14.2 0.0 copy-start.6
  14.2 0.9 pad_maximum_fusion
  15.1 0.0 all-gather.2.cloned.1.call-update
  15.2 0.2 reduce-window.8
  15.4 0.1 select_reduce_fusion.1
  15.4 0.8 copy.14.high_ref
  16.2 0.8 copy.13.low_ref
  17.0 0.7 fusion.12
  17.7 3.1 %pad_add_fusion.span_ref = s32[4]{0:T(128)} fusion(s32[1]{0:T(128)} %bitcast.6, s32[1]{0:T(128)} %bitcast.5, s32[1]{0:T(128)} %bitcast.4, s32[1]{0:T(128)} %bitcast.3), kind=kLoop, calls=%fused_computation.29 | loop fusion | flops 12 | bytes 32 | tf_op jit(solution)/shard_map/stack | solution.py:191
  20.8 3.3 %constant_dynamic-slice_fusion = (bf16[768,768]{1,0:T(8,128)(2,1)}, bf16[768,768]{1,0:T(8,128)(2,1)}) fusion(bf16[768,1536]{1,0:T(8,128)(2,1)} %param.17, s32[]{:T(128)S(6)} %select_n.27, s32[]{:T(128)S(6)} %select_n.22), kind=kLoop, calls=%fused_computation.31 | loop fusion | bytes 4718600 | tf_op jit(solution)/shard_map/dynamic_slice | solution.py:198
  24.1 1.5 convolution_convert_fusion.2.query_ref
  25.6 166.5 %all-gather.2.cloned.1.call-done.key_ref.value_ref = bf16[12288,1536]{1,0:T(8,128)(2,1)} async-done(((bf16[192,1536]{1,0:T(8,128)(2,1)}), bf16[12288,1536]{1,0:T(8,128)(2,1)}) %all-gather.2.cloned.1.call-update) | async-done | bytes 37748752 | tf_op jit(solution)/shard_map/all_gather | solution.py:194
  192.1 26.4 %shard_map.104 = (f32[192,768]{1,0:T(8,128)}, f32[192,768]{1,0:T(8,128)}) custom-call(s32[4]{0:T(128)} %pad_add_fusion.span_ref, bf16[192,768]{1,0:T(8,128)(2,1)} %convolution_convert_fusion.2.query_ref, bf16[12288,1536]{1,0:T(8,128)(2,1)} %all-gather.2.cloned.1.call-done.key_ref.value_ref, ...), custom_call_target="tpu_custom_call" | custom-call | tf_op jit(solution)/shard_map/pallas_call | solution.py:118
  218.5 0.7 collective-permute-start.1
  219.2 1.6 multiply_reduce_fusion.1
  220.8 0.1 dynamic-slice_add_fusion
  220.9 0.1 collective-permute-done.1
  221.0 0.9 add_convert_fusion
  (15 shorter events, 0.1 us)
Async XLA Ops:
  7.2 4.6 %copy-start = (bf16[1536,768]{1,0:T(8,128)(2,1)S(1)}, bf16[1536,768]{1,0:T(8,128)(2,1)}, u32[]{:S(2)}) copy-start(bf16[1536,768]{1,0:T(8,128)(2,1)} %param.15) | copy-start | bytes 7077892
  7.2 184.9 %all-gather.2.cloned.1.call-start = ((), (), s32[]{:S(2)}) async-start(), calls=%async_computation | async-start | bytes 38338560 | tf_op jit(solution)/shard_map/all_gather | solution.py:194
  7.2 4.0 %collective-permute-start = (bf16[192,768]{1,0:T(8,128)(2,1)}, bf16[192,768]{1,0:T(8,128)(2,1)S(1)}, u32[]{:S(2)}, u32[]{:S(2)}) collective-permute-start(bf16[192,768]{1,0:T(8,128)(2,1)} %param.9), channel_id=1, source_target_pairs={{0,1},{1,0},{2,3},{3,2},{4,5},{5,4},{6,7},{7,6},{8,9},{9,8},{10,11... | collective-permute-start | bytes 884744 | tf_op jit(solution)/shard_map/ppermute | solution.py:156
  8.8 2.4 %copy-start.3 = (f32[3,1536]{1,0:T(4,128)S(1)}, f32[3,1536]{1,0:T(4,128)}, u32[]{:S(2)}) copy-start(f32[3,1536]{1,0:T(4,128)} %param.13) | copy-start | bytes 55300
  8.8 2.4 %copy-start.1 = (bf16[192,768]{1,0:T(8,128)(2,1)S(1)}, bf16[192,768]{1,0:T(8,128)(2,1)}, u32[]{:S(2)}) copy-start(bf16[192,768]{1,0:T(8,128)(2,1)} %param.9) | copy-start | bytes 884740
  11.7 1.7 copy-start.4
  14.2 1.0 copy-start.6
  20.8 3.3 %copy-start.5 = (bf16[1536,768]{1,0:T(8,128)(2,1)S(1)}, bf16[1536,768]{1,0:T(8,128)(2,1)}, u32[]{:S(2)}) copy-start(bf16[1536,768]{1,0:T(8,128)(2,1)} %param.14) | copy-start | bytes 7077892
  218.5 2.5 %copy-start.2 = (f32[192,768]{1,0:T(8,128)S(1)}, f32[192,768]{1,0:T(8,128)}, u32[]{:S(2)}) copy-start(f32[192,768]{1,0:T(8,128)} %get-tuple-element.4) | copy-start | bytes 1769476
  218.5 2.5 %collective-permute-start.1 = (f32[192,768]{1,0:T(8,128)}, f32[192,768]{1,0:T(8,128)S(1)}, u32[]{:S(2)}, u32[]{:S(2)}) collective-permute-start(f32[192,768]{1,0:T(8,128)} %get-tuple-element.5), channel_id=1, source_target_pairs={{0,1},{1,0},{2,3},{3,2},{4,5},{5,4},{6,7},{7,6},{8,9},{9,8},{10,11... | collective-permute-start | bytes 1769480 | tf_op jit(solution)/shard_map/ppermute | solution.py:202
Sparse Core Ops, SparseCore 0:
  15.3 176.7 all-gather.1
